TPU v7x, 32 devices: a whole 2x2x4 slice. The times are simulated.
32 devices in a mesh: row: 8 (over z, y), col: 2 (over x), fiber: 2 (over core).
Axes of the slice: x: 2, y: 2, z: 4, core: 2. Of those that a mesh axis runs over, the one named last changes fastest.
Arguments:
- a_panels: float32 [3072, 2, 2, 768], P(('row', 'col'), 'fiber'), may hold values from -12 to 12
- b_panels: float32 [2, 2, 768, 2048], P('fiber', None, 'row', 'col'), may hold values from -0.15625 to 0.15625
- a_pattern: int32 [24, 2, 2, 6], P('row', 'fiber'), may hold values 0 or 1
- c_pattern: int32 [24, 16], P('row', 'col'), may hold values 0 or 1
Outputs:
- scaled: float32 [3072, 2048], P(('row', 'fiber'), 'col')
All inputs are finite; a program needn't handle non-finite values. No bound on the sum of `a_pattern` or of `c_pattern` on one device may be relied on, other than what follows from the above.
Results may differ from a plain program's by a relative error of at most 0.00013.
Values sent between devices are 32-bit elements; how exact they have to be, the bound alone decides.
No kernel may reach another device: no remote copies, remote signals or barrier semaphores. Data moves between devices by JAX's collectives and lax.ppermute only.
A program may use at most 64 MiB of HBM per device.

v0:
```python
import functools

import jax
import jax.numpy as jnp
from jax import lax
from jax.experimental import pallas as pl
from jax.experimental.pallas import tpu as pltpu
from jax.sharding import PartitionSpec as P


BLK = 128


EPS = 1e-06
LAST = 128
UNIT = 64


LINE = (0, 1, 3, 2)


def line_pairs(shift):
    size = len(LINE)
    return [
        (LINE[i] * 2 + y, LINE[(i + shift) % size] * 2 + y) for i in range(size) for y in range(2)
    ]


def line_at(z, step):
    place = jnp.where(z < 2, z, 5 - z)
    place = (place + step + len(LINE)) % len(LINE)
    return jnp.where(place < 2, place, 5 - place)


def all_sum(value, axis_name):
    size = lax.axis_size(axis_name)
    stride = 1
    while stride < size:
        rest = size // stride
        radix = next(p for p in range(2, rest + 1) if rest % p == 0)
        total = value
        for turn in range(1, radix):
            pairs = []
            for i in range(size):
                digit = i // stride % radix
                pairs.append((i, i + ((digit + turn) % radix - digit) * stride))
            total = total + lax.ppermute(value, axis_name, pairs)
        value = total
        stride *= radix
    return value


def gathered(a_panels, b_panels, a_pattern, c_pattern):
    _, _, sections, width = a_panels.shape
    block_rows, width_blocks = a_pattern.shape[0], a_pattern.shape[3]
    columns = b_panels.shape[3]
    local_rows = block_rows * BLK
    n_row, fibers = lax.axis_size("row"), lax.axis_size("fiber")
    share = local_rows // fibers
    total = jnp.zeros((local_rows, columns), jnp.float32)
    for section in range(sections):
        block = lax.all_gather(a_panels[:, 0, section, :], "col", axis=0, tiled=True)
        keep = a_pattern[:, 0, section, :].astype(jnp.float32)
        left = block.reshape(block_rows, BLK, width_blocks, BLK) * keep[:, None, :, None]
        right = lax.all_gather(b_panels[0, section], "row", axis=0, tiled=True)
        total = total + jnp.dot(
            left.reshape(local_rows, width),
            right,
            precision=lax.Precision.HIGH,
            preferred_element_type=jnp.float32,
        )
    keep = jnp.broadcast_to(
        c_pattern.astype(jnp.float32)[:, None, :, None],
        (block_rows, BLK, columns // BLK, BLK),
    ).reshape(local_rows, columns)
    merged = lax.psum_scatter(total, "fiber", scatter_dimension=0, tiled=True)
    product = merged * lax.dynamic_slice_in_dim(keep, lax.axis_index("fiber") * share, share, 0)
    inflated = product * product
    sums = all_sum(all_sum(jnp.sum(inflated, axis=0, keepdims=True), "fiber"), "row")
    return inflated / (sums / (share * fibers * n_row) + EPS)


def split(value):
    high = value.astype(jnp.bfloat16)
    low = (value - high.astype(jnp.float32)).astype(jnp.bfloat16)
    return high, low


def product3(a_high, a_low, b_high, b_low):
    def dot(x, y):
        return jnp.dot(x, y, preferred_element_type=jnp.float32)

    return dot(a_high, b_high) + (dot(a_high, b_low) + dot(a_low, b_high))


def left_kernel(groups, plan, pattern, *refs):
    sources, outs, turned = refs[: len(plan)], refs[len(plan) : -1], refs[-1]
    _, _, sections, width = sources[0].shape
    n_row, row, col = lax.axis_size("row"), lax.axis_index("row"), lax.axis_index("col")
    depth = width // n_row
    done = 0
    for source, (which, is_peer, first) in zip(sources, plan, strict=True):
        position = 1 - col if is_peer else col
        for g in range(source.shape[0] // UNIT):
            part = pl.ds(g * UNIT, UNIT)
            block_row = (position * (3 * UNIT) + first + g * UNIT) // BLK
            for s in range(sections):
                kept = []
                for w in range(width // BLK):
                    keep = pattern[which, block_row, s * (width // BLK) + w]
                    kept.append(jnp.where(keep != 0, source[part, 0, s, pl.ds(w * BLK, BLK)], 0.0))
                value = jnp.concatenate(kept, axis=1)
                for r in range(n_row):
                    turned[r, s] = value[:, r * depth : (r + 1) * depth]
            place = pl.ds(done, UNIT)
            for i, members in enumerate(groups):
                owners = [line_at(row // 2, step) * 2 + (row + turn) % 2 for step, turn in members]
                pieces = [turned[r, s] for r in owners for s in range(sections)]
                high, low = split(jnp.concatenate(pieces, axis=1))
                outs[2 * i][place, :] = high
                outs[2 * i + 1][place, :] = low
            done += UNIT


def put_shards(shards, b_high, b_low):
    _, sections, depth, _ = shards[0].shape
    for i in range(len(shards) * sections):
        part = pl.ds(i * depth, depth)
        b_high[part, :], b_low[part, :] = split(shards[i // sections][0, i % sections])


def stacked(refs):
    return jnp.concatenate([ref[...] for ref in refs], axis=0)


def group_kernel(sets, sizes, *refs):
    lefts = refs[: 2 * sets * len(sizes)]
    rest = refs[len(lefts) :]
    shards, (*near, out, b_high, b_low) = rest[: sum(sizes)], rest[sum(sizes) :]
    put_shards(shards, b_high, b_low)
    total = near[0][...] if near else None
    first = 0
    for i in range(len(sizes)):
        group = lefts[2 * sets * i : 2 * sets * (i + 1)]
        high, low = stacked(group[:sets]), stacked(group[sets:])
        part = pl.ds(first, high.shape[1])
        value = product3(high, low, b_high[part, :], b_low[part, :])
        total = value if total is None else total + value
        first += high.shape[1]
    out[...] = total


def far_value(first, *refs):
    highs, lows, (near, near_late, shard, b_high, b_low) = refs[:4], refs[4:8], refs[8:]
    put_shards([shard], b_high, b_low)
    value = product3(stacked(highs), stacked(lows), b_high[...], b_low[...])
    tile = slice(first, first + shard.shape[3])
    return value + jnp.concatenate([near[:, tile], near_late[:, tile]], axis=0)


def far_kernel(first, *refs):
    *ins, kept, sent, b_high, b_low = refs
    value = far_value(first, *ins, b_high, b_low)
    rows = kept.shape[1]
    flip = lax.axis_index("col") ^ lax.axis_index("fiber")
    for turn in range(2):

        @pl.when(flip == turn)
        def _():
            for p in range(4):
                y, x = divmod(p, 2)
                out = kept if x == turn else sent
                out[y] = value[p * rows : (p + 1) * rows]


def last_kernel(first, *refs):
    *ins, out, b_high, b_low = refs
    value = far_value(first, *ins, b_high, b_low)
    rows = out.shape[1]
    for p in range(4):
        out[p] = value[p * rows : (p + 1) * rows]


def squared(pattern, which, fiber, first, value):
    columns = value.shape[1]
    half = lax.axis_index("row") % 2 * (pattern.shape[2] // 2)
    out = []
    for g in range(value.shape[0] // UNIT):
        block_row = (fiber * value.shape[0] + g * UNIT) // BLK
        kept = []
        for w in range(columns // BLK):
            keep = pattern[which, block_row, half + first // BLK + w]
            piece = value[g * UNIT : (g + 1) * UNIT, w * BLK : (w + 1) * BLK]
            piece = jnp.where(keep != 0, piece, 0.0)
            kept.append(piece * piece)
        out.append(jnp.concatenate(kept, axis=1) if len(kept) > 1 else kept[0])
    return jnp.concatenate(out, axis=0)


def square_kernel(pattern, kept, received, stays, goes, sums):
    fiber = lax.axis_index("fiber")
    mine = squared(pattern, 0, fiber, 0, kept[0] + received[0])
    other = squared(pattern, 1, fiber, 0, kept[1] + received[1])
    stays[...], goes[...] = mine, other
    sums[...] = jnp.sum(mine, axis=0, keepdims=True) + jnp.sum(other, axis=0, keepdims=True)


def square_last_kernel(first, pattern, mine, received, early, stays, goes, sums):
    fiber, col = lax.axis_index("fiber"), lax.axis_index("col")
    total = None
    for y, target in ((0, stays), (1, goes)):
        for block in (1 - fiber, fiber):
            p = 2 * y + (block ^ col)
            value = squared(pattern, y, block, first, mine[p] + received[p])
            part = jnp.sum(value, axis=0, keepdims=True)
            total = part if total is None else total + part
        target[...] = value
    sums[:, :first] = early[...]
    sums[:, first:] = total


def scale_kernel(row_total, sums, other_sums, *refs):
    *parts, out = refs
    half = sums.shape[1]
    y = lax.axis_index("row") % 2
    for side, total, (early, last) in ((y, sums, parts[:2]), (1 - y, other_sums, parts[2:])):
        scale = total[...] / row_total + EPS
        cut = early.shape[1]
        out[:, pl.ds(pl.multiple_of(side * half, BLK), cut)] = early[...] / scale[:, :cut]
        out[:, pl.ds(pl.multiple_of(side * half + cut, BLK), half - cut)] = last[...] / scale[:, cut:]


def together(*values):
    return lax.optimization_barrier(values)


VMEM = pl.BlockSpec(memory_space=pltpu.VMEM)
SMEM = pl.BlockSpec(memory_space=pltpu.SMEM)


def call(kernel, out_shapes, specs, scratch=(), flops=0):
    def run(*args):
        moved = sum(a.size * a.dtype.itemsize for a in (*args, *out_shapes))
        return pl.pallas_call(
            kernel,
            out_shape=out_shapes,
            in_specs=specs,
            out_specs=[VMEM] * len(out_shapes),
            scratch_shapes=scratch,
            cost_estimate=pl.CostEstimate(flops=flops, bytes_accessed=moved, transcendentals=0),
            compiler_params=pltpu.CompilerParams(vmem_limit_bytes=16 * 2**20),
        )(*args)

    return run


def local(a_panels, b_panels, a_pattern, c_pattern):
    rows, _, sections, _ = a_panels.shape
    block_rows = a_pattern.shape[0]
    depth, columns = b_panels.shape[2:]
    n_row, n_col, fibers = (lax.axis_size(name) for name in ("row", "col", "fiber"))
    local_rows = rows * n_col
    share = local_rows // fibers
    if (n_row, n_col, fibers, sections, rows, columns) != (8, 2, 2, 2, 3 * UNIT, 1024):
        return gathered(a_panels, b_panels, a_pattern, c_pattern)

    f32, bf16 = jnp.float32, jnp.bfloat16
    shape = jax.ShapeDtypeStruct
    half = columns // 2
    cut = half - LAST
    my_y = lax.axis_index("row") & 1
    swap = [(0, 1), (1, 0)]
    swap_y = [(r, r ^ 1) for r in range(n_row)]

    def columns_half(side):
        where = (0, 0, 0, side * half)
        sizes = (*b_panels.shape[:3], half)
        return lax.dynamic_slice(b_panels, where, sizes, allow_negative_indices=False)

    own, gives = columns_half(my_y), columns_half(1 - my_y)
    shards = {(0, 0): own}
    shards[0, 1] = lax.ppermute(gives, "row", swap_y)
    for turn in range(2):
        shards[-1, turn] = lax.ppermute(shards[0, turn], "row", line_pairs(1))
        shards[1, turn] = lax.ppermute(shards[0, turn], "row", line_pairs(-1))
    shards[2, 0] = lax.ppermute(shards[-1, 0], "row", line_pairs(1))
    far_early = lax.ppermute(shards[-1, 1][..., :cut], "row", line_pairs(1))
    far_last = lax.ppermute(shards[-1, 1][..., cut:], "row", line_pairs(1))

    units = [a_panels[u * UNIT : (u + 1) * UNIT] for u in range(3)]
    x2 = lax.ppermute(units[2], "col", swap)
    y0 = lax.ppermute(units[0], "row", swap_y)
    y1 = lax.ppermute(units[1], "row", swap_y)
    x01 = lax.ppermute(a_panels[: 2 * UNIT], "col", swap)
    d2 = lax.ppermute(x2, "row", swap_y)
    y2 = lax.ppermute(units[2], "row", swap_y)
    d0 = lax.ppermute(y0, "col", swap)
    d1 = lax.ppermute(y1, "col", swap)
    a_table = a_pattern.reshape(block_rows, -1)
    a_table = jnp.stack([a_table, lax.ppermute(a_table, "row", swap_y)])
    c_table = jnp.stack([c_pattern, lax.ppermute(c_pattern, "row", swap_y)])

    groups = [[(0, 0), (0, 1), (-1, 0), (1, 0)], [(-1, 1), (1, 1), (2, 0)], [(2, 1)]]
    shard_depth = sections * depth

    def left(*sources):
        arrays = [source for source, *_ in sources]
        plan = tuple((y, x, first) for _, y, x, first in sources)
        count = sum(source.shape[0] for source in arrays)
        parts = [shape((count, len(m) * shard_depth), bf16) for m in groups for _ in range(2)]
        return call(
            functools.partial(left_kernel, groups, plan),
            parts,
            [SMEM] + [VMEM] * len(arrays),
            [pltpu.VMEM((n_row, sections, UNIT, depth), f32)],
        )(a_table, *arrays)

    early_sets = [
        left((a_panels, 0, False, 0)),
        left((x01, 0, True, 0), (x2, 0, True, 2 * UNIT)),
        left((y0, 1, False, 0), (y1, 1, False, UNIT)),
    ]

    def picked(sets, g):
        return [s[2 * g] for s in sets] + [s[2 * g + 1] for s in sets]

    def product(sets, which, *near):
        lefts = [part for g in which for part in picked(sets, g)]
        members = [shards[m] for g in which for m in groups[g]]
        count = sum(s[0].shape[0] for s in sets)
        factor = pltpu.VMEM((len(members) * shard_depth, half), bf16)
        (total,) = call(
            functools.partial(group_kernel, len(sets), tuple(len(groups[g]) for g in which)),
            [shape((count, half), f32)],
            [VMEM] * (len(lefts) + len(members) + len(near)),
            [factor, factor],
            6 * count * half * len(members) * shard_depth,
        )(*lefts, *members, *near)
        return total

    near = product(early_sets, [0])
    y2, near = together(y2, near)
    late_set = left((y2, 1, False, 2 * UNIT), (d0, 1, True, 0), (d1, 1, True, UNIT), (d2, 1, True, 2 * UNIT))

    near = product(early_sets, [1], near)
    near_late = product([late_set], [0, 1])

    far_lefts = picked([*early_sets, late_set], 2)

    def far(kernel, first, shard, outs):
        factor = pltpu.VMEM((shard_depth, shard.shape[3]), bf16)
        return call(
            functools.partial(kernel, first),
            outs,
            [VMEM] * (len(far_lefts) + 3),
            [factor, factor],
            6 * 4 * rows * shard.shape[3] * shard_depth,
        )(*far_lefts, near, near_late, shard)

    kept, sent = far(far_kernel, 0, far_early, [shape((2, rows, cut), f32)] * 2)
    received = lax.ppermute(sent, "fiber", swap)
    (mine,) = far(last_kernel, cut, far_last, [shape((4, rows, LAST), f32)])
    theirs = lax.ppermute(mine, "fiber", swap)
    stays, goes, sums = call(
        square_kernel, [shape((rows, cut), f32)] * 2 + [shape((1, cut), f32)], [SMEM, VMEM, VMEM]
    )(c_table, kept, received)
    comes = lax.ppermute(goes, "row", swap_y)
    sums = sums + lax.ppermute(sums, "fiber", swap)
    last_stays, last_goes, sums = call(
        functools.partial(square_last_kernel, cut),
        [shape((rows, LAST), f32)] * 2 + [shape((1, half), f32)],
        [SMEM, VMEM, VMEM, VMEM],
    )(c_table, mine, theirs, sums)
    last_comes = lax.ppermute(last_goes, "row", swap_y)
    for bit in (2, 4):
        sums = sums + lax.ppermute(sums, "row", [(r, r ^ bit) for r in range(n_row)])
    other_sums = lax.ppermute(sums, "row", swap_y)
    (out,) = call(
        functools.partial(scale_kernel, share * fibers * n_row), [shape((share, columns), f32)], [VMEM] * 6
    )(sums, other_sums, stays, last_stays, comes, last_comes)
    return out


def solution(mesh):
    placed = (
        P(("row", "col"), "fiber", None, None),
        P("fiber", None, "row", "col"),
        P("row", "fiber", None, None),
        P("row", "col"),
    )

    return jax.shard_map(local, mesh=mesh, in_specs=placed, out_specs=P(("row", "fiber"), "col"), check_vma=False)
```

profile of v0, /device:TPU:0, one launch (start us, length us, event | category | flops | bytes accessed | tf_op | source)
XLA Modules:
  0.0 106.3 jit_solution(6723927258818782160)
XLA Ops:
  0.0 2.7 %fusion = (f32[64,1,2,768]{3,2,1,0:T(2,128)S(1)}, f32[64,1,2,768]{3,2,1,0:T(2,128)}, f32[64,1,2,768]{3,2,1,0:T(2,128)}) fusion(f32[192,1,2,768]{3,2,1,0:T(2,128)} %refs_0_.1), kind=kLoop, calls=%fused_computation.4 | loop fusion | bytes 2359296 | tf_op jit(solution)/shard_map/slice | solution.py:290
  2.7 3.0 %collective-permute-start.4 = (f32[64,1,2,768]{3,2,1,0:T(2,128)}, f32[64,1,2,768]{3,2,1,0:T(2,128)}, u32[]{:S(2)}, u32[]{:S(2)}) collective-permute-start(f32[64,1,2,768]{3,2,1,0:T(2,128)} %get-tuple-element.75), channel_id=1, source_target_pairs={{0,4},{4,0},{8,12},{12,8},{16,20},{20,16},{24,28},{28,24},{1,5},{5... | collective-permute-start | bytes 1179656 | tf_op jit(solution)/shard_map/ppermute | solution.py:292
  5.8 2.0 %collective-permute-start.1 = (s32[3,12]{1,0:T(4,128)S(1)}, s32[3,12]{1,0:T(4,128)S(1)}, u32[]{:S(2)}, u32[]{:S(2)}) collective-permute-start(s32[3,12]{1,0:T(4,128)S(1)} %reshape.3), channel_id=1, source_target_pairs={{0,4},{4,0},{8,12},{12,8},{16,20},{20,16},{24,28},{28,24},{1,5},{5... | collective-permute-start | bytes 440 | tf_op jit(solution)/shard_map/ppermute | solution.py:300
  7.8 1.5 %collective-permute-start.3 = (f32[64,1,2,768]{3,2,1,0:T(2,128)}, f32[64,1,2,768]{3,2,1,0:T(2,128)}, u32[]{:S(2)}, u32[]{:S(2)}) collective-permute-start(f32[64,1,2,768]{3,2,1,0:T(2,128)} %get-tuple-element.74), channel_id=1, source_target_pairs={{0,2},{2,0},{1,3},{3,1},{4,6},{6,4},{5,7},{7,5},{8,10},{10,8},{9,1... | collective-permute-start | bytes 1179656 | tf_op jit(solution)/shard_map/ppermute | solution.py:291
  10.8 12.7 %collective-permute-done.1 = s32[3,12]{1,0:T(4,128)S(1)} collective-permute-done((s32[3,12]{1,0:T(4,128)S(1)}, s32[3,12]{1,0:T(4,128)S(1)}, u32[]{:S(2)}, u32[]{:S(2)}) %collective-permute-start.1) | collective-permute-done | bytes 176 | tf_op jit(solution)/shard_map/ppermute | solution.py:300
  23.5 1.7 %collective-permute-start.7 = (f32[1,2,96,512]{3,2,1,0:T(8,128)S(1)}, f32[1,2,96,512]{3,2,1,0:T(8,128)}, u32[]{:S(2)}, u32[]{:S(2)}) collective-permute-start(f32[1,2,96,512]{3,2,1,0:T(8,128)S(1)} %get-tuple-element.76), channel_id=1, source_target_pairs={{0,4},{4,0},{8,12},{12,8},{16,20},{20,16},{24,28},{28,24},{1,5},{5... | collective-permute-start | bytes 1179656 | tf_op jit(solution)/shard_map/ppermute | solution.py:282
  25.3 1.6 %collective-permute-start.8 = (f32[1,2,96,512]{3,2,1,0:T(8,128)S(1)}, f32[1,2,96,512]{3,2,1,0:T(8,128)}, u32[]{:S(2)}, u32[]{:S(2)}) collective-permute-start(f32[1,2,96,512]{3,2,1,0:T(8,128)S(1)} %get-tuple-element.77.refs_6_.refs_4_), channel_id=1, source_target_pairs={{0,8},{4,12},{8,24},{12,28},{24,16},{28,20},{16,0},{20,4},{1,9},{5... | collective-permute-start | bytes 1179656 | tf_op jit(solution)/shard_map/ppermute | solution.py:284
  28.5 7.1 %collective-permute-done.7.refs_7_.refs_5_ = f32[1,2,96,512]{3,2,1,0:T(8,128)} collective-permute-done((f32[1,2,96,512]{3,2,1,0:T(8,128)S(1)}, f32[1,2,96,512]{3,2,1,0:T(8,128)}, u32[]{:S(2)}, u32[]{:S(2)}) %collective-permute-start.7) | collective-permute-done | bytes 393248 | tf_op jit(solution)/shard_map/ppermute | solution.py:282
  35.6 1.8 %collective-permute-start.13 = (f32[1,2,96,512]{3,2,1,0:T(8,128)}, f32[1,2,96,512]{3,2,1,0:T(8,128)S(1)}, u32[]{:S(2)}, u32[]{:S(2)}) collective-permute-start(f32[1,2,96,512]{3,2,1,0:T(8,128)} %collective-permute-done.7.refs_7_.refs_5_), channel_id=1, source_target_pairs={{0,8},{4,12},{8,24},{12,28},{24,16},{28,20},{16,0},{20,4},{1,9},{5... | collective-permute-start | bytes 1179656 | tf_op jit(solution)/shard_map/ppermute | solution.py:284
  38.9 8.7 %collective-permute-done.9.refs_9_.refs_7_ = f32[1,2,96,512]{3,2,1,0:T(8,128)S(1)} collective-permute-done((f32[1,2,96,512]{3,2,1,0:T(8,128)S(1)}, f32[1,2,96,512]{3,2,1,0:T(8,128)S(1)}, u32[]{:S(2)}, u32[]{:S(2)}) %collective-permute-start.9) | collective-permute-done | bytes 393248 | tf_op jit(solution)/shard_map/ppermute | solution.py:285
  48.4 1.5 %collective-permute-start.10 = (f32[64,1,2,768]{3,2,1,0:T(2,128)}, f32[64,1,2,768]{3,2,1,0:T(2,128)}, u32[]{:S(2)}, u32[]{:S(2)}) collective-permute-start(f32[64,1,2,768]{3,2,1,0:T(2,128)} %collective-permute-done.4.refs_0_), channel_id=1, source_target_pairs={{0,2},{2,0},{1,3},{3,1},{4,6},{6,4},{5,7},{7,5},{8,10},{10,8},{9,1... | collective-permute-start | bytes 1179656 | tf_op jit(solution)/shard_map/ppermute | solution.py:297
  52.8 3.9 %collective-permute-start.14 = (f32[1,2,96,512]{3,2,1,0:T(8,128)}, f32[1,2,96,512]{3,2,1,0:T(8,128)S(1)}, u32[]{:S(2)}, u32[]{:S(2)}) collective-permute-start(f32[1,2,96,512]{3,2,1,0:T(8,128)} %collective-permute-done.7.refs_7_.refs_5_), channel_id=1, source_target_pairs={{0,16},{4,20},{8,0},{12,4},{24,8},{28,12},{16,24},{20,28},{1,17},{... | collective-permute-start | bytes 1179656 | tf_op jit(solution)/shard_map/ppermute | solution.py:285
  56.8 2.5 %shard_map.46 = (bf16[192,768]{1,0:T(8,128)(2,1)S(1)}, bf16[192,768]{1,0:T(8,128)(2,1)S(1)}, bf16[192,576]{1,0:T(8,128)(2,1)S(1)}, bf16[192,576]{1,0:T(8,128)(2,...) custom-call(s32[2,3,12]{2,1,0:T(4,128)S(1)} %pad_add_fusion.1.pattern, f32[192,1,2,768]{3,2,1,0:T(2,128)S(1)} %copy-done), custom_call_target="tpu_custom_call" | custom-call | bytes 2359584 | tf_op jit(solution)/shard_map/pallas_call | solution.py:244
  59.4 2.5 %shard_map.48 = (bf16[128,768]{1,0:T(8,128)(2,1)S(1)}, bf16[128,768]{1,0:T(8,128)(2,1)S(1)}, bf16[128,576]{1,0:T(8,128)(2,1)S(1)}, bf16[128,576]{1,0:T(8,128)(2,...) custom-call(s32[2,3,12]{2,1,0:T(4,128)S(1)} %pad_add_fusion.1.pattern, ...), custom_call_target="tpu_custom_call" | custom-call | bytes 1573152 | tf_op jit(solution)/shard_map/pallas_call | solution.py:244
  61.8 2.9 %shard_map.47 = (bf16[192,768]{1,0:T(8,128)(2,1)S(1)}, bf16[192,768]{1,0:T(8,128)(2,1)S(1)}, bf16[192,576]{1,0:T(8,128)(2,1)S(1)}, bf16[192,576]{1,0:T(8,128)(2,...) custom-call(s32[2,3,12]{2,1,0:T(4,128)S(1)} %pad_add_fusion.1.pattern, ...), custom_call_target="tpu_custom_call" | custom-call | bytes 2359584 | tf_op jit(solution)/shard_map/pallas_call | solution.py:244
  65.1 2.6 %shard_map.49.refs_9_ = f32[512,512]{1,0:T(8,128)S(1)} custom-call(bf16[192,768]{1,0:T(8,128)(2,1)S(1)} %get-tuple-element.42.refs_0_, bf16[192,768]{1,0:T(8,128)(2,1)S(1)} %get-tuple-element.43.refs_1_, bf16[128,768]{1,0:T(8,128)(2,1)S(1)} %get-tuple-element.44.refs_2_, bf16[192,768]{1,0:T(8,128)(2,1)S(1)} %get-tuple-element.45.refs_3_, ...), custom_call_target="tpu_custom_call" | custom-call | flops 1207959552 | bytes 4194304 | tf_op jit(solution)/shard_map/pallas_call | solution.py:244
  68.2 3.8 %shard_map.50 = (bf16[256,768]{1,0:T(8,128)(2,1)S(1)}, bf16[256,768]{1,0:T(8,128)(2,1)S(1)}, bf16[256,576]{1,0:T(8,128)(2,1)S(1)}, bf16[256,576]{1,0:T(8,128)(2,...) custom-call(s32[2,3,12]{2,1,0:T(4,128)S(1)} %pad_add_fusion.1.pattern, ...), custom_call_target="tpu_custom_call" | custom-call | bytes 3146016 | tf_op jit(solution)/shard_map/pallas_call | solution.py:244
  74.4 2.5 %shard_map.52.refs_9_ = f32[256,512]{1,0:T(8,128)S(1)} custom-call(bf16[256,768]{1,0:T(8,128)(2,1)S(1)} %get-tuple-element.61.refs_0_, bf16[256,768]{1,0:T(8,128)(2,1)S(1)} %get-tuple-element.62.refs_1_, bf16[256,576]{1,0:T(8,128)(2,1)S(1)} %get-tuple-element.63.refs_2_, bf16[256,576]{1,0:T(8,128)(2,1)S(1)} %get-tuple-element.64.refs_3_, ...), custom_call_target="tpu_custom_call" | custom-call | flops 1056964608 | bytes 4653056 | tf_op jit(solution)/shard_map/pallas_call | solution.py:244
  78.6 6.1 %collective-permute-done.16.refs_10_ = f32[1,2,96,128]{3,2,1,0:T(8,128)S(1)} collective-permute-done((f32[1,2,96,128]{3,2,1,0:T(8,128)S(1)}, f32[1,2,96,128]{3,2,1,0:T(8,128)S(1)}, u32[]{:S(2)}, u32[]{:S(2)}) %collective-permute-start.16) | collective-permute-done | bytes 98336 | tf_op jit(solution)/shard_map/ppermute | solution.py:288
  85.8 3.1 %collective-permute-done = s32[3,8]{1,0:T(4,128)S(1)} collective-permute-done((s32[3,8]{1,0:T(4,128)S(1)}, s32[3,8]{1,0:T(4,128)S(1)}, u32[]{:S(2)}, u32[]{:S(2)}) %collective-permute-start) | collective-permute-done | bytes 128 | tf_op jit(solution)/shard_map/ppermute | solution.py:301
  92.1 1.6 %collective-permute-start.25 = (f32[192,128]{1,0:T(8,128)S(1)}, f32[192,128]{1,0:T(8,128)S(1)}, u32[]{:S(2)}, u32[]{:S(2)}) collective-permute-start(f32[192,128]{1,0:T(8,128)S(1)} %get-tuple-element.72), channel_id=1, source_target_pairs={{0,4},{4,0},{8,12},{12,8},{16,20},{20,16},{24,28},{28,24},{1,5},{5... | collective-permute-start | bytes 294920 | tf_op jit(solution)/shard_map/ppermute | solution.py:374
  93.7 3.6 %collective-permute-done.21 = f32[1,512]{1,0:T(1,128)S(1)} collective-permute-done((f32[1,512]{1,0:T(1,128)S(1)}, f32[1,512]{1,0:T(1,128)S(1)}, u32[]{:S(2)}, u32[]{:S(2)}) %collective-permute-start.21) | collective-permute-done | bytes 2080 | tf_op jit(solution)/shard_map/ppermute | solution.py:376
  97.9 3.9 %collective-permute-done.22 = f32[1,512]{1,0:T(1,128)S(1)} collective-permute-done((f32[1,512]{1,0:T(1,128)S(1)}, f32[1,512]{1,0:T(1,128)S(1)}, u32[]{:S(2)}, u32[]{:S(2)}) %collective-permute-start.22) | collective-permute-done | bytes 2080 | tf_op jit(solution)/shard_map/ppermute | solution.py:376
  102.3 3.1 %collective-permute-done.23.other_sums = f32[1,512]{1,0:T(1,128)S(1)} collective-permute-done((f32[1,512]{1,0:T(1,128)S(1)}, f32[1,512]{1,0:T(1,128)S(1)}, u32[]{:S(2)}, u32[]{:S(2)}) %collective-permute-start.23) | collective-permute-done | bytes 2080 | tf_op jit(solution)/shard_map/ppermute | solution.py:377
  (68 shorter events, 19.8 us)
Async XLA Ops:
  2.7 22.6 %collective-permute-start.4 = (f32[64,1,2,768]{3,2,1,0:T(2,128)}, f32[64,1,2,768]{3,2,1,0:T(2,128)}, u32[]{:S(2)}, u32[]{:S(2)}) collective-permute-start(f32[64,1,2,768]{3,2,1,0:T(2,128)} %get-tuple-element.75), channel_id=1, source_target_pairs={{0,4},{4,0},{8,12},{12,8},{16,20},{20,16},{24,28},{28,24},{1,5},{5... | collective-permute-start | bytes 1179656 | tf_op jit(solution)/shard_map/ppermute | solution.py:292
  5.7 21.2 %collective-permute-start.5 = (f32[64,1,2,768]{3,2,1,0:T(2,128)S(1)}, f32[64,1,2,768]{3,2,1,0:T(2,128)}, u32[]{:S(2)}, u32[]{:S(2)}) collective-permute-start(f32[64,1,2,768]{3,2,1,0:T(2,128)S(1)} %get-tuple-element.73), channel_id=1, source_target_pairs={{0,4},{4,0},{8,12},{12,8},{16,20},{20,16},{24,28},{28,24},{1,5},{5... | collective-permute-start | bytes 1179656 | tf_op jit(solution)/shard_map/ppermute | solution.py:293
  5.8 17.8 %collective-permute-start.1 = (s32[3,12]{1,0:T(4,128)S(1)}, s32[3,12]{1,0:T(4,128)S(1)}, u32[]{:S(2)}, u32[]{:S(2)}) collective-permute-start(s32[3,12]{1,0:T(4,128)S(1)} %reshape.3), channel_id=1, source_target_pairs={{0,4},{4,0},{8,12},{12,8},{16,20},{20,16},{24,28},{28,24},{1,5},{5... | collective-permute-start | bytes 440 | tf_op jit(solution)/shard_map/ppermute | solution.py:300
  7.8 20.4 %collective-permute-start.3 = (f32[64,1,2,768]{3,2,1,0:T(2,128)}, f32[64,1,2,768]{3,2,1,0:T(2,128)}, u32[]{:S(2)}, u32[]{:S(2)}) collective-permute-start(f32[64,1,2,768]{3,2,1,0:T(2,128)} %get-tuple-element.74), channel_id=1, source_target_pairs={{0,2},{2,0},{1,3},{3,1},{4,6},{6,4},{5,7},{7,5},{8,10},{10,8},{9,1... | collective-permute-start | bytes 1179656 | tf_op jit(solution)/shard_map/ppermute | solution.py:291
  10.2 41.0 %collective-permute-start.2 = (f32[128,1,2,768]{3,2,1,0:T(2,128)}, f32[128,1,2,768]{3,2,1,0:T(2,128)S(1)}, u32[]{:S(2)}, u32[]{:S(2)}) collective-permute-start(f32[128,1,2,768]{3,2,1,0:T(2,128)} %slice.18), channel_id=1, source_target_pairs={{0,2},{2,0},{1,3},{3,1},{4,6},{6,4},{5,7},{7,5},{8,10},{10,8},{9,1... | collective-permute-start | bytes 2359304 | tf_op jit(solution)/shard_map/ppermute | solution.py:294
  23.5 12.1 %collective-permute-start.7 = (f32[1,2,96,512]{3,2,1,0:T(8,128)S(1)}, f32[1,2,96,512]{3,2,1,0:T(8,128)}, u32[]{:S(2)}, u32[]{:S(2)}) collective-permute-start(f32[1,2,96,512]{3,2,1,0:T(8,128)S(1)} %get-tuple-element.76), channel_id=1, source_target_pairs={{0,4},{4,0},{8,12},{12,8},{16,20},{20,16},{24,28},{28,24},{1,5},{5... | collective-permute-start | bytes 1179656 | tf_op jit(solution)/shard_map/ppermute | solution.py:282
  25.3 13.0 %collective-permute-start.8 = (f32[1,2,96,512]{3,2,1,0:T(8,128)S(1)}, f32[1,2,96,512]{3,2,1,0:T(8,128)}, u32[]{:S(2)}, u32[]{:S(2)}) collective-permute-start(f32[1,2,96,512]{3,2,1,0:T(8,128)S(1)} %get-tuple-element.77.refs_6_.refs_4_), channel_id=1, source_target_pairs={{0,8},{4,12},{8,24},{12,28},{24,16},{28,20},{16,0},{20,4},{1,9},{5... | collective-permute-start | bytes 1179656 | tf_op jit(solution)/shard_map/ppermute | solution.py:284
  26.9 20.8 %collective-permute-start.9 = (f32[1,2,96,512]{3,2,1,0:T(8,128)S(1)}, f32[1,2,96,512]{3,2,1,0:T(8,128)S(1)}, u32[]{:S(2)}, u32[]{:S(2)}) collective-permute-start(f32[1,2,96,512]{3,2,1,0:T(8,128)S(1)} %get-tuple-element.77.refs_6_.refs_4_), channel_id=1, source_target_pairs={{0,16},{4,20},{8,0},{12,4},{24,8},{28,12},{16,24},{20,28},{1,17},{... | collective-permute-start | bytes 1179656 | tf_op jit(solution)/shard_map/ppermute | solution.py:285
  28.2 21.7 %collective-permute-start.6 = (f32[64,1,2,768]{3,2,1,0:T(2,128)}, f32[64,1,2,768]{3,2,1,0:T(2,128)S(1)}, u32[]{:S(2)}, u32[]{:S(2)}) collective-permute-start(f32[64,1,2,768]{3,2,1,0:T(2,128)} %get-tuple-element.74), channel_id=1, source_target_pairs={{0,4},{4,0},{8,12},{12,8},{16,20},{20,16},{24,28},{28,24},{1,5},{5... | collective-permute-start | bytes 1179656 | tf_op jit(solution)/shard_map/ppermute | solution.py:296
  35.6 17.2 %collective-permute-start.13 = (f32[1,2,96,512]{3,2,1,0:T(8,128)}, f32[1,2,96,512]{3,2,1,0:T(8,128)S(1)}, u32[]{:S(2)}, u32[]{:S(2)}) collective-permute-start(f32[1,2,96,512]{3,2,1,0:T(8,128)} %collective-permute-done.7.refs_7_.refs_5_), channel_id=1, source_target_pairs={{0,8},{4,12},{8,24},{12,28},{24,16},{28,20},{16,0},{20,4},{1,9},{5... | collective-permute-start | bytes 1179656 | tf_op jit(solution)/shard_map/ppermute | solution.py:284
  38.3 26.5 %collective-permute-start.12 = (f32[64,1,2,768]{3,2,1,0:T(2,128)}, f32[64,1,2,768]{3,2,1,0:T(2,128)}, u32[]{:S(2)}, u32[]{:S(2)}) collective-permute-start(f32[64,1,2,768]{3,2,1,0:T(2,128)} %collective-permute-done.3.refs_1_), channel_id=1, source_target_pairs={{0,4},{4,0},{8,12},{12,8},{16,20},{20,16},{24,28},{28,24},{1,5},{5... | collective-permute-start | bytes 1179656 | tf_op jit(solution)/shard_map/ppermute | solution.py:295
  48.4 19.2 %collective-permute-start.10 = (f32[64,1,2,768]{3,2,1,0:T(2,128)}, f32[64,1,2,768]{3,2,1,0:T(2,128)}, u32[]{:S(2)}, u32[]{:S(2)}) collective-permute-start(f32[64,1,2,768]{3,2,1,0:T(2,128)} %collective-permute-done.4.refs_0_), channel_id=1, source_target_pairs={{0,2},{2,0},{1,3},{3,1},{4,6},{6,4},{5,7},{7,5},{8,10},{10,8},{9,1... | collective-permute-start | bytes 1179656 | tf_op jit(solution)/shard_map/ppermute | solution.py:297
  50.7 17.5 %collective-permute-start.11 = (f32[64,1,2,768]{3,2,1,0:T(2,128)}, f32[64,1,2,768]{3,2,1,0:T(2,128)}, u32[]{:S(2)}, u32[]{:S(2)}) collective-permute-start(f32[64,1,2,768]{3,2,1,0:T(2,128)} %collective-permute-done.5.refs_1_), channel_id=1, source_target_pairs={{0,2},{2,0},{1,3},{3,1},{4,6},{6,4},{5,7},{7,5},{8,10},{10,8},{9,1... | collective-permute-start | bytes 1179656 | tf_op jit(solution)/shard_map/ppermute | solution.py:298
  51.2 20.8 %collective-permute-start.15 = (f32[1,2,96,512]{3,2,1,0:T(8,128)}, f32[1,2,96,512]{3,2,1,0:T(8,128)S(1)}, u32[]{:S(2)}, u32[]{:S(2)}) collective-permute-start(f32[1,2,96,512]{3,2,1,0:T(8,128)} %collective-permute-done.8.refs_8_.refs_6_), channel_id=1, source_target_pairs={{0,8},{4,12},{8,24},{12,28},{24,16},{28,20},{16,0},{20,4},{1,9},{5... | collective-permute-start | bytes 1179656 | tf_op jit(solution)/shard_map/ppermute | solution.py:286
  52.8 20.2 %collective-permute-start.14 = (f32[1,2,96,512]{3,2,1,0:T(8,128)}, f32[1,2,96,512]{3,2,1,0:T(8,128)S(1)}, u32[]{:S(2)}, u32[]{:S(2)}) collective-permute-start(f32[1,2,96,512]{3,2,1,0:T(8,128)} %collective-permute-done.7.refs_7_.refs_5_), channel_id=1, source_target_pairs={{0,16},{4,20},{8,0},{12,4},{24,8},{28,12},{16,24},{20,28},{1,17},{... | collective-permute-start | bytes 1179656 | tf_op jit(solution)/shard_map/ppermute | solution.py:285
  64.8 12.8 %collective-permute-start.18 = (f32[1,2,96,384]{3,2,1,0:T(8,128)S(1)}, f32[1,2,96,384]{3,2,1,0:T(8,128)S(1)}, u32[]{:S(2)}, u32[]{:S(2)}) collective-permute-start(f32[1,2,96,384]{3,2,1,0:T(8,128)S(1)} %slice.25), channel_id=1, source_target_pairs={{0,8},{4,12},{8,24},{12,28},{24,16},{28,20},{16,0},{20,4},{1,9},{5... | collective-permute-start | bytes 884744 | tf_op jit(solution)/shard_map/ppermute | solution.py:287
  78.4 10.5 %collective-permute-start.19 = (f32[2,192,384]{2,1,0:T(8,128)S(1)}, f32[2,192,384]{2,1,0:T(8,128)S(1)}, u32[]{:S(2)}, u32[]{:S(2)}) collective-permute-start(f32[2,192,384]{2,1,0:T(8,128)S(1)} %get-tuple-element.66), channel_id=1, source_target_pairs={{0,1},{1,0},{2,3},{3,2},{4,5},{5,4},{6,7},{7,6},{8,9},{9,8},{10,11... | collective-permute-start | bytes 1769480 | tf_op jit(solution)/shard_map/ppermute | solution.py:361
  78.6 6.1 %collective-permute-start.16 = (f32[1,2,96,128]{3,2,1,0:T(8,128)S(1)}, f32[1,2,96,128]{3,2,1,0:T(8,128)S(1)}, u32[]{:S(2)}, u32[]{:S(2)}) collective-permute-start(f32[1,2,96,128]{3,2,1,0:T(8,128)S(1)} %slice.24), channel_id=1, source_target_pairs={{0,8},{4,12},{8,24},{12,28},{24,16},{28,20},{16,0},{20,4},{1,9},{5... | collective-permute-start | bytes 294920 | tf_op jit(solution)/shard_map/ppermute | solution.py:288
  85.2 6.2 %collective-permute-start.17 = (f32[4,192,128]{2,1,0:T(8,128)S(1)}, f32[4,192,128]{2,1,0:T(8,128)S(1)}, u32[]{:S(2)}, u32[]{:S(2)}) collective-permute-start(f32[4,192,128]{2,1,0:T(8,128)S(1)} %shard_map.53.mine), channel_id=1, source_target_pairs={{0,1},{1,0},{2,3},{3,2},{4,5},{5,4},{6,7},{7,6},{8,9},{9,8},{10,11... | collective-permute-start | bytes 1179656 | tf_op jit(solution)/shard_map/ppermute | solution.py:363
  85.3 3.7 %collective-permute-start = (s32[3,8]{1,0:T(4,128)S(1)}, s32[3,8]{1,0:T(4,128)S(1)}, u32[]{:S(2)}, u32[]{:S(2)}) collective-permute-start(s32[3,8]{1,0:T(4,128)S(1)} %copy-done.7), channel_id=1, source_target_pairs={{0,4},{4,0},{8,12},{12,8},{16,20},{20,16},{24,28},{28,24},{1,5},{5... | collective-permute-start | bytes 296 | tf_op jit(solution)/shard_map/ppermute | solution.py:301
  89.6 15.7 %collective-permute-start.24 = (f32[192,384]{1,0:T(8,128)S(1)}, f32[192,384]{1,0:T(8,128)S(1)}, u32[]{:S(2)}, u32[]{:S(2)}) collective-permute-start(f32[192,384]{1,0:T(8,128)S(1)} %get-tuple-element.71), channel_id=1, source_target_pairs={{0,4},{4,0},{8,12},{12,8},{16,20},{20,16},{24,28},{28,24},{1,5},{5... | collective-permute-start | bytes 884744 | tf_op jit(solution)/shard_map/ppermute | solution.py:367
  92.1 13.3 %collective-permute-start.25 = (f32[192,128]{1,0:T(8,128)S(1)}, f32[192,128]{1,0:T(8,128)S(1)}, u32[]{:S(2)}, u32[]{:S(2)}) collective-permute-start(f32[192,128]{1,0:T(8,128)S(1)} %get-tuple-element.72), channel_id=1, source_target_pairs={{0,4},{4,0},{8,12},{12,8},{16,20},{20,16},{24,28},{28,24},{1,5},{5... | collective-permute-start | bytes 294920 | tf_op jit(solution)/shard_map/ppermute | solution.py:374
  93.7 3.6 %collective-permute-start.21 = (f32[1,512]{1,0:T(1,128)S(1)}, f32[1,512]{1,0:T(1,128)S(1)}, u32[]{:S(2)}, u32[]{:S(2)}) collective-permute-start(f32[1,512]{1,0:T(1,128)S(1)} %get-tuple-element.68), channel_id=1, source_target_pairs={{0,8},{4,12},{8,0},{12,4},{16,24},{20,28},{24,16},{28,20},{1,9},{5... | collective-permute-start | bytes 6152 | tf_op jit(solution)/shard_map/ppermute | solution.py:376
  97.3 4.5 %collective-permute-start.22 = (f32[1,512]{1,0:T(1,128)S(1)}, f32[1,512]{1,0:T(1,128)S(1)}, u32[]{:S(2)}, u32[]{:S(2)}) collective-permute-start(f32[1,512]{1,0:T(1,128)S(1)} %add.10), channel_id=1, source_target_pairs={{0,16},{4,20},{8,24},{12,28},{16,0},{20,4},{24,8},{28,12},{1,17},{... | collective-permute-start | bytes 6152 | tf_op jit(solution)/shard_map/ppermute | solution.py:376
  (10 other events, 44.8 us)
where the time goes:
time: 107 us; the launch traced here: 106 us
  waiting for transfers between devices  53.5 us (50%)
  starting transfers between devices  25.4 us (24%)
  Pallas kernels  21.8 us (20%)
  local copies, waits for them, and re-layouts  5.38 us (5%)
    pallas_call x12, Pallas kernels, run(): pl.pallas_call(kernel, out_shape=out_shapes, in_specs=specs, out_specs=[V...  21.8 us
    ppermute x1, waiting for transfers between devices, local(): a_table = jnp.stack([a_table, lax.ppermute(a_table, 'row', swap_y)])  12.7 us
    ppermute x2, waiting for transfers between devices, local(): shards[1, turn] = lax.ppermute(shards[0, turn], 'row', line_pairs(-1))  9.76 us
    ppermute x2, waiting for transfers between devices, local(): lax.ppermute(sums, 'row', [(r, r ^ bit) for r in range(n_row)])  7.47 us
    ppermute x1, waiting for transfers between devices, local(): shards[0, 1] = lax.ppermute(gives, 'row', swap_y)  7.13 us
    ppermute x1, waiting for transfers between devices, local(): far_last = lax.ppermute(shards[-1, 1][..., cut:], 'row', line_pairs(1))  6.08 us
    ppermute x2, starting transfers between devices, local(): shards[1, turn] = lax.ppermute(shards[0, turn], 'row', line_pairs(-1))  5.29 us
    ppermute x2, starting transfers between devices, local(): shards[-1, turn] = lax.ppermute(shards[0, turn], 'row', line_pairs(1))  3.38 us
  transfers between devices with their start and end apart: 26, of which 14 were waited for; matrix products, arithmetic and copies ran while one was open for 1% of the time, Pallas kernels for 19%

commit v1 on v0

--- a/solution.py
+++ b/solution.py
@@ -93,7 +93,7 @@
     return dot(a_high, b_high) + (dot(a_high, b_low) + dot(a_low, b_high))
 
 
-def left_kernel(groups, plan, pattern, *refs):
+def left_kernel(groups, plan, pattern, other_pattern, *refs):
     sources, outs, turned = refs[: len(plan)], refs[len(plan) : -1], refs[-1]
     _, _, sections, width = sources[0].shape
     n_row, row, col = lax.axis_size("row"), lax.axis_index("row"), lax.axis_index("col")
@@ -107,7 +107,7 @@
             for s in range(sections):
                 kept = []
                 for w in range(width // BLK):
-                    keep = pattern[which, block_row, s * (width // BLK) + w]
+                    keep = (pattern, other_pattern)[which][block_row, 0, s, w]
                     kept.append(jnp.where(keep != 0, source[part, 0, s, pl.ds(w * BLK, BLK)], 0.0))
                 value = jnp.concatenate(kept, axis=1)
                 for r in range(n_row):
@@ -151,7 +151,8 @@
 
 
 def far_value(first, *refs):
-    highs, lows, (near, near_late, shard, b_high, b_low) = refs[:4], refs[4:8], refs[8:]
+    *lefts, near, near_late, shard, b_high, b_low = refs
+    highs, lows = lefts[: len(lefts) // 2], lefts[len(lefts) // 2 :]
     put_shards([shard], b_high, b_low)
     value = product3(stacked(highs), stacked(lows), b_high[...], b_low[...])
     tile = slice(first, first + shard.shape[3])
@@ -181,15 +182,15 @@
         out[p] = value[p * rows : (p + 1) * rows]
 
 
-def squared(pattern, which, fiber, first, value):
+def squared(pattern, fiber, first, value):
     columns = value.shape[1]
-    half = lax.axis_index("row") % 2 * (pattern.shape[2] // 2)
+    half = lax.axis_index("row") % 2 * (pattern.shape[1] // 2)
     out = []
     for g in range(value.shape[0] // UNIT):
         block_row = (fiber * value.shape[0] + g * UNIT) // BLK
         kept = []
         for w in range(columns // BLK):
-            keep = pattern[which, block_row, half + first // BLK + w]
+            keep = pattern[block_row, half + first // BLK + w]
             piece = value[g * UNIT : (g + 1) * UNIT, w * BLK : (w + 1) * BLK]
             piece = jnp.where(keep != 0, piece, 0.0)
             kept.append(piece * piece)
@@ -197,21 +198,21 @@
     return jnp.concatenate(out, axis=0)
 
 
-def square_kernel(pattern, kept, received, stays, goes, sums):
+def square_kernel(pattern, other_pattern, kept, received, stays, goes, sums):
     fiber = lax.axis_index("fiber")
-    mine = squared(pattern, 0, fiber, 0, kept[0] + received[0])
-    other = squared(pattern, 1, fiber, 0, kept[1] + received[1])
+    mine = squared(pattern, fiber, 0, kept[0] + received[0])
+    other = squared(other_pattern, fiber, 0, kept[1] + received[1])
     stays[...], goes[...] = mine, other
     sums[...] = jnp.sum(mine, axis=0, keepdims=True) + jnp.sum(other, axis=0, keepdims=True)
 
 
-def square_last_kernel(first, pattern, mine, received, early, stays, goes, sums):
+def square_last_kernel(first, pattern, other_pattern, mine, received, early, stays, goes, sums):
     fiber, col = lax.axis_index("fiber"), lax.axis_index("col")
     total = None
-    for y, target in ((0, stays), (1, goes)):
+    for y, (table, target) in enumerate(((pattern, stays), (other_pattern, goes))):
         for block in (1 - fiber, fiber):
             p = 2 * y + (block ^ col)
-            value = squared(pattern, y, block, first, mine[p] + received[p])
+            value = squared(table, block, first, mine[p] + received[p])
             part = jnp.sum(value, axis=0, keepdims=True)
             total = part if total is None else total + part
         target[...] = value
@@ -256,7 +257,6 @@
 
 def local(a_panels, b_panels, a_pattern, c_pattern):
     rows, _, sections, _ = a_panels.shape
-    block_rows = a_pattern.shape[0]
     depth, columns = b_panels.shape[2:]
     n_row, n_col, fibers = (lax.axis_size(name) for name in ("row", "col", "fiber"))
     local_rows = rows * n_col
@@ -277,9 +277,10 @@
         sizes = (*b_panels.shape[:3], half)
         return lax.dynamic_slice(b_panels, where, sizes, allow_negative_indices=False)
 
-    own, gives = columns_half(my_y), columns_half(1 - my_y)
+    own = columns_half(my_y)
+    b_panels, own = together(b_panels, own)
     shards = {(0, 0): own}
-    shards[0, 1] = lax.ppermute(gives, "row", swap_y)
+    shards[0, 1] = lax.ppermute(columns_half(1 - my_y), "row", swap_y)
     for turn in range(2):
         shards[-1, turn] = lax.ppermute(shards[0, turn], "row", line_pairs(1))
         shards[1, turn] = lax.ppermute(shards[0, turn], "row", line_pairs(-1))
@@ -287,18 +288,15 @@
     far_early = lax.ppermute(shards[-1, 1][..., :cut], "row", line_pairs(1))
     far_last = lax.ppermute(shards[-1, 1][..., cut:], "row", line_pairs(1))
 
-    units = [a_panels[u * UNIT : (u + 1) * UNIT] for u in range(3)]
-    x2 = lax.ppermute(units[2], "col", swap)
-    y0 = lax.ppermute(units[0], "row", swap_y)
-    y1 = lax.ppermute(units[1], "row", swap_y)
-    x01 = lax.ppermute(a_panels[: 2 * UNIT], "col", swap)
-    d2 = lax.ppermute(x2, "row", swap_y)
-    y2 = lax.ppermute(units[2], "row", swap_y)
+    from_x = lax.ppermute(a_panels, "col", swap)
+    y0, y1, y2 = (
+        lax.ppermute(a_panels[u * UNIT : (u + 1) * UNIT], "row", swap_y) for u in range(3)
+    )
+    d2 = lax.ppermute(from_x[2 * UNIT :], "row", swap_y)
     d0 = lax.ppermute(y0, "col", swap)
     d1 = lax.ppermute(y1, "col", swap)
-    a_table = a_pattern.reshape(block_rows, -1)
-    a_table = jnp.stack([a_table, lax.ppermute(a_table, "row", swap_y)])
-    c_table = jnp.stack([c_pattern, lax.ppermute(c_pattern, "row", swap_y)])
+    a_tables = [a_pattern, lax.ppermute(a_pattern, "row", swap_y)]
+    c_tables = [c_pattern, lax.ppermute(c_pattern, "row", swap_y)]
 
     groups = [[(0, 0), (0, 1), (-1, 0), (1, 0)], [(-1, 1), (1, 1), (2, 0)], [(2, 1)]]
     shard_depth = sections * depth
@@ -311,14 +309,12 @@
         return call(
             functools.partial(left_kernel, groups, plan),
             parts,
-            [SMEM] + [VMEM] * len(arrays),
+            [SMEM] * 2 + [VMEM] * len(arrays),
             [pltpu.VMEM((n_row, sections, UNIT, depth), f32)],
-        )(a_table, *arrays)
+        )(a_pattern, a_tables[max(y for y, *_ in plan)], *arrays)
 
     early_sets = [
-        left((a_panels, 0, False, 0)),
-        left((x01, 0, True, 0), (x2, 0, True, 2 * UNIT)),
-        left((y0, 1, False, 0), (y1, 1, False, UNIT)),
+        left((a_panels, 0, False, 0)), left((from_x, 0, True, 0)), left((y0, 1, False, 0), (y1, 1, False, UNIT))
     ]
 
     def picked(sets, g):
@@ -338,14 +334,14 @@
         )(*lefts, *members, *near)
         return total
 
-    near = product(early_sets, [0])
-    y2, near = together(y2, near)
-    late_set = left((y2, 1, False, 2 * UNIT), (d0, 1, True, 0), (d1, 1, True, UNIT), (d2, 1, True, 2 * UNIT))
-
-    near = product(early_sets, [1], near)
-    near_late = product([late_set], [0, 1])
-
-    far_lefts = picked([*early_sets, late_set], 2)
+    near = product(early_sets, [1], product(early_sets, [0]))
+    d2, d1, near = together(d2, d1, near)
+    late_sets = [
+        left((y2, 1, False, 2 * UNIT)), left((d0, 1, True, 0)), left((d1, 1, True, UNIT)), left((d2, 1, True, 2 * UNIT))
+    ]
+    near_late = product(late_sets, [0, 1])
+
+    far_lefts = picked([*early_sets, *late_sets], 2)
 
     def far(kernel, first, shard, outs):
         factor = pltpu.VMEM((shard_depth, shard.shape[3]), bf16)
@@ -362,15 +358,15 @@
     (mine,) = far(last_kernel, cut, far_last, [shape((4, rows, LAST), f32)])
     theirs = lax.ppermute(mine, "fiber", swap)
     stays, goes, sums = call(
-        square_kernel, [shape((rows, cut), f32)] * 2 + [shape((1, cut), f32)], [SMEM, VMEM, VMEM]
-    )(c_table, kept, received)
+        square_kernel, [shape((rows, cut), f32)] * 2 + [shape((1, cut), f32)], [SMEM, SMEM, VMEM, VMEM]
+    )(*c_tables, kept, received)
     comes = lax.ppermute(goes, "row", swap_y)
     sums = sums + lax.ppermute(sums, "fiber", swap)
     last_stays, last_goes, sums = call(
         functools.partial(square_last_kernel, cut),
         [shape((rows, LAST), f32)] * 2 + [shape((1, half), f32)],
-        [SMEM, VMEM, VMEM, VMEM],
-    )(c_table, mine, theirs, sums)
+        [SMEM, SMEM, VMEM, VMEM, VMEM],
+    )(*c_tables, mine, theirs, sums)
     last_comes = lax.ppermute(last_goes, "row", swap_y)
     for bit in (2, 4):
         sums = sums + lax.ppermute(sums, "row", [(r, r ^ bit) for r in range(n_row)])

time: 107 us -> 121 us (1.13)
  waiting for transfers between devices: 53.5 us -> 63 us
  starting transfers between devices: 25.4 us -> 34.1 us
  local copies, waits for them, and re-layouts: 5.38 us -> 2.43 us
    ppermute x2, waiting for transfers between devices: 1.82 us -> 23.4 us  [local(): shards[-1, turn] = lax.ppermute(shards[0, turn], 'row', line_pairs(1))]
    ppermute x2, waiting for transfers between devices: 9.76 us -> 0.01 us  [local(): shards[1, turn] = lax.ppermute(shards[0, turn], 'row', line_pairs(-1))]
    ppermute x9 -> x8, waiting for transfers between devices: 22.9 us -> 29.2 us  [the longest x1 23.5 us: local(): a_tables = [a_pattern, lax.ppermute(a_pattern, 'row', swap_y)]]
    ppermute x2, starting transfers between devices: 0.6 us -> 4.07 us  [local(): lax.ppermute(sums, 'row', [(r, r ^ bit) for r in range(n_row)])]
    ppermute x1, starting transfers between devices: 0.06 us -> 3.43 us  [local(): far_last = lax.ppermute(shards[-1, 1][..., cut:], 'row', line_pairs(1))]
    ppermute x1, waiting for transfers between devices: 6.08 us -> 2.71 us  [local(): far_last = lax.ppermute(shards[-1, 1][..., cut:], 'row', line_pairs(1))]
    ppermute x2, waiting for transfers between devices: 7.47 us -> 4.46 us  [local(): lax.ppermute(sums, 'row', [(r, r ^ bit) for r in range(n_row)])]
    ppermute x1, starting transfers between devices: 0.24 us -> 2.15 us  [local(): far_early = lax.ppermute(shards[-1, 1][..., :cut], 'row', line_pairs(1))]
  transfers between devices with their start and end apart: 26 -> 25, of which waited for: 14 -> 10; matrix products, arithmetic and copies ran while one was open for 1% -> 2% of each run, Pallas kernels for 19% -> 16%
where the time goes in v1:
time: 121 us
  waiting for transfers between devices  63 us (52%)
  starting transfers between devices  34.1 us (28%)
  Pallas kernels  20.7 us (17%)
  local copies, waits for them, and re-layouts  2.43 us (2%)
    ppermute x1, waiting for transfers between devices, local(): a_tables = [a_pattern, lax.ppermute(a_pattern, 'row', swap_y)]  23.5 us
    ppermute x2, waiting for transfers between devices, local(): shards[-1, turn] = lax.ppermute(shards[0, turn], 'row', line_pairs(1))  23.4 us
    pallas_call x15, Pallas kernels, run(): pl.pallas_call(kernel, out_shape=out_shapes, in_specs=specs, out_specs=[V...  20.7 us
    ppermute x2, waiting for transfers between devices, local(): lax.ppermute(sums, 'row', [(r, r ^ bit) for r in range(n_row)])  4.46 us
    ppermute x2, starting transfers between devices, local(): shards[1, turn] = lax.ppermute(shards[0, turn], 'row', line_pairs(-1))  4.18 us
    ppermute x2, starting transfers between devices, local(): shards[-1, turn] = lax.ppermute(shards[0, turn], 'row', line_pairs(1))  4.17 us
    ppermute x2, starting transfers between devices, local(): lax.ppermute(sums, 'row', [(r, r ^ bit) for r in range(n_row)])  4.07 us
    ppermute x3, waiting for transfers between devices, local(): lax.ppermute(a_panels[u * UNIT:(u + 1) * UNIT], 'row', swap_y)  3.7 us
  transfers between devices with their start and end apart: 25, of which 10 were waited for; matrix products, arithmetic and copies ran while one was open for 2% of the time, Pallas kernels for 16%

profile of v1, /device:TPU:0, one launch (start us, length us, event | category | flops | bytes accessed | tf_op | source)
XLA Modules:
  0.0 120.6 jit_solution(7191441738506440217)
XLA Ops:
  0.0 3.0 %collective-permute-start.1 = (f32[192,1,2,768]{3,2,1,0:T(2,128)}, f32[192,1,2,768]{3,2,1,0:T(2,128)S(1)}, u32[]{:S(2)}, u32[]{:S(2)}) collective-permute-start(f32[192,1,2,768]{3,2,1,0:T(2,128)} %refs_0_.1), channel_id=1, source_target_pairs={{0,2},{2,0},{1,3},{3,1},{4,6},{6,4},{5,7},{7,5},{8,10},{10,8},{9,1... | collective-permute-start | bytes 3538952 | tf_op jit(solution)/shard_map/ppermute | solution.py:291
  3.0 2.3 %fusion = (f32[64,1,2,768]{3,2,1,0:T(2,128)}, f32[64,1,2,768]{3,2,1,0:T(2,128)}, f32[64,1,2,768]{3,2,1,0:T(2,128)}) fusion(f32[192,1,2,768]{3,2,1,0:T(2,128)} %refs_0_.1), kind=kLoop, calls=%fused_computation.2 | loop fusion | bytes 2359296 | tf_op jit(solution)/shard_map/slice | solution.py:293
  7.4 1.6 %collective-permute-start.9 = (f32[1,2,96,512]{3,2,1,0:T(8,128)S(1)}, f32[1,2,96,512]{3,2,1,0:T(8,128)S(1)}, u32[]{:S(2)}, u32[]{:S(2)}) collective-permute-start(f32[1,2,96,512]{3,2,1,0:T(8,128)S(1)} %constant_dynamic-slice_fusion), channel_id=1, source_target_pairs={{0,4},{4,0},{8,12},{12,8},{16,20},{20,16},{24,28},{28,24},{1,5},{5... | collective-permute-start | bytes 1179656 | tf_op jit(solution)/shard_map/ppermute | solution.py:283
  9.5 23.5 %collective-permute-done.2.other_pattern = s32[3,1,2,6]{3,2,1,0:T(2,128)S(1)} collective-permute-done((s32[3,1,2,6]{3,2,1,0:T(2,128)S(1)}, s32[3,1,2,6]{3,2,1,0:T(2,128)S(1)}, u32[]{:S(2)}, u32[]{:S(2)}) %collective-permute-start.2) | collective-permute-done | bytes 176 | tf_op jit(solution)/shard_map/ppermute | solution.py:298
  34.5 1.6 %collective-permute-start.12 = (f32[1,2,96,512]{3,2,1,0:T(8,128)S(1)}, f32[1,2,96,512]{3,2,1,0:T(8,128)S(1)}, u32[]{:S(2)}, u32[]{:S(2)}) collective-permute-start(f32[1,2,96,512]{3,2,1,0:T(8,128)S(1)} %constant_dynamic-slice_fusion.1.refs_6_.refs_16_), channel_id=1, source_target_pairs={{0,8},{4,12},{8,24},{12,28},{24,16},{28,20},{16,0},{20,4},{1,9},{5... | collective-permute-start | bytes 1179656 | tf_op jit(solution)/shard_map/ppermute | solution.py:285
  36.6 2.6 %collective-permute-start.10 = (f32[1,2,96,512]{3,2,1,0:T(8,128)S(1)}, f32[1,2,96,512]{3,2,1,0:T(8,128)S(1)}, u32[]{:S(2)}, u32[]{:S(2)}) collective-permute-start(f32[1,2,96,512]{3,2,1,0:T(8,128)S(1)} %collective-permute-done.9.refs_7_.refs_17_), channel_id=1, source_target_pairs={{0,8},{4,12},{8,24},{12,28},{24,16},{28,20},{16,0},{20,4},{1,9},{5... | collective-permute-start | bytes 1179656 | tf_op jit(solution)/shard_map/ppermute | solution.py:285
  39.2 3.7 %collective-permute-done.5.refs_0_ = f32[64,1,2,768]{3,2,1,0:T(2,128)S(1)} collective-permute-done((f32[64,1,2,768]{3,2,1,0:T(2,128)}, f32[64,1,2,768]{3,2,1,0:T(2,128)S(1)}, u32[]{:S(2)}, u32[]{:S(2)}) %collective-permute-start.5) | collective-permute-done | bytes 393248 | tf_op jit(solution)/shard_map/ppermute | solution.py:293
  42.9 2.6 %collective-permute-start.14 = (f32[1,2,96,512]{3,2,1,0:T(8,128)S(1)}, f32[1,2,96,512]{3,2,1,0:T(8,128)S(1)}, u32[]{:S(2)}, u32[]{:S(2)}) collective-permute-start(f32[1,2,96,512]{3,2,1,0:T(8,128)S(1)} %constant_dynamic-slice_fusion.1.refs_6_.refs_16_), channel_id=1, source_target_pairs={{0,16},{4,20},{8,0},{12,4},{24,8},{28,12},{16,24},{20,28},{1,17},{... | collective-permute-start | bytes 1179656 | tf_op jit(solution)/shard_map/ppermute | solution.py:286
  45.5 2.0 %collective-permute-done.12.refs_8_.refs_18_ = f32[1,2,96,512]{3,2,1,0:T(8,128)S(1)} collective-permute-done((f32[1,2,96,512]{3,2,1,0:T(8,128)S(1)}, f32[1,2,96,512]{3,2,1,0:T(8,128)S(1)}, u32[]{:S(2)}, u32[]{:S(2)}) %collective-permute-start.12) | collective-permute-done | bytes 393248 | tf_op jit(solution)/shard_map/ppermute | solution.py:285
  47.5 1.6 %collective-permute-start.11 = (f32[1,2,96,512]{3,2,1,0:T(8,128)S(1)}, f32[1,2,96,512]{3,2,1,0:T(8,128)S(1)}, u32[]{:S(2)}, u32[]{:S(2)}) collective-permute-start(f32[1,2,96,512]{3,2,1,0:T(8,128)S(1)} %collective-permute-done.9.refs_7_.refs_17_), channel_id=1, source_target_pairs={{0,16},{4,20},{8,0},{12,4},{24,8},{28,12},{16,24},{20,28},{1,17},{... | collective-permute-start | bytes 1179656 | tf_op jit(solution)/shard_map/ppermute | solution.py:286
  50.1 21.4 %collective-permute-done.10.refs_6_.refs_20_ = f32[1,2,96,512]{3,2,1,0:T(8,128)S(1)} collective-permute-done((f32[1,2,96,512]{3,2,1,0:T(8,128)S(1)}, f32[1,2,96,512]{3,2,1,0:T(8,128)S(1)}, u32[]{:S(2)}, u32[]{:S(2)}) %collective-permute-start.10) | collective-permute-done | bytes 393248 | tf_op jit(solution)/shard_map/ppermute | solution.py:285
  72.1 2.5 %shard_map.46 = (bf16[192,768]{1,0:T(8,128)(2,1)S(1)}, bf16[192,768]{1,0:T(8,128)(2,1)S(1)}, bf16[192,576]{1,0:T(8,128)(2,1)S(1)}, bf16[192,576]{1,0:T(8,128)(2,...) custom-call(s32[3,1,2,6]{3,2,1,0:T(2,128)S(1)} %copy-done.2, s32[3,1,2,6]{3,2,1,0:T(2,128)S(1)} %copy-done.2, ...), custom_call_target="tpu_custom_call" | custom-call | bytes 2359584 | tf_op jit(solution)/shard_map/pallas_call | solution.py:245
  74.6 2.4 %shard_map.48 = (bf16[128,768]{1,0:T(8,128)(2,1)S(1)}, bf16[128,768]{1,0:T(8,128)(2,1)S(1)}, bf16[128,576]{1,0:T(8,128)(2,1)S(1)}, bf16[128,576]{1,0:T(8,128)(2,...) custom-call(s32[3,1,2,6]{3,2,1,0:T(2,128)S(1)} %copy-done.2, ...), custom_call_target="tpu_custom_call" | custom-call | bytes 1573152 | tf_op jit(solution)/shard_map/pallas_call | solution.py:245
  79.7 2.5 %shard_map.47 = (bf16[192,768]{1,0:T(8,128)(2,1)S(1)}, bf16[192,768]{1,0:T(8,128)(2,1)S(1)}, bf16[192,576]{1,0:T(8,128)(2,1)S(1)}, bf16[192,576]{1,0:T(8,128)(2,...) custom-call(s32[3,1,2,6]{3,2,1,0:T(2,128)S(1)} %copy-done.2, s32[3,1,2,6]{3,2,1,0:T(2,128)S(1)} %copy-done.2, ...), custom_call_target="tpu_custom_call" | custom-call | bytes 2359584 | tf_op jit(solution)/shard_map/pallas_call | solution.py:245
  82.3 2.2 %collective-permute-start.17 = (f32[1,2,96,384]{3,2,1,0:T(8,128)S(1)}, f32[1,2,96,384]{3,2,1,0:T(8,128)S(1)}, u32[]{:S(2)}, u32[]{:S(2)}) collective-permute-start(f32[1,2,96,384]{3,2,1,0:T(8,128)S(1)} %slice.26), channel_id=1, source_target_pairs={{0,8},{4,12},{8,24},{12,28},{24,16},{28,20},{16,0},{20,4},{1,9},{5... | collective-permute-start | bytes 884744 | tf_op jit(solution)/shard_map/ppermute | solution.py:288
  92.3 3.4 %collective-permute-start.15 = (f32[1,2,96,128]{3,2,1,0:T(8,128)S(1)}, f32[1,2,96,128]{3,2,1,0:T(8,128)S(1)}, u32[]{:S(2)}, u32[]{:S(2)}) collective-permute-start(f32[1,2,96,128]{3,2,1,0:T(8,128)S(1)} %slice.25), channel_id=1, source_target_pairs={{0,8},{4,12},{8,24},{12,28},{24,16},{28,20},{16,0},{20,4},{1,9},{5... | collective-permute-start | bytes 294920 | tf_op jit(solution)/shard_map/ppermute | solution.py:289
  95.8 2.7 %collective-permute-done.15.refs_16_ = f32[1,2,96,128]{3,2,1,0:T(8,128)S(1)} collective-permute-done((f32[1,2,96,128]{3,2,1,0:T(8,128)S(1)}, f32[1,2,96,128]{3,2,1,0:T(8,128)S(1)}, u32[]{:S(2)}, u32[]{:S(2)}) %collective-permute-start.15) | collective-permute-done | bytes 98336 | tf_op jit(solution)/shard_map/ppermute | solution.py:289
  99.1 1.6 %collective-permute-start = (s32[3,8]{1,0:T(4,128)S(1)}, s32[3,8]{1,0:T(4,128)S(1)}, u32[]{:S(2)}, u32[]{:S(2)}) collective-permute-start(s32[3,8]{1,0:T(4,128)S(1)} %copy-done.3), channel_id=1, source_target_pairs={{0,4},{4,0},{8,12},{12,8},{16,20},{20,16},{24,28},{28,24},{1,5},{5... | collective-permute-start | bytes 296 | tf_op jit(solution)/shard_map/ppermute | solution.py:299
  100.7 2.0 %collective-permute-done.other_pattern = s32[3,8]{1,0:T(4,128)S(1)} collective-permute-done((s32[3,8]{1,0:T(4,128)S(1)}, s32[3,8]{1,0:T(4,128)S(1)}, u32[]{:S(2)}, u32[]{:S(2)}) %collective-permute-start) | collective-permute-done | bytes 128 | tf_op jit(solution)/shard_map/ppermute | solution.py:299
  103.4 1.6 %collective-permute-start.23 = (f32[192,384]{1,0:T(8,128)S(1)}, f32[192,384]{1,0:T(8,128)S(1)}, u32[]{:S(2)}, u32[]{:S(2)}) collective-permute-start(f32[192,384]{1,0:T(8,128)S(1)} %get-tuple-element.113), channel_id=1, source_target_pairs={{0,4},{4,0},{8,12},{12,8},{16,20},{20,16},{24,28},{28,24},{1,5},{5... | collective-permute-start | bytes 884744 | tf_op jit(solution)/shard_map/ppermute | solution.py:363
  107.5 2.5 %collective-permute-start.20 = (f32[1,512]{1,0:T(1,128)S(1)}, f32[1,512]{1,0:T(1,128)S(1)}, u32[]{:S(2)}, u32[]{:S(2)}) collective-permute-start(f32[1,512]{1,0:T(1,128)S(1)} %get-tuple-element.110), channel_id=1, source_target_pairs={{0,8},{4,12},{8,0},{12,4},{16,24},{20,28},{24,16},{28,20},{1,9},{5... | collective-permute-start | bytes 6152 | tf_op jit(solution)/shard_map/ppermute | solution.py:372
  111.5 1.6 %collective-permute-start.21 = (f32[1,512]{1,0:T(1,128)S(1)}, f32[1,512]{1,0:T(1,128)S(1)}, u32[]{:S(2)}, u32[]{:S(2)}) collective-permute-start(f32[1,512]{1,0:T(1,128)S(1)} %add.10), channel_id=1, source_target_pairs={{0,16},{4,20},{8,24},{12,28},{16,0},{20,4},{24,8},{28,12},{1,17},{... | collective-permute-start | bytes 6152 | tf_op jit(solution)/shard_map/ppermute | solution.py:372
  113.1 2.9 %collective-permute-done.21 = f32[1,512]{1,0:T(1,128)S(1)} collective-permute-done((f32[1,512]{1,0:T(1,128)S(1)}, f32[1,512]{1,0:T(1,128)S(1)}, u32[]{:S(2)}, u32[]{:S(2)}) %collective-permute-start.21) | collective-permute-done | bytes 2080 | tf_op jit(solution)/shard_map/ppermute | solution.py:372
  117.5 2.0 %collective-permute-done.22.other_sums = f32[1,512]{1,0:T(1,128)S(1)} collective-permute-done((f32[1,512]{1,0:T(1,128)S(1)}, f32[1,512]{1,0:T(1,128)S(1)}, u32[]{:S(2)}, u32[]{:S(2)}) %collective-permute-start.22) | collective-permute-done | bytes 2080 | tf_op jit(solution)/shard_map/ppermute | solution.py:373
  (58 shorter events, 24.5 us)
Async XLA Ops:
  0.0 49.1 %collective-permute-start.1 = (f32[192,1,2,768]{3,2,1,0:T(2,128)}, f32[192,1,2,768]{3,2,1,0:T(2,128)S(1)}, u32[]{:S(2)}, u32[]{:S(2)}) collective-permute-start(f32[192,1,2,768]{3,2,1,0:T(2,128)} %refs_0_.1), channel_id=1, source_target_pairs={{0,2},{2,0},{1,3},{3,1},{4,6},{6,4},{5,7},{7,5},{8,10},{10,8},{9,1... | collective-permute-start | bytes 3538952 | tf_op jit(solution)/shard_map/ppermute | solution.py:291
  5.2 29.2 %collective-permute-start.3 = (f32[64,1,2,768]{3,2,1,0:T(2,128)}, f32[64,1,2,768]{3,2,1,0:T(2,128)}, u32[]{:S(2)}, u32[]{:S(2)}) collective-permute-start(f32[64,1,2,768]{3,2,1,0:T(2,128)} %get-tuple-element.116), channel_id=1, source_target_pairs={{0,4},{4,0},{8,12},{12,8},{16,20},{20,16},{24,28},{28,24},{1,5},{5... | collective-permute-start | bytes 1179656 | tf_op jit(solution)/shard_map/ppermute | solution.py:293
  6.8 29.3 %collective-permute-start.4 = (f32[64,1,2,768]{3,2,1,0:T(2,128)}, f32[64,1,2,768]{3,2,1,0:T(2,128)}, u32[]{:S(2)}, u32[]{:S(2)}) collective-permute-start(f32[64,1,2,768]{3,2,1,0:T(2,128)} %get-tuple-element.117), channel_id=1, source_target_pairs={{0,4},{4,0},{8,12},{12,8},{16,20},{20,16},{24,28},{28,24},{1,5},{5... | collective-permute-start | bytes 1179656 | tf_op jit(solution)/shard_map/ppermute | solution.py:293
  7.4 29.2 %collective-permute-start.9 = (f32[1,2,96,512]{3,2,1,0:T(8,128)S(1)}, f32[1,2,96,512]{3,2,1,0:T(8,128)S(1)}, u32[]{:S(2)}, u32[]{:S(2)}) collective-permute-start(f32[1,2,96,512]{3,2,1,0:T(8,128)S(1)} %constant_dynamic-slice_fusion), channel_id=1, source_target_pairs={{0,4},{4,0},{8,12},{12,8},{16,20},{20,16},{24,28},{28,24},{1,5},{5... | collective-permute-start | bytes 1179656 | tf_op jit(solution)/shard_map/ppermute | solution.py:283
  8.9 24.0 %collective-permute-start.2 = (s32[3,1,2,6]{3,2,1,0:T(2,128)S(1)}, s32[3,1,2,6]{3,2,1,0:T(2,128)S(1)}, u32[]{:S(2)}, u32[]{:S(2)}) collective-permute-start(s32[3,1,2,6]{3,2,1,0:T(2,128)S(1)} %copy-done.2), channel_id=1, source_target_pairs={{0,4},{4,0},{8,12},{12,8},{16,20},{20,16},{24,28},{28,24},{1,5},{5... | collective-permute-start | bytes 440 | tf_op jit(solution)/shard_map/ppermute | solution.py:298
  33.0 9.9 %collective-permute-start.5 = (f32[64,1,2,768]{3,2,1,0:T(2,128)}, f32[64,1,2,768]{3,2,1,0:T(2,128)S(1)}, u32[]{:S(2)}, u32[]{:S(2)}) collective-permute-start(f32[64,1,2,768]{3,2,1,0:T(2,128)} %get-tuple-element.115), channel_id=1, source_target_pairs={{0,4},{4,0},{8,12},{12,8},{16,20},{20,16},{24,28},{28,24},{1,5},{5... | collective-permute-start | bytes 1179656 | tf_op jit(solution)/shard_map/ppermute | solution.py:293
  34.5 13.0 %collective-permute-start.12 = (f32[1,2,96,512]{3,2,1,0:T(8,128)S(1)}, f32[1,2,96,512]{3,2,1,0:T(8,128)S(1)}, u32[]{:S(2)}, u32[]{:S(2)}) collective-permute-start(f32[1,2,96,512]{3,2,1,0:T(8,128)S(1)} %constant_dynamic-slice_fusion.1.refs_6_.refs_16_), channel_id=1, source_target_pairs={{0,8},{4,12},{8,24},{12,28},{24,16},{28,20},{16,0},{20,4},{1,9},{5... | collective-permute-start | bytes 1179656 | tf_op jit(solution)/shard_map/ppermute | solution.py:285
  36.1 13.5 %collective-permute-start.6 = (f32[64,1,2,768]{3,2,1,0:T(2,128)}, f32[64,1,2,768]{3,2,1,0:T(2,128)S(1)}, u32[]{:S(2)}, u32[]{:S(2)}) collective-permute-start(f32[64,1,2,768]{3,2,1,0:T(2,128)} %collective-permute-done.3.refs_0_), channel_id=1, source_target_pairs={{0,2},{2,0},{1,3},{3,1},{4,6},{6,4},{5,7},{7,5},{8,10},{10,8},{9,1... | collective-permute-start | bytes 1179656 | tf_op jit(solution)/shard_map/ppermute | solution.py:296
  36.6 35.0 %collective-permute-start.10 = (f32[1,2,96,512]{3,2,1,0:T(8,128)S(1)}, f32[1,2,96,512]{3,2,1,0:T(8,128)S(1)}, u32[]{:S(2)}, u32[]{:S(2)}) collective-permute-start(f32[1,2,96,512]{3,2,1,0:T(8,128)S(1)} %collective-permute-done.9.refs_7_.refs_17_), channel_id=1, source_target_pairs={{0,8},{4,12},{8,24},{12,28},{24,16},{28,20},{16,0},{20,4},{1,9},{5... | collective-permute-start | bytes 1179656 | tf_op jit(solution)/shard_map/ppermute | solution.py:285
  42.9 39.4 %collective-permute-start.14 = (f32[1,2,96,512]{3,2,1,0:T(8,128)S(1)}, f32[1,2,96,512]{3,2,1,0:T(8,128)S(1)}, u32[]{:S(2)}, u32[]{:S(2)}) collective-permute-start(f32[1,2,96,512]{3,2,1,0:T(8,128)S(1)} %constant_dynamic-slice_fusion.1.refs_6_.refs_16_), channel_id=1, source_target_pairs={{0,16},{4,20},{8,0},{12,4},{24,8},{28,12},{16,24},{20,28},{1,17},{... | collective-permute-start | bytes 1179656 | tf_op jit(solution)/shard_map/ppermute | solution.py:286
  47.5 38.4 %collective-permute-start.11 = (f32[1,2,96,512]{3,2,1,0:T(8,128)S(1)}, f32[1,2,96,512]{3,2,1,0:T(8,128)S(1)}, u32[]{:S(2)}, u32[]{:S(2)}) collective-permute-start(f32[1,2,96,512]{3,2,1,0:T(8,128)S(1)} %collective-permute-done.9.refs_7_.refs_17_), channel_id=1, source_target_pairs={{0,16},{4,20},{8,0},{12,4},{24,8},{28,12},{16,24},{20,28},{1,17},{... | collective-permute-start | bytes 1179656 | tf_op jit(solution)/shard_map/ppermute | solution.py:286
  49.1 36.8 %collective-permute-start.13 = (f32[1,2,96,512]{3,2,1,0:T(8,128)S(1)}, f32[1,2,96,512]{3,2,1,0:T(8,128)S(1)}, u32[]{:S(2)}, u32[]{:S(2)}) collective-permute-start(f32[1,2,96,512]{3,2,1,0:T(8,128)S(1)} %collective-permute-done.12.refs_8_.refs_18_), channel_id=1, source_target_pairs={{0,8},{4,12},{8,24},{12,28},{24,16},{28,20},{16,0},{20,4},{1,9},{5... | collective-permute-start | bytes 1179656 | tf_op jit(solution)/shard_map/ppermute | solution.py:287
  49.5 37.7 %collective-permute-start.8 = (f32[64,1,2,768]{3,2,1,0:T(2,128)}, f32[64,1,2,768]{3,2,1,0:T(2,128)S(1)}, u32[]{:S(2)}, u32[]{:S(2)}) collective-permute-start(f32[64,1,2,768]{3,2,1,0:T(2,128)} %collective-permute-done.4.refs_1_), channel_id=1, source_target_pairs={{0,2},{2,0},{1,3},{3,1},{4,6},{6,4},{5,7},{7,5},{8,10},{10,8},{9,1... | collective-permute-start | bytes 1179656 | tf_op jit(solution)/shard_map/ppermute | solution.py:297
  71.5 15.7 %collective-permute-start.7 = (f32[64,1,2,768]{3,2,1,0:T(2,128)S(1)}, f32[64,1,2,768]{3,2,1,0:T(2,128)S(1)}, u32[]{:S(2)}, u32[]{:S(2)}) collective-permute-start(f32[64,1,2,768]{3,2,1,0:T(2,128)S(1)} %slice.24), channel_id=1, source_target_pairs={{0,4},{4,0},{8,12},{12,8},{16,20},{20,16},{24,28},{28,24},{1,5},{5... | collective-permute-start | bytes 1179656 | tf_op jit(solution)/shard_map/ppermute | solution.py:295
  82.3 9.1 %collective-permute-start.17 = (f32[1,2,96,384]{3,2,1,0:T(8,128)S(1)}, f32[1,2,96,384]{3,2,1,0:T(8,128)S(1)}, u32[]{:S(2)}, u32[]{:S(2)}) collective-permute-start(f32[1,2,96,384]{3,2,1,0:T(8,128)S(1)} %slice.26), channel_id=1, source_target_pairs={{0,8},{4,12},{8,24},{12,28},{24,16},{28,20},{16,0},{20,4},{1,9},{5... | collective-permute-start | bytes 884744 | tf_op jit(solution)/shard_map/ppermute | solution.py:288
  92.2 10.5 %collective-permute-start.18 = (f32[2,192,384]{2,1,0:T(8,128)S(1)}, f32[2,192,384]{2,1,0:T(8,128)S(1)}, u32[]{:S(2)}, u32[]{:S(2)}) collective-permute-start(f32[2,192,384]{2,1,0:T(8,128)S(1)} %get-tuple-element.108), channel_id=1, source_target_pairs={{0,1},{1,0},{2,3},{3,2},{4,5},{5,4},{6,7},{7,6},{8,9},{9,8},{10,11... | collective-permute-start | bytes 1769480 | tf_op jit(solution)/shard_map/ppermute | solution.py:357
  92.3 6.1 %collective-permute-start.15 = (f32[1,2,96,128]{3,2,1,0:T(8,128)S(1)}, f32[1,2,96,128]{3,2,1,0:T(8,128)S(1)}, u32[]{:S(2)}, u32[]{:S(2)}) collective-permute-start(f32[1,2,96,128]{3,2,1,0:T(8,128)S(1)} %slice.25), channel_id=1, source_target_pairs={{0,8},{4,12},{8,24},{12,28},{24,16},{28,20},{16,0},{20,4},{1,9},{5... | collective-permute-start | bytes 294920 | tf_op jit(solution)/shard_map/ppermute | solution.py:289
  99.0 7.2 %collective-permute-start.16 = (f32[4,192,128]{2,1,0:T(8,128)S(1)}, f32[4,192,128]{2,1,0:T(8,128)S(1)}, u32[]{:S(2)}, u32[]{:S(2)}) collective-permute-start(f32[4,192,128]{2,1,0:T(8,128)S(1)} %shard_map.56.mine), channel_id=1, source_target_pairs={{0,1},{1,0},{2,3},{3,2},{4,5},{5,4},{6,7},{7,6},{8,9},{9,8},{10,11... | collective-permute-start | bytes 1179656 | tf_op jit(solution)/shard_map/ppermute | solution.py:359
  99.1 3.7 %collective-permute-start = (s32[3,8]{1,0:T(4,128)S(1)}, s32[3,8]{1,0:T(4,128)S(1)}, u32[]{:S(2)}, u32[]{:S(2)}) collective-permute-start(s32[3,8]{1,0:T(4,128)S(1)} %copy-done.3), channel_id=1, source_target_pairs={{0,4},{4,0},{8,12},{12,8},{16,20},{20,16},{24,28},{28,24},{1,5},{5... | collective-permute-start | bytes 296 | tf_op jit(solution)/shard_map/ppermute | solution.py:299
  103.4 16.2 %collective-permute-start.23 = (f32[192,384]{1,0:T(8,128)S(1)}, f32[192,384]{1,0:T(8,128)S(1)}, u32[]{:S(2)}, u32[]{:S(2)}) collective-permute-start(f32[192,384]{1,0:T(8,128)S(1)} %get-tuple-element.113), channel_id=1, source_target_pairs={{0,4},{4,0},{8,12},{12,8},{16,20},{20,16},{24,28},{28,24},{1,5},{5... | collective-permute-start | bytes 884744 | tf_op jit(solution)/shard_map/ppermute | solution.py:363
  106.9 12.7 %collective-permute-start.24 = (f32[192,128]{1,0:T(8,128)S(1)}, f32[192,128]{1,0:T(8,128)S(1)}, u32[]{:S(2)}, u32[]{:S(2)}) collective-permute-start(f32[192,128]{1,0:T(8,128)S(1)} %get-tuple-element.114), channel_id=1, source_target_pairs={{0,4},{4,0},{8,12},{12,8},{16,20},{20,16},{24,28},{28,24},{1,5},{5... | collective-permute-start | bytes 294920 | tf_op jit(solution)/shard_map/ppermute | solution.py:370
  107.5 4.0 %collective-permute-start.20 = (f32[1,512]{1,0:T(1,128)S(1)}, f32[1,512]{1,0:T(1,128)S(1)}, u32[]{:S(2)}, u32[]{:S(2)}) collective-permute-start(f32[1,512]{1,0:T(1,128)S(1)} %get-tuple-element.110), channel_id=1, source_target_pairs={{0,8},{4,12},{8,0},{12,4},{16,24},{20,28},{24,16},{28,20},{1,9},{5... | collective-permute-start | bytes 6152 | tf_op jit(solution)/shard_map/ppermute | solution.py:372
  111.5 4.5 %collective-permute-start.21 = (f32[1,512]{1,0:T(1,128)S(1)}, f32[1,512]{1,0:T(1,128)S(1)}, u32[]{:S(2)}, u32[]{:S(2)}) collective-permute-start(f32[1,512]{1,0:T(1,128)S(1)} %add.10), channel_id=1, source_target_pairs={{0,16},{4,20},{8,24},{12,28},{16,0},{20,4},{24,8},{28,12},{1,17},{... | collective-permute-start | bytes 6152 | tf_op jit(solution)/shard_map/ppermute | solution.py:372
  116.0 3.6 %collective-permute-start.22 = (f32[1,512]{1,0:T(1,128)S(1)}, f32[1,512]{1,0:T(1,128)S(1)}, u32[]{:S(2)}, u32[]{:S(2)}) collective-permute-start(f32[1,512]{1,0:T(1,128)S(1)} %add.11.sums), channel_id=1, source_target_pairs={{0,4},{4,0},{8,12},{12,8},{16,20},{20,16},{24,28},{28,24},{1,5},{5... | collective-permute-start | bytes 6152 | tf_op jit(solution)/shard_map/ppermute | solution.py:373
  (5 other events, 83.6 us)

commit v2 on v1

--- a/solution.py
+++ b/solution.py
@@ -133,20 +133,19 @@
     return jnp.concatenate([ref[...] for ref in refs], axis=0)
 
 
-def group_kernel(sets, sizes, *refs):
-    lefts = refs[: 2 * sets * len(sizes)]
-    rest = refs[len(lefts) :]
-    shards, (*near, out, b_high, b_low) = rest[: sum(sizes)], rest[sum(sizes) :]
-    put_shards(shards, b_high, b_low)
-    total = near[0][...] if near else None
-    first = 0
-    for i in range(len(sizes)):
+def split_kernel(*refs):
+    *shards, high, low = refs
+    put_shards(shards, high, low)
+
+
+def group_kernel(sets, groups, *refs):
+    lefts, rights, out = refs[: 2 * sets * groups], refs[2 * sets * groups : -1], refs[-1]
+    total = None
+    for i in range(groups):
         group = lefts[2 * sets * i : 2 * sets * (i + 1)]
-        high, low = stacked(group[:sets]), stacked(group[sets:])
-        part = pl.ds(first, high.shape[1])
-        value = product3(high, low, b_high[part, :], b_low[part, :])
+        right = rights[2 * i : 2 * i + 2]
+        value = product3(stacked(group[:sets]), stacked(group[sets:]), right[0][...], right[1][...])
         total = value if total is None else total + value
-        first += high.shape[1]
     out[...] = total
 
 
@@ -320,26 +319,29 @@
     def picked(sets, g):
         return [s[2 * g] for s in sets] + [s[2 * g + 1] for s in sets]
 
-    def product(sets, which, *near):
-        lefts = [part for g in which for part in picked(sets, g)]
-        members = [shards[m] for g in which for m in groups[g]]
+    rights = []
+    for g in range(2):
+        members = [shards[m] for m in groups[g]]
+        rights += call(
+            split_kernel, [shape((len(members) * shard_depth, half), bf16)] * 2, [VMEM] * len(members)
+        )(*members)
+
+    def product(sets):
+        lefts = [part for g in range(2) for part in picked(sets, g)]
         count = sum(s[0].shape[0] for s in sets)
-        factor = pltpu.VMEM((len(members) * shard_depth, half), bf16)
         (total,) = call(
-            functools.partial(group_kernel, len(sets), tuple(len(groups[g]) for g in which)),
+            functools.partial(group_kernel, len(sets), 2),
             [shape((count, half), f32)],
-            [VMEM] * (len(lefts) + len(members) + len(near)),
-            [factor, factor],
-            6 * count * half * len(members) * shard_depth,
-        )(*lefts, *members, *near)
+            [VMEM] * (len(lefts) + len(rights)),
+            flops=6 * count * half * 7 * shard_depth,
+        )(*lefts, *rights)
         return total
 
-    near = product(early_sets, [1], product(early_sets, [0]))
+    early_sets += [left((y2, 1, False, 2 * UNIT)), left((d0, 1, True, 0))]
+    near = product(early_sets)
     d2, d1, near = together(d2, d1, near)
-    late_sets = [
-        left((y2, 1, False, 2 * UNIT)), left((d0, 1, True, 0)), left((d1, 1, True, UNIT)), left((d2, 1, True, 2 * UNIT))
-    ]
-    near_late = product(late_sets, [0, 1])
+    late_sets = [left((d1, 1, True, UNIT)), left((d2, 1, True, 2 * UNIT))]
+    near_late = product(late_sets)
 
     far_lefts = picked([*early_sets, *late_sets], 2)
 

time: 121 us -> 93.4 us (0.77)
  waiting for transfers between devices: 63 us -> 50.4 us
  starting transfers between devices: 34.1 us -> 21.7 us
  local copies, waits for them, and re-layouts: 2.43 us -> 0.57 us
    ppermute x1, waiting for transfers between devices: 23.5 us -> 5.61 us  [local(): a_tables = [a_pattern, lax.ppermute(a_pattern, 'row', swap_y)]]
    ppermute x2, waiting for transfers between devices: 23.4 us -> 11.2 us  [local(): shards[-1, turn] = lax.ppermute(shards[0, turn], 'row', line_pairs(1))]
    ppermute x3, waiting for transfers between devices: 3.7 us -> 10.3 us  [local(): lax.ppermute(a_panels[u * UNIT:(u + 1) * UNIT], 'row', swap_y)]
    ppermute x2, starting transfers between devices: 4.17 us -> 0.72 us  [local(): shards[-1, turn] = lax.ppermute(shards[0, turn], 'row', line_pairs(1))]
    ppermute x2, starting transfers between devices: 4.07 us -> 0.98 us  [local(): lax.ppermute(sums, 'row', [(r, r ^ bit) for r in range(n_row)])]
    ppermute x1, waiting for transfers between devices: 2.71 us -> 5.35 us  [local(): far_last = lax.ppermute(shards[-1, 1][..., cut:], 'row', line_pairs(1))]
    ppermute x1, starting transfers between devices: 3.43 us -> 0.8 us  [local(): far_last = lax.ppermute(shards[-1, 1][..., cut:], 'row', line_pairs(1))]
    ppermute x2, waiting for transfers between devices: 4.46 us -> 7.09 us  [local(): lax.ppermute(sums, 'row', [(r, r ^ bit) for r in range(n_row)])]
  transfers between devices with their start and end apart: 25 -> 25, of which waited for: 10 -> 13; matrix products, arithmetic and copies ran while one was open for 2% -> 1% of each run, Pallas kernels for 16% -> 20%
where the time goes in v2:
time: 93.4 us; the launch traced here: 93.3 us
  waiting for transfers between devices  50.4 us (54%)
  starting transfers between devices  21.7 us (23%)
  Pallas kernels  20.4 us (22%)
    pallas_call x16, Pallas kernels, run(): pl.pallas_call(kernel, out_shape=out_shapes, in_specs=specs, out_specs=[V...  20.4 us
    ppermute x2, waiting for transfers between devices, local(): shards[-1, turn] = lax.ppermute(shards[0, turn], 'row', line_pairs(1))  11.2 us
    ppermute x3, waiting for transfers between devices, local(): lax.ppermute(a_panels[u * UNIT:(u + 1) * UNIT], 'row', swap_y)  10.3 us
    ppermute x2, waiting for transfers between devices, local(): lax.ppermute(sums, 'row', [(r, r ^ bit) for r in range(n_row)])  7.09 us
    ppermute x1, waiting for transfers between devices, local(): a_tables = [a_pattern, lax.ppermute(a_pattern, 'row', swap_y)]  5.61 us
    ppermute x1, waiting for transfers between devices, local(): far_last = lax.ppermute(shards[-1, 1][..., cut:], 'row', line_pairs(1))  5.35 us
    ppermute x2, starting transfers between devices, local(): shards[1, turn] = lax.ppermute(shards[0, turn], 'row', line_pairs(-1))  5.18 us
    ppermute x1, waiting for transfers between devices, local(): c_tables = [c_pattern, lax.ppermute(c_pattern, 'row', swap_y)]  3.24 us
  transfers between devices with their start and end apart: 25, of which 13 were waited for; matrix products, arithmetic and copies ran while one was open for 1% of the time, Pallas kernels for 20%

profile of v2, /device:TPU:0, one launch (start us, length us, event | category | flops | bytes accessed | tf_op | source)
XLA Modules:
  0.0 93.3 jit_solution(4943972473404381929)
XLA Ops:
  0.0 3.0 %collective-permute-start.1 = (f32[192,1,2,768]{3,2,1,0:T(2,128)}, f32[192,1,2,768]{3,2,1,0:T(2,128)S(1)}, u32[]{:S(2)}, u32[]{:S(2)}) collective-permute-start(f32[192,1,2,768]{3,2,1,0:T(2,128)} %refs_0_.1), channel_id=1, source_target_pairs={{0,2},{2,0},{1,3},{3,1},{4,6},{6,4},{5,7},{7,5},{8,10},{10,8},{9,1... | collective-permute-start | bytes 3538952 | tf_op jit(solution)/shard_map/ppermute | solution.py:290
  3.1 1.6 %collective-permute-start.9 = (f32[1,2,96,512]{3,2,1,0:T(8,128)S(1)}, f32[1,2,96,512]{3,2,1,0:T(8,128)S(1)}, u32[]{:S(2)}, u32[]{:S(2)}) collective-permute-start(f32[1,2,96,512]{3,2,1,0:T(8,128)S(1)} %constant_dynamic-slice_fusion), channel_id=1, source_target_pairs={{0,4},{4,0},{8,12},{12,8},{16,20},{20,16},{24,28},{28,24},{1,5},{5... | collective-permute-start | bytes 1179656 | tf_op jit(solution)/shard_map/ppermute | solution.py:282
  4.7 2.6 %collective-permute-start.11 = (f32[1,2,96,512]{3,2,1,0:T(8,128)S(1)}, f32[1,2,96,512]{3,2,1,0:T(8,128)S(1)}, u32[]{:S(2)}, u32[]{:S(2)}) collective-permute-start(f32[1,2,96,512]{3,2,1,0:T(8,128)S(1)} %constant_dynamic-slice_fusion.1.refs_0_), channel_id=1, source_target_pairs={{0,16},{4,20},{8,0},{12,4},{24,8},{28,12},{16,24},{20,28},{1,17},{... | collective-permute-start | bytes 1179656 | tf_op jit(solution)/shard_map/ppermute | solution.py:285
  8.2 5.6 %collective-permute-done.2.other_pattern = s32[3,1,2,6]{3,2,1,0:T(2,128)S(1)} collective-permute-done((s32[3,1,2,6]{3,2,1,0:T(2,128)S(1)}, s32[3,1,2,6]{3,2,1,0:T(2,128)S(1)}, u32[]{:S(2)}, u32[]{:S(2)}) %collective-permute-start.2) | collective-permute-done | bytes 176 | tf_op jit(solution)/shard_map/ppermute | solution.py:297
  13.8 1.5 %collective-permute-start.3 = (f32[64,1,2,768]{3,2,1,0:T(2,128)S(1)}, f32[64,1,2,768]{3,2,1,0:T(2,128)S(1)}, u32[]{:S(2)}, u32[]{:S(2)}) collective-permute-start(f32[64,1,2,768]{3,2,1,0:T(2,128)S(1)} %get-tuple-element.124), channel_id=1, source_target_pairs={{0,4},{4,0},{8,12},{12,8},{16,20},{20,16},{24,28},{28,24},{1,5},{5... | collective-permute-start | bytes 1179656 | tf_op jit(solution)/shard_map/ppermute | solution.py:292
  17.4 8.0 %collective-permute-done.10.refs_2_ = f32[1,2,96,512]{3,2,1,0:T(8,128)S(1)} collective-permute-done((f32[1,2,96,512]{3,2,1,0:T(8,128)S(1)}, f32[1,2,96,512]{3,2,1,0:T(8,128)S(1)}, u32[]{:S(2)}, u32[]{:S(2)}) %collective-permute-start.10) | collective-permute-done | bytes 393248 | tf_op jit(solution)/shard_map/ppermute | solution.py:284
  26.1 1.4 %collective-permute-start.6 = (f32[64,1,2,768]{3,2,1,0:T(2,128)S(1)}, f32[64,1,2,768]{3,2,1,0:T(2,128)S(1)}, u32[]{:S(2)}, u32[]{:S(2)}) collective-permute-start(f32[64,1,2,768]{3,2,1,0:T(2,128)S(1)} %collective-permute-done.3.refs_0_), channel_id=1, source_target_pairs={{0,2},{2,0},{1,3},{3,1},{4,6},{6,4},{5,7},{7,5},{8,10},{10,8},{9,1... | collective-permute-start | bytes 1179656 | tf_op jit(solution)/shard_map/ppermute | solution.py:295
  27.4 6.8 %collective-permute-done.5.refs_0_ = f32[64,1,2,768]{3,2,1,0:T(2,128)S(1)} collective-permute-done((f32[64,1,2,768]{3,2,1,0:T(2,128)S(1)}, f32[64,1,2,768]{3,2,1,0:T(2,128)S(1)}, u32[]{:S(2)}, u32[]{:S(2)}) %collective-permute-start.5) | collective-permute-done | bytes 393248 | tf_op jit(solution)/shard_map/ppermute | solution.py:292
  34.2 2.6 %collective-permute-start.13 = (f32[1,2,96,512]{3,2,1,0:T(8,128)S(1)}, f32[1,2,96,512]{3,2,1,0:T(8,128)S(1)}, u32[]{:S(2)}, u32[]{:S(2)}) collective-permute-start(f32[1,2,96,512]{3,2,1,0:T(8,128)S(1)} %collective-permute-done.9.refs_1_), channel_id=1, source_target_pairs={{0,16},{4,20},{8,0},{12,4},{24,8},{28,12},{16,24},{20,28},{1,17},{... | collective-permute-start | bytes 1179656 | tf_op jit(solution)/shard_map/ppermute | solution.py:285
  36.9 3.5 %collective-permute-done.4.refs_1_ = f32[64,1,2,768]{3,2,1,0:T(2,128)S(1)} collective-permute-done((f32[64,1,2,768]{3,2,1,0:T(2,128)S(1)}, f32[64,1,2,768]{3,2,1,0:T(2,128)S(1)}, u32[]{:S(2)}, u32[]{:S(2)}) %collective-permute-start.4) | collective-permute-done | bytes 393248 | tf_op jit(solution)/shard_map/ppermute | solution.py:292
  40.4 1.6 %collective-permute-start.8 = (f32[64,1,2,768]{3,2,1,0:T(2,128)S(1)}, f32[64,1,2,768]{3,2,1,0:T(2,128)S(1)}, u32[]{:S(2)}, u32[]{:S(2)}) collective-permute-start(f32[64,1,2,768]{3,2,1,0:T(2,128)S(1)} %collective-permute-done.4.refs_1_), channel_id=1, source_target_pairs={{0,2},{2,0},{1,3},{3,1},{4,6},{6,4},{5,7},{7,5},{8,10},{10,8},{9,1... | collective-permute-start | bytes 1179656 | tf_op jit(solution)/shard_map/ppermute | solution.py:296
  42.0 3.2 %collective-permute-done.12.refs_0_ = f32[1,2,96,512]{3,2,1,0:T(8,128)S(1)} collective-permute-done((f32[1,2,96,512]{3,2,1,0:T(8,128)S(1)}, f32[1,2,96,512]{3,2,1,0:T(8,128)S(1)}, u32[]{:S(2)}, u32[]{:S(2)}) %collective-permute-start.12) | collective-permute-done | bytes 393248 | tf_op jit(solution)/shard_map/ppermute | solution.py:284
  45.2 2.5 %shard_map.46 = (bf16[192,768]{1,0:T(8,128)(2,1)S(1)}, bf16[192,768]{1,0:T(8,128)(2,1)S(1)}, bf16[192,576]{1,0:T(8,128)(2,1)S(1)}, bf16[192,576]{1,0:T(8,128)(2,...) custom-call(s32[3,1,2,6]{3,2,1,0:T(2,128)S(1)} %copy-done.2, s32[3,1,2,6]{3,2,1,0:T(2,128)S(1)} %copy-done.2, ...), custom_call_target="tpu_custom_call" | custom-call | bytes 2359584 | tf_op jit(solution)/shard_map/pallas_call | solution.py:244
  48.0 1.9 %shard_map.48 = (bf16[128,768]{1,0:T(8,128)(2,1)S(1)}, bf16[128,768]{1,0:T(8,128)(2,1)S(1)}, bf16[128,576]{1,0:T(8,128)(2,1)S(1)}, bf16[128,576]{1,0:T(8,128)(2,...) custom-call(s32[3,1,2,6]{3,2,1,0:T(2,128)S(1)} %copy-done.2, ...), custom_call_target="tpu_custom_call" | custom-call | bytes 1573152 | tf_op jit(solution)/shard_map/pallas_call | solution.py:244
  50.0 1.3 %shard_map.49 = (bf16[64,768]{1,0:T(8,128)(2,1)S(1)}, bf16[64,768]{1,0:T(8,128)(2,1)S(1)}, bf16[64,576]{1,0:T(8,128)(2,1)S(1)}, bf16[64,576]{1,0:T(8,128)(2,1)S(...) custom-call(s32[3,1,2,6]{3,2,1,0:T(2,128)S(1)} %copy-done.2, ...), custom_call_target="tpu_custom_call" | custom-call | bytes 786720 | tf_op jit(solution)/shard_map/pallas_call | solution.py:244
  52.9 2.2 %collective-permute-done.14.refs_2_ = f32[1,2,96,512]{3,2,1,0:T(8,128)S(1)} collective-permute-done((f32[1,2,96,512]{3,2,1,0:T(8,128)S(1)}, f32[1,2,96,512]{3,2,1,0:T(8,128)S(1)}, u32[]{:S(2)}, u32[]{:S(2)}) %collective-permute-start.14) | collective-permute-done | bytes 393248 | tf_op jit(solution)/shard_map/ppermute | solution.py:286
  55.3 2.5 %shard_map.47 = (bf16[192,768]{1,0:T(8,128)(2,1)S(1)}, bf16[192,768]{1,0:T(8,128)(2,1)S(1)}, bf16[192,576]{1,0:T(8,128)(2,1)S(1)}, bf16[192,576]{1,0:T(8,128)(2,...) custom-call(s32[3,1,2,6]{3,2,1,0:T(2,128)S(1)} %copy-done.2, s32[3,1,2,6]{3,2,1,0:T(2,128)S(1)} %copy-done.2, ...), custom_call_target="tpu_custom_call" | custom-call | bytes 2359584 | tf_op jit(solution)/shard_map/pallas_call | solution.py:244
  57.8 3.2 %shard_map.53.refs_14_ = f32[640,512]{1,0:T(8,128)S(1)} custom-call(bf16[192,768]{1,0:T(8,128)(2,1)S(1)} %get-tuple-element.69.refs_0_, bf16[192,768]{1,0:T(8,128)(2,1)S(1)} %get-tuple-element.70.refs_1_, bf16[128,768]{1,0:T(8,128)(2,1)S(1)} %get-tuple-element.71.refs_2_, bf16[64,768]{1,0:T(8,128)(2,1)S(1)} %get-tuple-element.72.refs_3_, ...), custom_call_target="tpu_custom_call" | custom-call | flops 2642411520 | bytes 7503872 | tf_op jit(solution)/shard_map/pallas_call | solution.py:244
  66.3 5.3 %collective-permute-done.15.refs_16_ = f32[1,2,96,128]{3,2,1,0:T(8,128)S(1)} collective-permute-done((f32[1,2,96,128]{3,2,1,0:T(8,128)S(1)}, f32[1,2,96,128]{3,2,1,0:T(8,128)S(1)}, u32[]{:S(2)}, u32[]{:S(2)}) %collective-permute-start.15) | collective-permute-done | bytes 98336 | tf_op jit(solution)/shard_map/ppermute | solution.py:288
  72.6 3.2 %collective-permute-done.other_pattern = s32[3,8]{1,0:T(4,128)S(1)} collective-permute-done((s32[3,8]{1,0:T(4,128)S(1)}, s32[3,8]{1,0:T(4,128)S(1)}, u32[]{:S(2)}, u32[]{:S(2)}) %collective-permute-start) | collective-permute-done | bytes 128 | tf_op jit(solution)/shard_map/ppermute | solution.py:298
  78.9 1.7 %collective-permute-start.24 = (f32[192,128]{1,0:T(8,128)S(1)}, f32[192,128]{1,0:T(8,128)S(1)}, u32[]{:S(2)}, u32[]{:S(2)}) collective-permute-start(f32[192,128]{1,0:T(8,128)S(1)} %get-tuple-element.122), channel_id=1, source_target_pairs={{0,4},{4,0},{8,12},{12,8},{16,20},{20,16},{24,28},{28,24},{1,5},{5... | collective-permute-start | bytes 294920 | tf_op jit(solution)/shard_map/ppermute | solution.py:372
  80.6 3.6 %collective-permute-done.20 = f32[1,512]{1,0:T(1,128)S(1)} collective-permute-done((f32[1,512]{1,0:T(1,128)S(1)}, f32[1,512]{1,0:T(1,128)S(1)}, u32[]{:S(2)}, u32[]{:S(2)}) %collective-permute-start.20) | collective-permute-done | bytes 2080 | tf_op jit(solution)/shard_map/ppermute | solution.py:374
  85.2 3.5 %collective-permute-done.21 = f32[1,512]{1,0:T(1,128)S(1)} collective-permute-done((f32[1,512]{1,0:T(1,128)S(1)}, f32[1,512]{1,0:T(1,128)S(1)}, u32[]{:S(2)}, u32[]{:S(2)}) %collective-permute-start.21) | collective-permute-done | bytes 2080 | tf_op jit(solution)/shard_map/ppermute | solution.py:374
  89.0 3.2 %collective-permute-done.22.other_sums = f32[1,512]{1,0:T(1,128)S(1)} collective-permute-done((f32[1,512]{1,0:T(1,128)S(1)}, f32[1,512]{1,0:T(1,128)S(1)}, u32[]{:S(2)}, u32[]{:S(2)}) %collective-permute-start.22) | collective-permute-done | bytes 2080 | tf_op jit(solution)/shard_map/ppermute | solution.py:375
  (59 shorter events, 17.2 us)
Async XLA Ops:
  0.0 36.8 %collective-permute-start.1 = (f32[192,1,2,768]{3,2,1,0:T(2,128)}, f32[192,1,2,768]{3,2,1,0:T(2,128)S(1)}, u32[]{:S(2)}, u32[]{:S(2)}) collective-permute-start(f32[192,1,2,768]{3,2,1,0:T(2,128)} %refs_0_.1), channel_id=1, source_target_pairs={{0,2},{2,0},{1,3},{3,1},{4,6},{6,4},{5,7},{7,5},{8,10},{10,8},{9,1... | collective-permute-start | bytes 3538952 | tf_op jit(solution)/shard_map/ppermute | solution.py:290
  3.1 12.2 %collective-permute-start.9 = (f32[1,2,96,512]{3,2,1,0:T(8,128)S(1)}, f32[1,2,96,512]{3,2,1,0:T(8,128)S(1)}, u32[]{:S(2)}, u32[]{:S(2)}) collective-permute-start(f32[1,2,96,512]{3,2,1,0:T(8,128)S(1)} %constant_dynamic-slice_fusion), channel_id=1, source_target_pairs={{0,4},{4,0},{8,12},{12,8},{16,20},{20,16},{24,28},{28,24},{1,5},{5... | collective-permute-start | bytes 1179656 | tf_op jit(solution)/shard_map/ppermute | solution.py:282
  4.7 12.1 %collective-permute-start.11 = (f32[1,2,96,512]{3,2,1,0:T(8,128)S(1)}, f32[1,2,96,512]{3,2,1,0:T(8,128)S(1)}, u32[]{:S(2)}, u32[]{:S(2)}) collective-permute-start(f32[1,2,96,512]{3,2,1,0:T(8,128)S(1)} %constant_dynamic-slice_fusion.1.refs_0_), channel_id=1, source_target_pairs={{0,16},{4,20},{8,0},{12,4},{24,8},{28,12},{16,24},{20,28},{1,17},{... | collective-permute-start | bytes 1179656 | tf_op jit(solution)/shard_map/ppermute | solution.py:285
  7.3 18.0 %collective-permute-start.10 = (f32[1,2,96,512]{3,2,1,0:T(8,128)S(1)}, f32[1,2,96,512]{3,2,1,0:T(8,128)S(1)}, u32[]{:S(2)}, u32[]{:S(2)}) collective-permute-start(f32[1,2,96,512]{3,2,1,0:T(8,128)S(1)} %constant_dynamic-slice_fusion.1.refs_0_), channel_id=1, source_target_pairs={{0,8},{4,12},{8,24},{12,28},{24,16},{28,20},{16,0},{20,4},{1,9},{5... | collective-permute-start | bytes 1179656 | tf_op jit(solution)/shard_map/ppermute | solution.py:284
  7.3 6.5 %collective-permute-start.2 = (s32[3,1,2,6]{3,2,1,0:T(2,128)S(1)}, s32[3,1,2,6]{3,2,1,0:T(2,128)S(1)}, u32[]{:S(2)}, u32[]{:S(2)}) collective-permute-start(s32[3,1,2,6]{3,2,1,0:T(2,128)S(1)} %copy-done.2), channel_id=1, source_target_pairs={{0,4},{4,0},{8,12},{12,8},{16,20},{20,16},{24,28},{28,24},{1,5},{5... | collective-permute-start | bytes 440 | tf_op jit(solution)/shard_map/ppermute | solution.py:297
  13.8 12.2 %collective-permute-start.3 = (f32[64,1,2,768]{3,2,1,0:T(2,128)S(1)}, f32[64,1,2,768]{3,2,1,0:T(2,128)S(1)}, u32[]{:S(2)}, u32[]{:S(2)}) collective-permute-start(f32[64,1,2,768]{3,2,1,0:T(2,128)S(1)} %get-tuple-element.124), channel_id=1, source_target_pairs={{0,4},{4,0},{8,12},{12,8},{16,20},{20,16},{24,28},{28,24},{1,5},{5... | collective-permute-start | bytes 1179656 | tf_op jit(solution)/shard_map/ppermute | solution.py:292
  15.4 18.9 %collective-permute-start.5 = (f32[64,1,2,768]{3,2,1,0:T(2,128)S(1)}, f32[64,1,2,768]{3,2,1,0:T(2,128)S(1)}, u32[]{:S(2)}, u32[]{:S(2)}) collective-permute-start(f32[64,1,2,768]{3,2,1,0:T(2,128)S(1)} %get-tuple-element.123), channel_id=1, source_target_pairs={{0,4},{4,0},{8,12},{12,8},{16,20},{20,16},{24,28},{28,24},{1,5},{5... | collective-permute-start | bytes 1179656 | tf_op jit(solution)/shard_map/ppermute | solution.py:292
  16.8 23.6 %collective-permute-start.4 = (f32[64,1,2,768]{3,2,1,0:T(2,128)S(1)}, f32[64,1,2,768]{3,2,1,0:T(2,128)S(1)}, u32[]{:S(2)}, u32[]{:S(2)}) collective-permute-start(f32[64,1,2,768]{3,2,1,0:T(2,128)S(1)} %get-tuple-element.125), channel_id=1, source_target_pairs={{0,4},{4,0},{8,12},{12,8},{16,20},{20,16},{24,28},{28,24},{1,5},{5... | collective-permute-start | bytes 1179656 | tf_op jit(solution)/shard_map/ppermute | solution.py:292
  25.3 19.9 %collective-permute-start.12 = (f32[1,2,96,512]{3,2,1,0:T(8,128)S(1)}, f32[1,2,96,512]{3,2,1,0:T(8,128)S(1)}, u32[]{:S(2)}, u32[]{:S(2)}) collective-permute-start(f32[1,2,96,512]{3,2,1,0:T(8,128)S(1)} %collective-permute-done.9.refs_1_), channel_id=1, source_target_pairs={{0,8},{4,12},{8,24},{12,28},{24,16},{28,20},{16,0},{20,4},{1,9},{5... | collective-permute-start | bytes 1179656 | tf_op jit(solution)/shard_map/ppermute | solution.py:284
  26.1 25.3 %collective-permute-start.6 = (f32[64,1,2,768]{3,2,1,0:T(2,128)S(1)}, f32[64,1,2,768]{3,2,1,0:T(2,128)S(1)}, u32[]{:S(2)}, u32[]{:S(2)}) collective-permute-start(f32[64,1,2,768]{3,2,1,0:T(2,128)S(1)} %collective-permute-done.3.refs_0_), channel_id=1, source_target_pairs={{0,2},{2,0},{1,3},{3,1},{4,6},{6,4},{5,7},{7,5},{8,10},{10,8},{9,1... | collective-permute-start | bytes 1179656 | tf_op jit(solution)/shard_map/ppermute | solution.py:295
  34.2 18.7 %collective-permute-start.13 = (f32[1,2,96,512]{3,2,1,0:T(8,128)S(1)}, f32[1,2,96,512]{3,2,1,0:T(8,128)S(1)}, u32[]{:S(2)}, u32[]{:S(2)}) collective-permute-start(f32[1,2,96,512]{3,2,1,0:T(8,128)S(1)} %collective-permute-done.9.refs_1_), channel_id=1, source_target_pairs={{0,16},{4,20},{8,0},{12,4},{24,8},{28,12},{16,24},{20,28},{1,17},{... | collective-permute-start | bytes 1179656 | tf_op jit(solution)/shard_map/ppermute | solution.py:285
  36.8 18.3 %collective-permute-start.14 = (f32[1,2,96,512]{3,2,1,0:T(8,128)S(1)}, f32[1,2,96,512]{3,2,1,0:T(8,128)S(1)}, u32[]{:S(2)}, u32[]{:S(2)}) collective-permute-start(f32[1,2,96,512]{3,2,1,0:T(8,128)S(1)} %collective-permute-done.10.refs_2_), channel_id=1, source_target_pairs={{0,8},{4,12},{8,24},{12,28},{24,16},{28,20},{16,0},{20,4},{1,9},{5... | collective-permute-start | bytes 1179656 | tf_op jit(solution)/shard_map/ppermute | solution.py:286
  40.4 20.6 %collective-permute-start.8 = (f32[64,1,2,768]{3,2,1,0:T(2,128)S(1)}, f32[64,1,2,768]{3,2,1,0:T(2,128)S(1)}, u32[]{:S(2)}, u32[]{:S(2)}) collective-permute-start(f32[64,1,2,768]{3,2,1,0:T(2,128)S(1)} %collective-permute-done.4.refs_1_), channel_id=1, source_target_pairs={{0,2},{2,0},{1,3},{3,1},{4,6},{6,4},{5,7},{7,5},{8,10},{10,8},{9,1... | collective-permute-start | bytes 1179656 | tf_op jit(solution)/shard_map/ppermute | solution.py:296
  45.2 15.8 %collective-permute-start.7 = (f32[64,1,2,768]{3,2,1,0:T(2,128)S(1)}, f32[64,1,2,768]{3,2,1,0:T(2,128)S(1)}, u32[]{:S(2)}, u32[]{:S(2)}) collective-permute-start(f32[64,1,2,768]{3,2,1,0:T(2,128)S(1)} %slice.24), channel_id=1, source_target_pairs={{0,4},{4,0},{8,12},{12,8},{16,20},{20,16},{24,28},{28,24},{1,5},{5... | collective-permute-start | bytes 1179656 | tf_op jit(solution)/shard_map/ppermute | solution.py:294
  51.3 13.2 %collective-permute-start.17 = (f32[1,2,96,384]{3,2,1,0:T(8,128)S(1)}, f32[1,2,96,384]{3,2,1,0:T(8,128)S(1)}, u32[]{:S(2)}, u32[]{:S(2)}) collective-permute-start(f32[1,2,96,384]{3,2,1,0:T(8,128)S(1)} %slice.26), channel_id=1, source_target_pairs={{0,8},{4,12},{8,24},{12,28},{24,16},{28,20},{16,0},{20,4},{1,9},{5... | collective-permute-start | bytes 884744 | tf_op jit(solution)/shard_map/ppermute | solution.py:287
  65.4 10.5 %collective-permute-start.18 = (f32[2,192,384]{2,1,0:T(8,128)S(1)}, f32[2,192,384]{2,1,0:T(8,128)S(1)}, u32[]{:S(2)}, u32[]{:S(2)}) collective-permute-start(f32[2,192,384]{2,1,0:T(8,128)S(1)} %get-tuple-element.116), channel_id=1, source_target_pairs={{0,1},{1,0},{2,3},{3,2},{4,5},{5,4},{6,7},{7,6},{8,9},{9,8},{10,11... | collective-permute-start | bytes 1769480 | tf_op jit(solution)/shard_map/ppermute | solution.py:359
  65.5 6.1 %collective-permute-start.15 = (f32[1,2,96,128]{3,2,1,0:T(8,128)S(1)}, f32[1,2,96,128]{3,2,1,0:T(8,128)S(1)}, u32[]{:S(2)}, u32[]{:S(2)}) collective-permute-start(f32[1,2,96,128]{3,2,1,0:T(8,128)S(1)} %slice.25), channel_id=1, source_target_pairs={{0,8},{4,12},{8,24},{12,28},{24,16},{28,20},{16,0},{20,4},{1,9},{5... | collective-permute-start | bytes 294920 | tf_op jit(solution)/shard_map/ppermute | solution.py:288
  72.1 6.0 %collective-permute-start.16 = (f32[4,192,128]{2,1,0:T(8,128)S(1)}, f32[4,192,128]{2,1,0:T(8,128)S(1)}, u32[]{:S(2)}, u32[]{:S(2)}) collective-permute-start(f32[4,192,128]{2,1,0:T(8,128)S(1)} %shard_map.57.mine), channel_id=1, source_target_pairs={{0,1},{1,0},{2,3},{3,2},{4,5},{5,4},{6,7},{7,6},{8,9},{9,8},{10,11... | collective-permute-start | bytes 1179656 | tf_op jit(solution)/shard_map/ppermute | solution.py:361
  72.2 3.7 %collective-permute-start = (s32[3,8]{1,0:T(4,128)S(1)}, s32[3,8]{1,0:T(4,128)S(1)}, u32[]{:S(2)}, u32[]{:S(2)}) collective-permute-start(s32[3,8]{1,0:T(4,128)S(1)} %copy-done.3), channel_id=1, source_target_pairs={{0,4},{4,0},{8,12},{12,8},{16,20},{20,16},{24,28},{28,24},{1,5},{5... | collective-permute-start | bytes 296 | tf_op jit(solution)/shard_map/ppermute | solution.py:298
  76.6 15.7 %collective-permute-start.23 = (f32[192,384]{1,0:T(8,128)S(1)}, f32[192,384]{1,0:T(8,128)S(1)}, u32[]{:S(2)}, u32[]{:S(2)}) collective-permute-start(f32[192,384]{1,0:T(8,128)S(1)} %get-tuple-element.121), channel_id=1, source_target_pairs={{0,4},{4,0},{8,12},{12,8},{16,20},{20,16},{24,28},{28,24},{1,5},{5... | collective-permute-start | bytes 884744 | tf_op jit(solution)/shard_map/ppermute | solution.py:365
  78.9 13.4 %collective-permute-start.24 = (f32[192,128]{1,0:T(8,128)S(1)}, f32[192,128]{1,0:T(8,128)S(1)}, u32[]{:S(2)}, u32[]{:S(2)}) collective-permute-start(f32[192,128]{1,0:T(8,128)S(1)} %get-tuple-element.122), channel_id=1, source_target_pairs={{0,4},{4,0},{8,12},{12,8},{16,20},{20,16},{24,28},{28,24},{1,5},{5... | collective-permute-start | bytes 294920 | tf_op jit(solution)/shard_map/ppermute | solution.py:372
  80.6 3.6 %collective-permute-start.20 = (f32[1,512]{1,0:T(1,128)S(1)}, f32[1,512]{1,0:T(1,128)S(1)}, u32[]{:S(2)}, u32[]{:S(2)}) collective-permute-start(f32[1,512]{1,0:T(1,128)S(1)} %get-tuple-element.118), channel_id=1, source_target_pairs={{0,8},{4,12},{8,0},{12,4},{16,24},{20,28},{24,16},{28,20},{1,9},{5... | collective-permute-start | bytes 6152 | tf_op jit(solution)/shard_map/ppermute | solution.py:374
  84.2 4.5 %collective-permute-start.21 = (f32[1,512]{1,0:T(1,128)S(1)}, f32[1,512]{1,0:T(1,128)S(1)}, u32[]{:S(2)}, u32[]{:S(2)}) collective-permute-start(f32[1,512]{1,0:T(1,128)S(1)} %add.10), channel_id=1, source_target_pairs={{0,16},{4,20},{8,24},{12,28},{16,0},{20,4},{24,8},{28,12},{1,17},{... | collective-permute-start | bytes 6152 | tf_op jit(solution)/shard_map/ppermute | solution.py:374
  88.7 3.6 %collective-permute-start.22 = (f32[1,512]{1,0:T(1,128)S(1)}, f32[1,512]{1,0:T(1,128)S(1)}, u32[]{:S(2)}, u32[]{:S(2)}) collective-permute-start(f32[1,512]{1,0:T(1,128)S(1)} %add.11.sums), channel_id=1, source_target_pairs={{0,4},{4,0},{8,12},{12,8},{16,20},{20,16},{24,28},{28,24},{1,5},{5... | collective-permute-start | bytes 6152 | tf_op jit(solution)/shard_map/ppermute | solution.py:375
  (5 other events, 26.0 us)

commit v3 on v2

--- a/solution.py
+++ b/solution.py
@@ -122,11 +122,12 @@
             done += UNIT
 
 
-def put_shards(shards, b_high, b_low):
+def put_shards(shards, b_high, b_low, tiles=None):
     _, sections, depth, _ = shards[0].shape
     for i in range(len(shards) * sections):
         part = pl.ds(i * depth, depth)
-        b_high[part, :], b_low[part, :] = split(shards[i // sections][0, i % sections])
+        tile = tiles[i // sections] if tiles else slice(None)
+        b_high[part, :], b_low[part, :] = split(shards[i // sections][0, i % sections, :, tile])
 
 
 def stacked(refs):
@@ -150,11 +151,11 @@
 
 
 def far_value(first, *refs):
-    *lefts, near, near_late, shard, b_high, b_low = refs
+    *lefts, near, near_late, hop, shard, b_high, b_low = refs
     highs, lows = lefts[: len(lefts) // 2], lefts[len(lefts) // 2 :]
-    put_shards([shard], b_high, b_low)
+    tile = slice(first, first + shard.shape[3])
+    put_shards([hop, shard], b_high, b_low, [tile, slice(None)])
     value = product3(stacked(highs), stacked(lows), b_high[...], b_low[...])
-    tile = slice(first, first + shard.shape[3])
     return value + jnp.concatenate([near[:, tile], near_late[:, tile]], axis=0)
 
 
@@ -297,7 +298,7 @@
     a_tables = [a_pattern, lax.ppermute(a_pattern, "row", swap_y)]
     c_tables = [c_pattern, lax.ppermute(c_pattern, "row", swap_y)]
 
-    groups = [[(0, 0), (0, 1), (-1, 0), (1, 0)], [(-1, 1), (1, 1), (2, 0)], [(2, 1)]]
+    groups = [[(0, 0), (0, 1), (-1, 0), (1, 0)], [(-1, 1), (1, 1)], [(2, 0), (2, 1)]]
     shard_depth = sections * depth
 
     def left(*sources):
@@ -313,7 +314,7 @@
         )(a_pattern, a_tables[max(y for y, *_ in plan)], *arrays)
 
     early_sets = [
-        left((a_panels, 0, False, 0)), left((from_x, 0, True, 0)), left((y0, 1, False, 0), (y1, 1, False, UNIT))
+        left((a_panels, 0, False, 0)), left((from_x, 0, True, 0)), left((y0, 1, False, 0)), left((y1, 1, False, UNIT))
     ]
 
     def picked(sets, g):
@@ -333,27 +334,29 @@
             functools.partial(group_kernel, len(sets), 2),
             [shape((count, half), f32)],
             [VMEM] * (len(lefts) + len(rights)),
-            flops=6 * count * half * 7 * shard_depth,
+            flops=6 * count * half * 6 * shard_depth,
         )(*lefts, *rights)
         return total
 
     early_sets += [left((y2, 1, False, 2 * UNIT)), left((d0, 1, True, 0))]
     near = product(early_sets)
     d2, d1, near = together(d2, d1, near)
-    late_sets = [left((d1, 1, True, UNIT)), left((d2, 1, True, 2 * UNIT))]
+    late_sets = [left((d1, 1, True, UNIT))]
+    d2, late_sets[0] = together(d2, late_sets[0])
+    late_sets.append(left((d2, 1, True, 2 * UNIT)))
     near_late = product(late_sets)
 
     far_lefts = picked([*early_sets, *late_sets], 2)
 
     def far(kernel, first, shard, outs):
-        factor = pltpu.VMEM((shard_depth, shard.shape[3]), bf16)
+        factor = pltpu.VMEM((2 * shard_depth, shard.shape[3]), bf16)
         return call(
             functools.partial(kernel, first),
             outs,
-            [VMEM] * (len(far_lefts) + 3),
+            [VMEM] * (len(far_lefts) + 4),
             [factor, factor],
-            6 * 4 * rows * shard.shape[3] * shard_depth,
-        )(*far_lefts, near, near_late, shard)
+            6 * 4 * rows * shard.shape[3] * 2 * shard_depth,
+        )(*far_lefts, near, near_late, shards[2, 0], shard)
 
     kept, sent = far(far_kernel, 0, far_early, [shape((2, rows, cut), f32)] * 2)
     received = lax.ppermute(sent, "fiber", swap)

time: 93.4 us -> 95.2 us (1.019)
  waiting for transfers between devices: 50.4 us -> 45.5 us
  starting transfers between devices: 21.7 us -> 26.4 us
  Pallas kernels: 20.4 us -> 22.3 us
    ppermute x1, waiting for transfers between devices: 0.01 us -> 8.25 us  [local(): shards[0, 1] = lax.ppermute(columns_half(1 - my_y), 'row', swap_y)]
    ppermute x2, waiting for transfers between devices: 11.2 us -> 4.17 us  [local(): shards[-1, turn] = lax.ppermute(shards[0, turn], 'row', line_pairs(1))]
    ppermute x1, waiting for transfers between devices: 5.61 us -> 1.29 us  [local(): a_tables = [a_pattern, lax.ppermute(a_pattern, 'row', swap_y)]]
    ppermute x1, starting transfers between devices: 0.24 us -> 2.83 us  [local(): far_early = lax.ppermute(shards[-1, 1][..., :cut], 'row', line_pairs(1))]
    ppermute x3, waiting for transfers between devices: 10.3 us -> 12.6 us  [local(): lax.ppermute(a_panels[u * UNIT:(u + 1) * UNIT], 'row', swap_y)]
    ppermute x1, waiting for transfers between devices: 2.21 us -> 0.01 us  [local(): shards[2, 0] = lax.ppermute(shards[-1, 0], 'row', line_pairs(1))]
    pallas_call x16 -> x17, Pallas kernels: 20.4 us -> 22.3 us  [run(): pl.pallas_call(kernel, out_shape=out_shapes, in_specs=specs, out_specs=[V...]
    ppermute x1, starting transfers between devices: 0.41 us -> 1.58 us  [local(): c_tables = [c_pattern, lax.ppermute(c_pattern, 'row', swap_y)]]
  transfers between devices with their start and end apart: 25 -> 25, of which waited for: 13 -> 13; matrix products, arithmetic and copies ran while one was open for 1% -> 1% of each run, Pallas kernels for 20% -> 21%
where the time goes in v3:
time: 95.2 us; the launch traced here: 95 us
  waiting for transfers between devices  45.5 us (48%)
  starting transfers between devices  26.4 us (28%)
  Pallas kernels  22.3 us (23%)
    pallas_call x17, Pallas kernels, run(): pl.pallas_call(kernel, out_shape=out_shapes, in_specs=specs, out_specs=[V...  22.3 us
    ppermute x3, waiting for transfers between devices, local(): lax.ppermute(a_panels[u * UNIT:(u + 1) * UNIT], 'row', swap_y)  12.6 us
    ppermute x1, waiting for transfers between devices, local(): shards[0, 1] = lax.ppermute(columns_half(1 - my_y), 'row', swap_y)  8.25 us
    ppermute x2, waiting for transfers between devices, local(): lax.ppermute(sums, 'row', [(r, r ^ bit) for r in range(n_row)])  8.06 us
    ppermute x1, waiting for transfers between devices, local(): far_last = lax.ppermute(shards[-1, 1][..., cut:], 'row', line_pairs(1))  5.84 us
    ppermute x2, starting transfers between devices, local(): shards[1, turn] = lax.ppermute(shards[0, turn], 'row', line_pairs(-1))  5.56 us
    ppermute x2, waiting for transfers between devices, local(): shards[-1, turn] = lax.ppermute(shards[0, turn], 'row', line_pairs(1))  4.17 us
    ppermute x3, starting transfers between devices, local(): lax.ppermute(a_panels[u * UNIT:(u + 1) * UNIT], 'row', swap_y)  3.55 us
  transfers between devices with their start and end apart: 25, of which 13 were waited for; matrix products, arithmetic and copies ran while one was open for 1% of the time, Pallas kernels for 21%

profile of v3, /device:TPU:0, one launch (start us, length us, event | category | flops | bytes accessed | tf_op | source)
XLA Modules:
  0.0 95.0 jit_solution(15445939127090909263)
XLA Ops:
  0.0 3.0 %collective-permute-start.1 = (f32[192,1,2,768]{3,2,1,0:T(2,128)}, f32[192,1,2,768]{3,2,1,0:T(2,128)S(1)}, u32[]{:S(2)}, u32[]{:S(2)}) collective-permute-start(f32[192,1,2,768]{3,2,1,0:T(2,128)} %refs_0_.1), channel_id=1, source_target_pairs={{0,2},{2,0},{1,3},{3,1},{4,6},{6,4},{5,7},{7,5},{8,10},{10,8},{9,1... | collective-permute-start | bytes 3538952 | tf_op jit(solution)/shard_map/ppermute | solution.py:291
  3.0 2.6 %collective-permute-start.11 = (f32[1,2,96,512]{3,2,1,0:T(8,128)S(1)}, f32[1,2,96,512]{3,2,1,0:T(8,128)}, u32[]{:S(2)}, u32[]{:S(2)}) collective-permute-start(f32[1,2,96,512]{3,2,1,0:T(8,128)S(1)} %constant_dynamic-slice_fusion.1.refs_0_), channel_id=1, source_target_pairs={{0,16},{4,20},{8,0},{12,4},{24,8},{28,12},{16,24},{20,28},{1,17},{... | collective-permute-start | bytes 1179656 | tf_op jit(solution)/shard_map/ppermute | solution.py:286
  5.7 1.5 %collective-permute-start.2 = (s32[3,1,2,6]{3,2,1,0:T(2,128)}, s32[3,1,2,6]{3,2,1,0:T(2,128)S(1)}, u32[]{:S(2)}, u32[]{:S(2)}) collective-permute-start(s32[3,1,2,6]{3,2,1,0:T(2,128)} %pattern.17), channel_id=1, source_target_pairs={{0,4},{4,0},{8,12},{12,8},{16,20},{20,16},{24,28},{28,24},{1,5},{5... | collective-permute-start | bytes 440 | tf_op jit(solution)/shard_map/ppermute | solution.py:298
  9.5 1.5 %collective-permute-start.3 = (f32[64,1,2,768]{3,2,1,0:T(2,128)S(1)}, f32[64,1,2,768]{3,2,1,0:T(2,128)S(1)}, u32[]{:S(2)}, u32[]{:S(2)}) collective-permute-start(f32[64,1,2,768]{3,2,1,0:T(2,128)S(1)} %get-tuple-element.150), channel_id=1, source_target_pairs={{0,4},{4,0},{8,12},{12,8},{16,20},{20,16},{24,28},{28,24},{1,5},{5... | collective-permute-start | bytes 1179656 | tf_op jit(solution)/shard_map/ppermute | solution.py:293
  11.0 8.2 %collective-permute-done.9.refs_1_ = f32[1,2,96,512]{3,2,1,0:T(8,128)S(1)} collective-permute-done((f32[1,2,96,512]{3,2,1,0:T(8,128)S(1)}, f32[1,2,96,512]{3,2,1,0:T(8,128)S(1)}, u32[]{:S(2)}, u32[]{:S(2)}) %collective-permute-start.9) | collective-permute-done | bytes 393248 | tf_op jit(solution)/shard_map/ppermute | solution.py:283
  19.8 1.5 %collective-permute-start.5 = (f32[64,1,2,768]{3,2,1,0:T(2,128)S(1)}, f32[64,1,2,768]{3,2,1,0:T(2,128)S(1)}, u32[]{:S(2)}, u32[]{:S(2)}) collective-permute-start(f32[64,1,2,768]{3,2,1,0:T(2,128)S(1)} %get-tuple-element.149), channel_id=1, source_target_pairs={{0,4},{4,0},{8,12},{12,8},{16,20},{20,16},{24,28},{28,24},{1,5},{5... | collective-permute-start | bytes 1179656 | tf_op jit(solution)/shard_map/ppermute | solution.py:293
  21.3 2.8 %collective-permute-done.10.refs_2_ = f32[1,2,96,512]{3,2,1,0:T(8,128)} collective-permute-done((f32[1,2,96,512]{3,2,1,0:T(8,128)S(1)}, f32[1,2,96,512]{3,2,1,0:T(8,128)}, u32[]{:S(2)}, u32[]{:S(2)}) %collective-permute-start.10) | collective-permute-done | bytes 393248 | tf_op jit(solution)/shard_map/ppermute | solution.py:285
  24.8 2.9 %collective-permute-done.3.refs_0_ = f32[64,1,2,768]{3,2,1,0:T(2,128)S(1)} collective-permute-done((f32[64,1,2,768]{3,2,1,0:T(2,128)S(1)}, f32[64,1,2,768]{3,2,1,0:T(2,128)S(1)}, u32[]{:S(2)}, u32[]{:S(2)}) %collective-permute-start.3) | collective-permute-done | bytes 393248 | tf_op jit(solution)/shard_map/ppermute | solution.py:293
  27.7 2.9 %collective-permute-start.13 = (f32[1,2,96,512]{3,2,1,0:T(8,128)S(1)}, f32[1,2,96,512]{3,2,1,0:T(8,128)S(1)}, u32[]{:S(2)}, u32[]{:S(2)}) collective-permute-start(f32[1,2,96,512]{3,2,1,0:T(8,128)S(1)} %collective-permute-done.9.refs_1_), channel_id=1, source_target_pairs={{0,16},{4,20},{8,0},{12,4},{24,8},{28,12},{16,24},{20,28},{1,17},{... | collective-permute-start | bytes 1179656 | tf_op jit(solution)/shard_map/ppermute | solution.py:286
  31.8 4.3 %collective-permute-done.4.refs_0_ = f32[64,1,2,768]{3,2,1,0:T(2,128)S(1)} collective-permute-done((f32[64,1,2,768]{3,2,1,0:T(2,128)S(1)}, f32[64,1,2,768]{3,2,1,0:T(2,128)S(1)}, u32[]{:S(2)}, u32[]{:S(2)}) %collective-permute-start.4) | collective-permute-done | bytes 393248 | tf_op jit(solution)/shard_map/ppermute | solution.py:293
  37.2 5.4 %collective-permute-done.5.refs_0_ = f32[64,1,2,768]{3,2,1,0:T(2,128)S(1)} collective-permute-done((f32[64,1,2,768]{3,2,1,0:T(2,128)S(1)}, f32[64,1,2,768]{3,2,1,0:T(2,128)S(1)}, u32[]{:S(2)}, u32[]{:S(2)}) %collective-permute-start.5) | collective-permute-done | bytes 393248 | tf_op jit(solution)/shard_map/ppermute | solution.py:293
  43.1 1.4 %collective-permute-done.12.refs_0_ = f32[1,2,96,512]{3,2,1,0:T(8,128)S(1)} collective-permute-done((f32[1,2,96,512]{3,2,1,0:T(8,128)S(1)}, f32[1,2,96,512]{3,2,1,0:T(8,128)S(1)}, u32[]{:S(2)}, u32[]{:S(2)}) %collective-permute-start.12) | collective-permute-done | bytes 393248 | tf_op jit(solution)/shard_map/ppermute | solution.py:285
  44.8 2.8 %collective-permute-start.17 = (f32[1,2,96,384]{3,2,1,0:T(8,128)S(1)}, f32[1,2,96,384]{3,2,1,0:T(8,128)S(1)}, u32[]{:S(2)}, u32[]{:S(2)}) collective-permute-start(f32[1,2,96,384]{3,2,1,0:T(8,128)S(1)} %slice.26), channel_id=1, source_target_pairs={{0,8},{4,12},{8,24},{12,28},{24,16},{28,20},{16,0},{20,4},{1,9},{5... | collective-permute-start | bytes 884744 | tf_op jit(solution)/shard_map/ppermute | solution.py:288
  47.6 2.6 %shard_map.46 = (bf16[192,768]{1,0:T(8,128)(2,1)S(1)}, bf16[192,768]{1,0:T(8,128)(2,1)S(1)}, bf16[192,384]{1,0:T(8,128)(2,1)S(1)}, bf16[192,384]{1,0:T(8,128)(2,...) custom-call(s32[3,1,2,6]{3,2,1,0:T(2,128)S(1)} %copy-done.2, s32[3,1,2,6]{3,2,1,0:T(2,128)S(1)} %copy-done.2, ...), custom_call_target="tpu_custom_call" | custom-call | bytes 2359584 | tf_op jit(solution)/shard_map/pallas_call | solution.py:245
  57.0 2.6 %shard_map.47 = (bf16[192,768]{1,0:T(8,128)(2,1)S(1)}, bf16[192,768]{1,0:T(8,128)(2,1)S(1)}, bf16[192,384]{1,0:T(8,128)(2,1)S(1)}, bf16[192,384]{1,0:T(8,128)(2,...) custom-call(s32[3,1,2,6]{3,2,1,0:T(2,128)S(1)} %copy-done.2, s32[3,1,2,6]{3,2,1,0:T(2,128)S(1)} %copy-done.2, ...), custom_call_target="tpu_custom_call" | custom-call | bytes 2359584 | tf_op jit(solution)/shard_map/pallas_call | solution.py:245
  59.5 2.7 %shard_map.54.refs_16_ = f32[640,512]{1,0:T(8,128)S(1)} custom-call(bf16[192,768]{1,0:T(8,128)(2,1)S(1)} %get-tuple-element.83.refs_0_, bf16[192,768]{1,0:T(8,128)(2,1)S(1)} %get-tuple-element.84.refs_1_, bf16[64,768]{1,0:T(8,128)(2,1)S(1)} %get-tuple-element.85.refs_2_, bf16[64,768]{1,0:T(8,128)(2,1)S(1)} %get-tuple-element.86.refs_3_, ...), custom_call_target="tpu_custom_call" | custom-call | flops 2264924160 | bytes 6619136 | tf_op jit(solution)/shard_map/pallas_call | solution.py:245
  67.4 5.8 %collective-permute-done.15.refs_19_ = f32[1,2,96,128]{3,2,1,0:T(8,128)S(1)} collective-permute-done((f32[1,2,96,128]{3,2,1,0:T(8,128)S(1)}, f32[1,2,96,128]{3,2,1,0:T(8,128)S(1)}, u32[]{:S(2)}, u32[]{:S(2)}) %collective-permute-start.15) | collective-permute-done | bytes 98336 | tf_op jit(solution)/shard_map/ppermute | solution.py:289
  74.0 1.6 %collective-permute-start = (s32[3,8]{1,0:T(4,128)S(1)}, s32[3,8]{1,0:T(4,128)S(1)}, u32[]{:S(2)}, u32[]{:S(2)}) collective-permute-start(s32[3,8]{1,0:T(4,128)S(1)} %copy-done.3), channel_id=1, source_target_pairs={{0,4},{4,0},{8,12},{12,8},{16,20},{20,16},{24,28},{28,24},{1,5},{5... | collective-permute-start | bytes 296 | tf_op jit(solution)/shard_map/ppermute | solution.py:299
  75.6 2.1 %collective-permute-done.other_pattern = s32[3,8]{1,0:T(4,128)S(1)} collective-permute-done((s32[3,8]{1,0:T(4,128)S(1)}, s32[3,8]{1,0:T(4,128)S(1)}, u32[]{:S(2)}, u32[]{:S(2)}) %collective-permute-start) | collective-permute-done | bytes 128 | tf_op jit(solution)/shard_map/ppermute | solution.py:299
  78.4 1.6 %collective-permute-start.23 = (f32[192,384]{1,0:T(8,128)S(1)}, f32[192,384]{1,0:T(8,128)S(1)}, u32[]{:S(2)}, u32[]{:S(2)}) collective-permute-start(f32[192,384]{1,0:T(8,128)S(1)} %get-tuple-element.147), channel_id=1, source_target_pairs={{0,4},{4,0},{8,12},{12,8},{16,20},{20,16},{24,28},{28,24},{1,5},{5... | collective-permute-start | bytes 884744 | tf_op jit(solution)/shard_map/ppermute | solution.py:368
  82.4 3.6 %collective-permute-done.20 = f32[1,512]{1,0:T(1,128)S(1)} collective-permute-done((f32[1,512]{1,0:T(1,128)S(1)}, f32[1,512]{1,0:T(1,128)S(1)}, u32[]{:S(2)}, u32[]{:S(2)}) %collective-permute-start.20) | collective-permute-done | bytes 2080 | tf_op jit(solution)/shard_map/ppermute | solution.py:377
  86.0 4.5 %collective-permute-done.21 = f32[1,512]{1,0:T(1,128)S(1)} collective-permute-done((f32[1,512]{1,0:T(1,128)S(1)}, f32[1,512]{1,0:T(1,128)S(1)}, u32[]{:S(2)}, u32[]{:S(2)}) %collective-permute-start.21) | collective-permute-done | bytes 2080 | tf_op jit(solution)/shard_map/ppermute | solution.py:377
  90.5 1.5 %collective-permute-start.22 = (f32[1,512]{1,0:T(1,128)S(1)}, f32[1,512]{1,0:T(1,128)S(1)}, u32[]{:S(2)}, u32[]{:S(2)}) collective-permute-start(f32[1,512]{1,0:T(1,128)S(1)} %add.11.sums), channel_id=1, source_target_pairs={{0,4},{4,0},{8,12},{12,8},{16,20},{20,16},{24,28},{28,24},{1,5},{5... | collective-permute-start | bytes 6152 | tf_op jit(solution)/shard_map/ppermute | solution.py:378
  92.0 2.1 %collective-permute-done.22.other_sums = f32[1,512]{1,0:T(1,128)S(1)} collective-permute-done((f32[1,512]{1,0:T(1,128)S(1)}, f32[1,512]{1,0:T(1,128)S(1)}, u32[]{:S(2)}, u32[]{:S(2)}) %collective-permute-start.22) | collective-permute-done | bytes 2080 | tf_op jit(solution)/shard_map/ppermute | solution.py:378
  (60 shorter events, 23.3 us)
Async XLA Ops:
  0.0 30.6 %collective-permute-start.1 = (f32[192,1,2,768]{3,2,1,0:T(2,128)}, f32[192,1,2,768]{3,2,1,0:T(2,128)S(1)}, u32[]{:S(2)}, u32[]{:S(2)}) collective-permute-start(f32[192,1,2,768]{3,2,1,0:T(2,128)} %refs_0_.1), channel_id=1, source_target_pairs={{0,2},{2,0},{1,3},{3,1},{4,6},{6,4},{5,7},{7,5},{8,10},{10,8},{9,1... | collective-permute-start | bytes 3538952 | tf_op jit(solution)/shard_map/ppermute | solution.py:291
  3.0 16.8 %collective-permute-start.11 = (f32[1,2,96,512]{3,2,1,0:T(8,128)S(1)}, f32[1,2,96,512]{3,2,1,0:T(8,128)}, u32[]{:S(2)}, u32[]{:S(2)}) collective-permute-start(f32[1,2,96,512]{3,2,1,0:T(8,128)S(1)} %constant_dynamic-slice_fusion.1.refs_0_), channel_id=1, source_target_pairs={{0,16},{4,20},{8,0},{12,4},{24,8},{28,12},{16,24},{20,28},{1,17},{... | collective-permute-start | bytes 1179656 | tf_op jit(solution)/shard_map/ppermute | solution.py:286
  5.7 18.4 %collective-permute-start.10 = (f32[1,2,96,512]{3,2,1,0:T(8,128)S(1)}, f32[1,2,96,512]{3,2,1,0:T(8,128)}, u32[]{:S(2)}, u32[]{:S(2)}) collective-permute-start(f32[1,2,96,512]{3,2,1,0:T(8,128)S(1)} %constant_dynamic-slice_fusion.1.refs_0_), channel_id=1, source_target_pairs={{0,8},{4,12},{8,24},{12,28},{24,16},{28,20},{16,0},{20,4},{1,9},{5... | collective-permute-start | bytes 1179656 | tf_op jit(solution)/shard_map/ppermute | solution.py:285
  5.7 3.8 %collective-permute-start.2 = (s32[3,1,2,6]{3,2,1,0:T(2,128)}, s32[3,1,2,6]{3,2,1,0:T(2,128)S(1)}, u32[]{:S(2)}, u32[]{:S(2)}) collective-permute-start(s32[3,1,2,6]{3,2,1,0:T(2,128)} %pattern.17), channel_id=1, source_target_pairs={{0,4},{4,0},{8,12},{12,8},{16,20},{20,16},{24,28},{28,24},{1,5},{5... | collective-permute-start | bytes 440 | tf_op jit(solution)/shard_map/ppermute | solution.py:298
  7.2 12.1 %collective-permute-start.9 = (f32[1,2,96,512]{3,2,1,0:T(8,128)S(1)}, f32[1,2,96,512]{3,2,1,0:T(8,128)S(1)}, u32[]{:S(2)}, u32[]{:S(2)}) collective-permute-start(f32[1,2,96,512]{3,2,1,0:T(8,128)S(1)} %constant_dynamic-slice_fusion), channel_id=1, source_target_pairs={{0,4},{4,0},{8,12},{12,8},{16,20},{20,16},{24,28},{28,24},{1,5},{5... | collective-permute-start | bytes 1179656 | tf_op jit(solution)/shard_map/ppermute | solution.py:283
  9.5 18.2 %collective-permute-start.3 = (f32[64,1,2,768]{3,2,1,0:T(2,128)S(1)}, f32[64,1,2,768]{3,2,1,0:T(2,128)S(1)}, u32[]{:S(2)}, u32[]{:S(2)}) collective-permute-start(f32[64,1,2,768]{3,2,1,0:T(2,128)S(1)} %get-tuple-element.150), channel_id=1, source_target_pairs={{0,4},{4,0},{8,12},{12,8},{16,20},{20,16},{24,28},{28,24},{1,5},{5... | collective-permute-start | bytes 1179656 | tf_op jit(solution)/shard_map/ppermute | solution.py:293
  19.3 16.9 %collective-permute-start.4 = (f32[64,1,2,768]{3,2,1,0:T(2,128)S(1)}, f32[64,1,2,768]{3,2,1,0:T(2,128)S(1)}, u32[]{:S(2)}, u32[]{:S(2)}) collective-permute-start(f32[64,1,2,768]{3,2,1,0:T(2,128)S(1)} %get-tuple-element.151), channel_id=1, source_target_pairs={{0,4},{4,0},{8,12},{12,8},{16,20},{20,16},{24,28},{28,24},{1,5},{5... | collective-permute-start | bytes 1179656 | tf_op jit(solution)/shard_map/ppermute | solution.py:293
  19.8 22.8 %collective-permute-start.5 = (f32[64,1,2,768]{3,2,1,0:T(2,128)S(1)}, f32[64,1,2,768]{3,2,1,0:T(2,128)S(1)}, u32[]{:S(2)}, u32[]{:S(2)}) collective-permute-start(f32[64,1,2,768]{3,2,1,0:T(2,128)S(1)} %get-tuple-element.149), channel_id=1, source_target_pairs={{0,4},{4,0},{8,12},{12,8},{16,20},{20,16},{24,28},{28,24},{1,5},{5... | collective-permute-start | bytes 1179656 | tf_op jit(solution)/shard_map/ppermute | solution.py:293
  24.1 20.4 %collective-permute-start.12 = (f32[1,2,96,512]{3,2,1,0:T(8,128)S(1)}, f32[1,2,96,512]{3,2,1,0:T(8,128)S(1)}, u32[]{:S(2)}, u32[]{:S(2)}) collective-permute-start(f32[1,2,96,512]{3,2,1,0:T(8,128)S(1)} %collective-permute-done.9.refs_1_), channel_id=1, source_target_pairs={{0,8},{4,12},{8,24},{12,28},{24,16},{28,20},{16,0},{20,4},{1,9},{5... | collective-permute-start | bytes 1179656 | tf_op jit(solution)/shard_map/ppermute | solution.py:285
  27.7 17.1 %collective-permute-start.13 = (f32[1,2,96,512]{3,2,1,0:T(8,128)S(1)}, f32[1,2,96,512]{3,2,1,0:T(8,128)S(1)}, u32[]{:S(2)}, u32[]{:S(2)}) collective-permute-start(f32[1,2,96,512]{3,2,1,0:T(8,128)S(1)} %collective-permute-done.9.refs_1_), channel_id=1, source_target_pairs={{0,16},{4,20},{8,0},{12,4},{24,8},{28,12},{16,24},{20,28},{1,17},{... | collective-permute-start | bytes 1179656 | tf_op jit(solution)/shard_map/ppermute | solution.py:286
  30.6 25.0 %collective-permute-start.6 = (f32[64,1,2,768]{3,2,1,0:T(2,128)S(1)}, f32[64,1,2,768]{3,2,1,0:T(2,128)S(1)}, u32[]{:S(2)}, u32[]{:S(2)}) collective-permute-start(f32[64,1,2,768]{3,2,1,0:T(2,128)S(1)} %collective-permute-done.3.refs_0_), channel_id=1, source_target_pairs={{0,2},{2,0},{1,3},{3,1},{4,6},{6,4},{5,7},{7,5},{8,10},{10,8},{9,1... | collective-permute-start | bytes 1179656 | tf_op jit(solution)/shard_map/ppermute | solution.py:296
  36.1 26.1 %collective-permute-start.8 = (f32[64,1,2,768]{3,2,1,0:T(2,128)S(1)}, f32[64,1,2,768]{3,2,1,0:T(2,128)S(1)}, u32[]{:S(2)}, u32[]{:S(2)}) collective-permute-start(f32[64,1,2,768]{3,2,1,0:T(2,128)S(1)} %collective-permute-done.4.refs_0_), channel_id=1, source_target_pairs={{0,2},{2,0},{1,3},{3,1},{4,6},{6,4},{5,7},{7,5},{8,10},{10,8},{9,1... | collective-permute-start | bytes 1179656 | tf_op jit(solution)/shard_map/ppermute | solution.py:297
  42.6 19.7 %collective-permute-start.7 = (f32[64,1,2,768]{3,2,1,0:T(2,128)S(1)}, f32[64,1,2,768]{3,2,1,0:T(2,128)S(1)}, u32[]{:S(2)}, u32[]{:S(2)}) collective-permute-start(f32[64,1,2,768]{3,2,1,0:T(2,128)S(1)} %slice.24), channel_id=1, source_target_pairs={{0,4},{4,0},{8,12},{12,8},{16,20},{20,16},{24,28},{28,24},{1,5},{5... | collective-permute-start | bytes 1179656 | tf_op jit(solution)/shard_map/ppermute | solution.py:295
  44.5 21.1 %collective-permute-start.14 = (f32[1,2,96,512]{3,2,1,0:T(8,128)}, f32[1,2,96,512]{3,2,1,0:T(8,128)S(1)}, u32[]{:S(2)}, u32[]{:S(2)}) collective-permute-start(f32[1,2,96,512]{3,2,1,0:T(8,128)} %collective-permute-done.10.refs_2_), channel_id=1, source_target_pairs={{0,8},{4,12},{8,24},{12,28},{24,16},{28,20},{16,0},{20,4},{1,9},{5... | collective-permute-start | bytes 1179656 | tf_op jit(solution)/shard_map/ppermute | solution.py:287
  44.8 20.8 %collective-permute-start.17 = (f32[1,2,96,384]{3,2,1,0:T(8,128)S(1)}, f32[1,2,96,384]{3,2,1,0:T(8,128)S(1)}, u32[]{:S(2)}, u32[]{:S(2)}) collective-permute-start(f32[1,2,96,384]{3,2,1,0:T(8,128)S(1)} %slice.26), channel_id=1, source_target_pairs={{0,8},{4,12},{8,24},{12,28},{24,16},{28,20},{16,0},{20,4},{1,9},{5... | collective-permute-start | bytes 884744 | tf_op jit(solution)/shard_map/ppermute | solution.py:288
  67.0 10.6 %collective-permute-start.18 = (f32[2,192,384]{2,1,0:T(8,128)S(1)}, f32[2,192,384]{2,1,0:T(8,128)S(1)}, u32[]{:S(2)}, u32[]{:S(2)}) collective-permute-start(f32[2,192,384]{2,1,0:T(8,128)S(1)} %get-tuple-element.142), channel_id=1, source_target_pairs={{0,1},{1,0},{2,3},{3,2},{4,5},{5,4},{6,7},{7,6},{8,9},{9,8},{10,11... | collective-permute-start | bytes 1769480 | tf_op jit(solution)/shard_map/ppermute | solution.py:362
  67.1 6.1 %collective-permute-start.15 = (f32[1,2,96,128]{3,2,1,0:T(8,128)S(1)}, f32[1,2,96,128]{3,2,1,0:T(8,128)S(1)}, u32[]{:S(2)}, u32[]{:S(2)}) collective-permute-start(f32[1,2,96,128]{3,2,1,0:T(8,128)S(1)} %slice.25), channel_id=1, source_target_pairs={{0,8},{4,12},{8,24},{12,28},{24,16},{28,20},{16,0},{20,4},{1,9},{5... | collective-permute-start | bytes 294920 | tf_op jit(solution)/shard_map/ppermute | solution.py:289
  73.9 7.2 %collective-permute-start.16 = (f32[4,192,128]{2,1,0:T(8,128)S(1)}, f32[4,192,128]{2,1,0:T(8,128)S(1)}, u32[]{:S(2)}, u32[]{:S(2)}) collective-permute-start(f32[4,192,128]{2,1,0:T(8,128)S(1)} %shard_map.58.mine), channel_id=1, source_target_pairs={{0,1},{1,0},{2,3},{3,2},{4,5},{5,4},{6,7},{7,6},{8,9},{9,8},{10,11... | collective-permute-start | bytes 1179656 | tf_op jit(solution)/shard_map/ppermute | solution.py:364
  74.0 3.7 %collective-permute-start = (s32[3,8]{1,0:T(4,128)S(1)}, s32[3,8]{1,0:T(4,128)S(1)}, u32[]{:S(2)}, u32[]{:S(2)}) collective-permute-start(s32[3,8]{1,0:T(4,128)S(1)} %copy-done.3), channel_id=1, source_target_pairs={{0,4},{4,0},{8,12},{12,8},{16,20},{20,16},{24,28},{28,24},{1,5},{5... | collective-permute-start | bytes 296 | tf_op jit(solution)/shard_map/ppermute | solution.py:299
  78.4 15.7 %collective-permute-start.23 = (f32[192,384]{1,0:T(8,128)S(1)}, f32[192,384]{1,0:T(8,128)S(1)}, u32[]{:S(2)}, u32[]{:S(2)}) collective-permute-start(f32[192,384]{1,0:T(8,128)S(1)} %get-tuple-element.147), channel_id=1, source_target_pairs={{0,4},{4,0},{8,12},{12,8},{16,20},{20,16},{24,28},{28,24},{1,5},{5... | collective-permute-start | bytes 884744 | tf_op jit(solution)/shard_map/ppermute | solution.py:368
  81.8 12.2 %collective-permute-start.24 = (f32[192,128]{1,0:T(8,128)S(1)}, f32[192,128]{1,0:T(8,128)S(1)}, u32[]{:S(2)}, u32[]{:S(2)}) collective-permute-start(f32[192,128]{1,0:T(8,128)S(1)} %get-tuple-element.148), channel_id=1, source_target_pairs={{0,4},{4,0},{8,12},{12,8},{16,20},{20,16},{24,28},{28,24},{1,5},{5... | collective-permute-start | bytes 294920 | tf_op jit(solution)/shard_map/ppermute | solution.py:375
  82.4 3.6 %collective-permute-start.20 = (f32[1,512]{1,0:T(1,128)S(1)}, f32[1,512]{1,0:T(1,128)S(1)}, u32[]{:S(2)}, u32[]{:S(2)}) collective-permute-start(f32[1,512]{1,0:T(1,128)S(1)} %get-tuple-element.144), channel_id=1, source_target_pairs={{0,8},{4,12},{8,0},{12,4},{16,24},{20,28},{24,16},{28,20},{1,9},{5... | collective-permute-start | bytes 6152 | tf_op jit(solution)/shard_map/ppermute | solution.py:377
  86.0 4.5 %collective-permute-start.21 = (f32[1,512]{1,0:T(1,128)S(1)}, f32[1,512]{1,0:T(1,128)S(1)}, u32[]{:S(2)}, u32[]{:S(2)}) collective-permute-start(f32[1,512]{1,0:T(1,128)S(1)} %add.10), channel_id=1, source_target_pairs={{0,16},{4,20},{8,24},{12,28},{16,0},{20,4},{24,8},{28,12},{1,17},{... | collective-permute-start | bytes 6152 | tf_op jit(solution)/shard_map/ppermute | solution.py:377
  90.5 3.6 %collective-permute-start.22 = (f32[1,512]{1,0:T(1,128)S(1)}, f32[1,512]{1,0:T(1,128)S(1)}, u32[]{:S(2)}, u32[]{:S(2)}) collective-permute-start(f32[1,512]{1,0:T(1,128)S(1)} %add.11.sums), channel_id=1, source_target_pairs={{0,4},{4,0},{8,12},{12,8},{16,20},{20,16},{24,28},{28,24},{1,5},{5... | collective-permute-start | bytes 6152 | tf_op jit(solution)/shard_map/ppermute | solution.py:378
  (5 other events, 58.2 us)

commit v4 on v2

--- a/solution.py
+++ b/solution.py
@@ -149,13 +149,19 @@
     out[...] = total
 
 
+def hop_kernel(sets, *refs):
+    lefts, (*nears, shard, out, b_high, b_low) = refs[: 2 * sets], refs[2 * sets :]
+    put_shards([shard], b_high, b_low)
+    value = product3(stacked(lefts[:sets]), stacked(lefts[sets:]), b_high[...], b_low[...])
+    out[...] = value + stacked(nears)
+
+
 def far_value(first, *refs):
-    *lefts, near, near_late, shard, b_high, b_low = refs
+    *lefts, near, shard, b_high, b_low = refs
     highs, lows = lefts[: len(lefts) // 2], lefts[len(lefts) // 2 :]
     put_shards([shard], b_high, b_low)
     value = product3(stacked(highs), stacked(lows), b_high[...], b_low[...])
-    tile = slice(first, first + shard.shape[3])
-    return value + jnp.concatenate([near[:, tile], near_late[:, tile]], axis=0)
+    return value + near[:, first : first + shard.shape[3]]
 
 
 def far_kernel(first, *refs):
@@ -297,7 +303,7 @@
     a_tables = [a_pattern, lax.ppermute(a_pattern, "row", swap_y)]
     c_tables = [c_pattern, lax.ppermute(c_pattern, "row", swap_y)]
 
-    groups = [[(0, 0), (0, 1), (-1, 0), (1, 0)], [(-1, 1), (1, 1), (2, 0)], [(2, 1)]]
+    groups = [[(0, 0), (0, 1), (-1, 0), (1, 0)], [(-1, 1), (1, 1)], [(2, 0)], [(2, 1)]]
     shard_depth = sections * depth
 
     def left(*sources):
@@ -313,7 +319,10 @@
         )(a_pattern, a_tables[max(y for y, *_ in plan)], *arrays)
 
     early_sets = [
-        left((a_panels, 0, False, 0)), left((from_x, 0, True, 0)), left((y0, 1, False, 0), (y1, 1, False, UNIT))
+        left((a_panels, 0, False, 0)),
+        left((from_x, 0, True, 0)),
+        left((y0, 1, False, 0)),
+        left((y1, 1, False, UNIT)),
     ]
 
     def picked(sets, g):
@@ -323,7 +332,9 @@
     for g in range(2):
         members = [shards[m] for m in groups[g]]
         rights += call(
-            split_kernel, [shape((len(members) * shard_depth, half), bf16)] * 2, [VMEM] * len(members)
+            split_kernel,
+            [shape((len(members) * shard_depth, half), bf16)] * 2,
+            [VMEM] * len(members),
         )(*members)
 
     def product(sets):
@@ -333,34 +344,49 @@
             functools.partial(group_kernel, len(sets), 2),
             [shape((count, half), f32)],
             [VMEM] * (len(lefts) + len(rights)),
-            flops=6 * count * half * 7 * shard_depth,
+            flops=6 * count * half * 6 * shard_depth,
         )(*lefts, *rights)
         return total
 
     early_sets += [left((y2, 1, False, 2 * UNIT)), left((d0, 1, True, 0))]
     near = product(early_sets)
     d2, d1, near = together(d2, d1, near)
-    late_sets = [left((d1, 1, True, UNIT)), left((d2, 1, True, 2 * UNIT))]
+    late_sets = [left((d1, 1, True, UNIT))]
+    d2, late_sets[0] = together(d2, late_sets[0])
+    late_sets.append(left((d2, 1, True, 2 * UNIT)))
     near_late = product(late_sets)
 
-    far_lefts = picked([*early_sets, *late_sets], 2)
+    all_sets = [*early_sets, *late_sets]
+    hop_lefts = picked(all_sets, 2)
+    factor = pltpu.VMEM((shard_depth, half), bf16)
+    (near,) = call(
+        functools.partial(hop_kernel, len(all_sets)),
+        [shape((4 * rows, half), f32)],
+        [VMEM] * (len(hop_lefts) + 3),
+        [factor, factor],
+        6 * 4 * rows * half * shard_depth,
+    )(*hop_lefts, near, near_late, shards[2, 0])
+
+    far_lefts = picked(all_sets, 3)
 
     def far(kernel, first, shard, outs):
         factor = pltpu.VMEM((shard_depth, shard.shape[3]), bf16)
         return call(
             functools.partial(kernel, first),
             outs,
-            [VMEM] * (len(far_lefts) + 3),
+            [VMEM] * (len(far_lefts) + 2),
             [factor, factor],
             6 * 4 * rows * shard.shape[3] * shard_depth,
-        )(*far_lefts, near, near_late, shard)
+        )(*far_lefts, near, shard)
 
     kept, sent = far(far_kernel, 0, far_early, [shape((2, rows, cut), f32)] * 2)
     received = lax.ppermute(sent, "fiber", swap)
     (mine,) = far(last_kernel, cut, far_last, [shape((4, rows, LAST), f32)])
     theirs = lax.ppermute(mine, "fiber", swap)
     stays, goes, sums = call(
-        square_kernel, [shape((rows, cut), f32)] * 2 + [shape((1, cut), f32)], [SMEM, SMEM, VMEM, VMEM]
+        square_kernel,
+        [shape((rows, cut), f32)] * 2 + [shape((1, cut), f32)],
+        [SMEM, SMEM, VMEM, VMEM],
     )(*c_tables, kept, received)
     comes = lax.ppermute(goes, "row", swap_y)
     sums = sums + lax.ppermute(sums, "fiber", swap)
@@ -374,7 +400,9 @@
         sums = sums + lax.ppermute(sums, "row", [(r, r ^ bit) for r in range(n_row)])
     other_sums = lax.ppermute(sums, "row", swap_y)
     (out,) = call(
-        functools.partial(scale_kernel, share * fibers * n_row), [shape((share, columns), f32)], [VMEM] * 6
+        functools.partial(scale_kernel, share * fibers * n_row),
+        [shape((share, columns), f32)],
+        [VMEM] * 6,
     )(sums, other_sums, stays, last_stays, comes, last_comes)
     return out
 
@@ -387,4 +415,6 @@
         P("row", "col"),
     )
 
-    return jax.shard_map(local, mesh=mesh, in_specs=placed, out_specs=P(("row", "fiber"), "col"), check_vma=False)
+    return jax.shard_map(
+        local, mesh=mesh, in_specs=placed, out_specs=P(("row", "fiber"), "col"), check_vma=False
+    )

time: 93.4 us -> 95.4 us (1.021)
  starting transfers between devices: 21.7 us -> 26.7 us
  waiting for transfers between devices: 50.4 us -> 45.5 us
  Pallas kernels: 20.4 us -> 22.3 us
    ppermute x1, waiting for transfers between devices: 0.01 us -> 8.26 us  [local(): shards[0, 1] = lax.ppermute(columns_half(1 - my_y), 'row', swap_y)]
    ppermute x2, waiting for transfers between devices: 11.2 us -> 4.14 us  [local(): shards[-1, turn] = lax.ppermute(shards[0, turn], 'row', line_pairs(1))]
    ppermute x1, waiting for transfers between devices: 5.61 us -> 1.29 us  [local(): a_tables = [a_pattern, lax.ppermute(a_pattern, 'row', swap_y)]]
    ppermute x1, starting transfers between devices: 0.24 us -> 3 us  [local(): far_early = lax.ppermute(shards[-1, 1][..., :cut], 'row', line_pairs(1))]
    ppermute x3, waiting for transfers between devices: 10.3 us -> 12.6 us  [local(): lax.ppermute(a_panels[u * UNIT:(u + 1) * UNIT], 'row', swap_y)]
    ppermute x1, waiting for transfers between devices: 2.21 us -> 0.01 us  [local(): shards[2, 0] = lax.ppermute(shards[-1, 0], 'row', line_pairs(1))]
    pallas_call x16 -> x18, Pallas kernels: 20.4 us -> 22.3 us  [run(): pl.pallas_call(kernel, out_shape=out_shapes, in_specs=specs, out_specs=[V...]
    ppermute x1, starting transfers between devices: 0.41 us -> 1.59 us  [local(): c_tables = [c_pattern, lax.ppermute(c_pattern, 'row', swap_y)]]
  transfers between devices with their start and end apart: 25 -> 25, of which waited for: 13 -> 13; matrix products, arithmetic and copies ran while one was open for 1% -> 1% of each run, Pallas kernels for 20% -> 21%
where the time goes in v4:
time: 95.4 us; the launch traced here: 95.3 us
  waiting for transfers between devices  45.5 us (48%)
  starting transfers between devices  26.7 us (28%)
  Pallas kernels  22.3 us (23%)
    pallas_call x18, Pallas kernels, run(): pl.pallas_call(kernel, out_shape=out_shapes, in_specs=specs, out_specs=[V...  22.3 us
    ppermute x3, waiting for transfers between devices, local(): lax.ppermute(a_panels[u * UNIT:(u + 1) * UNIT], 'row', swap_y)  12.6 us
    ppermute x1, waiting for transfers between devices, local(): shards[0, 1] = lax.ppermute(columns_half(1 - my_y), 'row', swap_y)  8.26 us
    ppermute x2, waiting for transfers between devices, local(): lax.ppermute(sums, 'row', [(r, r ^ bit) for r in range(n_row)])  8.06 us
    ppermute x1, waiting for transfers between devices, local(): far_last = lax.ppermute(shards[-1, 1][..., cut:], 'row', line_pairs(1))  5.82 us
    ppermute x2, starting transfers between devices, local(): shards[1, turn] = lax.ppermute(shards[0, turn], 'row', line_pairs(-1))  5.56 us
    ppermute x2, waiting for transfers between devices, local(): shards[-1, turn] = lax.ppermute(shards[0, turn], 'row', line_pairs(1))  4.14 us
    ppermute x3, starting transfers between devices, local(): lax.ppermute(a_panels[u * UNIT:(u + 1) * UNIT], 'row', swap_y)  3.54 us
  transfers between devices with their start and end apart: 25, of which 13 were waited for; matrix products, arithmetic and copies ran while one was open for 1% of the time, Pallas kernels for 21%

profile of v4, /device:TPU:0, one launch (start us, length us, event | category | flops | bytes accessed | tf_op | source)
XLA Modules:
  0.0 95.3 jit_solution(8047829396180583957)
XLA Ops:
  0.0 3.0 %collective-permute-start.1 = (f32[192,1,2,768]{3,2,1,0:T(2,128)}, f32[192,1,2,768]{3,2,1,0:T(2,128)S(1)}, u32[]{:S(2)}, u32[]{:S(2)}) collective-permute-start(f32[192,1,2,768]{3,2,1,0:T(2,128)} %refs_0_.1), channel_id=1, source_target_pairs={{0,2},{2,0},{1,3},{3,1},{4,6},{6,4},{5,7},{7,5},{8,10},{10,8},{9,1... | collective-permute-start | bytes 3538952 | tf_op jit(solution)/shard_map/ppermute | solution.py:296
  3.0 2.6 %collective-permute-start.11 = (f32[1,2,96,512]{3,2,1,0:T(8,128)S(1)}, f32[1,2,96,512]{3,2,1,0:T(8,128)}, u32[]{:S(2)}, u32[]{:S(2)}) collective-permute-start(f32[1,2,96,512]{3,2,1,0:T(8,128)S(1)} %constant_dynamic-slice_fusion.1.refs_0_), channel_id=1, source_target_pairs={{0,16},{4,20},{8,0},{12,4},{24,8},{28,12},{16,24},{20,28},{1,17},{... | collective-permute-start | bytes 1179656 | tf_op jit(solution)/shard_map/ppermute | solution.py:291
  5.7 1.5 %collective-permute-start.2 = (s32[3,1,2,6]{3,2,1,0:T(2,128)}, s32[3,1,2,6]{3,2,1,0:T(2,128)S(1)}, u32[]{:S(2)}, u32[]{:S(2)}) collective-permute-start(s32[3,1,2,6]{3,2,1,0:T(2,128)} %pattern.17), channel_id=1, source_target_pairs={{0,4},{4,0},{8,12},{12,8},{16,20},{20,16},{24,28},{28,24},{1,5},{5... | collective-permute-start | bytes 440 | tf_op jit(solution)/shard_map/ppermute | solution.py:303
  9.5 1.5 %collective-permute-start.3 = (f32[64,1,2,768]{3,2,1,0:T(2,128)S(1)}, f32[64,1,2,768]{3,2,1,0:T(2,128)S(1)}, u32[]{:S(2)}, u32[]{:S(2)}) collective-permute-start(f32[64,1,2,768]{3,2,1,0:T(2,128)S(1)} %get-tuple-element.186), channel_id=1, source_target_pairs={{0,4},{4,0},{8,12},{12,8},{16,20},{20,16},{24,28},{28,24},{1,5},{5... | collective-permute-start | bytes 1179656 | tf_op jit(solution)/shard_map/ppermute | solution.py:298
  11.0 8.3 %collective-permute-done.9.refs_1_ = f32[1,2,96,512]{3,2,1,0:T(8,128)S(1)} collective-permute-done((f32[1,2,96,512]{3,2,1,0:T(8,128)S(1)}, f32[1,2,96,512]{3,2,1,0:T(8,128)S(1)}, u32[]{:S(2)}, u32[]{:S(2)}) %collective-permute-start.9) | collective-permute-done | bytes 393248 | tf_op jit(solution)/shard_map/ppermute | solution.py:288
  19.8 1.5 %collective-permute-start.5 = (f32[64,1,2,768]{3,2,1,0:T(2,128)S(1)}, f32[64,1,2,768]{3,2,1,0:T(2,128)S(1)}, u32[]{:S(2)}, u32[]{:S(2)}) collective-permute-start(f32[64,1,2,768]{3,2,1,0:T(2,128)S(1)} %get-tuple-element.185), channel_id=1, source_target_pairs={{0,4},{4,0},{8,12},{12,8},{16,20},{20,16},{24,28},{28,24},{1,5},{5... | collective-permute-start | bytes 1179656 | tf_op jit(solution)/shard_map/ppermute | solution.py:298
  21.3 2.8 %collective-permute-done.10.refs_2_ = f32[1,2,96,512]{3,2,1,0:T(8,128)} collective-permute-done((f32[1,2,96,512]{3,2,1,0:T(8,128)S(1)}, f32[1,2,96,512]{3,2,1,0:T(8,128)}, u32[]{:S(2)}, u32[]{:S(2)}) %collective-permute-start.10) | collective-permute-done | bytes 393248 | tf_op jit(solution)/shard_map/ppermute | solution.py:290
  24.8 2.9 %collective-permute-done.3.refs_0_ = f32[64,1,2,768]{3,2,1,0:T(2,128)S(1)} collective-permute-done((f32[64,1,2,768]{3,2,1,0:T(2,128)S(1)}, f32[64,1,2,768]{3,2,1,0:T(2,128)S(1)}, u32[]{:S(2)}, u32[]{:S(2)}) %collective-permute-start.3) | collective-permute-done | bytes 393248 | tf_op jit(solution)/shard_map/ppermute | solution.py:298
  27.7 2.9 %collective-permute-start.13 = (f32[1,2,96,512]{3,2,1,0:T(8,128)S(1)}, f32[1,2,96,512]{3,2,1,0:T(8,128)S(1)}, u32[]{:S(2)}, u32[]{:S(2)}) collective-permute-start(f32[1,2,96,512]{3,2,1,0:T(8,128)S(1)} %collective-permute-done.9.refs_1_), channel_id=1, source_target_pairs={{0,16},{4,20},{8,0},{12,4},{24,8},{28,12},{16,24},{20,28},{1,17},{... | collective-permute-start | bytes 1179656 | tf_op jit(solution)/shard_map/ppermute | solution.py:291
  31.8 4.3 %collective-permute-done.4.refs_0_ = f32[64,1,2,768]{3,2,1,0:T(2,128)S(1)} collective-permute-done((f32[64,1,2,768]{3,2,1,0:T(2,128)S(1)}, f32[64,1,2,768]{3,2,1,0:T(2,128)S(1)}, u32[]{:S(2)}, u32[]{:S(2)}) %collective-permute-start.4) | collective-permute-done | bytes 393248 | tf_op jit(solution)/shard_map/ppermute | solution.py:298
  37.3 5.4 %collective-permute-done.5.refs_0_ = f32[64,1,2,768]{3,2,1,0:T(2,128)S(1)} collective-permute-done((f32[64,1,2,768]{3,2,1,0:T(2,128)S(1)}, f32[64,1,2,768]{3,2,1,0:T(2,128)S(1)}, u32[]{:S(2)}, u32[]{:S(2)}) %collective-permute-start.5) | collective-permute-done | bytes 393248 | tf_op jit(solution)/shard_map/ppermute | solution.py:298
  43.1 1.4 %collective-permute-done.12.refs_0_ = f32[1,2,96,512]{3,2,1,0:T(8,128)S(1)} collective-permute-done((f32[1,2,96,512]{3,2,1,0:T(8,128)S(1)}, f32[1,2,96,512]{3,2,1,0:T(8,128)S(1)}, u32[]{:S(2)}, u32[]{:S(2)}) %collective-permute-start.12) | collective-permute-done | bytes 393248 | tf_op jit(solution)/shard_map/ppermute | solution.py:290
  44.8 2.5 %shard_map.46 = (bf16[192,768]{1,0:T(8,128)(2,1)S(1)}, bf16[192,768]{1,0:T(8,128)(2,1)S(1)}, bf16[192,384]{1,0:T(8,128)(2,1)S(1)}, bf16[192,384]{1,0:T(8,128)(2,...) custom-call(s32[3,1,2,6]{3,2,1,0:T(2,128)S(1)} %copy-done.2, ...), custom_call_target="tpu_custom_call" | custom-call | bytes 2359584 | tf_op jit(solution)/shard_map/pallas_call | solution.py:250
  52.7 3.0 %collective-permute-start.17 = (f32[1,2,96,384]{3,2,1,0:T(8,128)S(1)}, f32[1,2,96,384]{3,2,1,0:T(8,128)S(1)}, u32[]{:S(2)}, u32[]{:S(2)}) collective-permute-start(f32[1,2,96,384]{3,2,1,0:T(8,128)S(1)} %slice.26), channel_id=1, source_target_pairs={{0,8},{4,12},{8,24},{12,28},{24,16},{28,20},{16,0},{20,4},{1,9},{5... | collective-permute-start | bytes 884744 | tf_op jit(solution)/shard_map/ppermute | solution.py:293
  57.1 2.5 %shard_map.47 = (bf16[192,768]{1,0:T(8,128)(2,1)S(1)}, bf16[192,768]{1,0:T(8,128)(2,1)S(1)}, bf16[192,384]{1,0:T(8,128)(2,1)S(1)}, bf16[192,384]{1,0:T(8,128)(2,...) custom-call(s32[3,1,2,6]{3,2,1,0:T(2,128)S(1)} %copy-done.2, ...), custom_call_target="tpu_custom_call" | custom-call | bytes 2359584 | tf_op jit(solution)/shard_map/pallas_call | solution.py:250
  59.7 2.7 %shard_map.54.refs_16_ = f32[640,512]{1,0:T(8,128)S(1)} custom-call(bf16[192,768]{1,0:T(8,128)(2,1)S(1)} %get-tuple-element.101.refs_0_, bf16[192,768]{1,0:T(8,128)(2,1)S(1)} %get-tuple-element.102.refs_1_, bf16[64,768]{1,0:T(8,128)(2,1)S(1)} %get-tuple-element.103.refs_2_, bf16[64,768]{1,0:T(8,128)(2,1)S(1)} %get-tuple-element.104.refs_3_, ...), custom_call_target="tpu_custom_call" | custom-call | flops 2264924160 | bytes 6619136 | tf_op jit(solution)/shard_map/pallas_call | solution.py:250
  67.8 5.8 %collective-permute-done.15.refs_17_ = f32[1,2,96,128]{3,2,1,0:T(8,128)S(1)} collective-permute-done((f32[1,2,96,128]{3,2,1,0:T(8,128)S(1)}, f32[1,2,96,128]{3,2,1,0:T(8,128)S(1)}, u32[]{:S(2)}, u32[]{:S(2)}) %collective-permute-start.15) | collective-permute-done | bytes 98336 | tf_op jit(solution)/shard_map/ppermute | solution.py:294
  74.2 1.6 %collective-permute-start = (s32[3,8]{1,0:T(4,128)S(1)}, s32[3,8]{1,0:T(4,128)S(1)}, u32[]{:S(2)}, u32[]{:S(2)}) collective-permute-start(s32[3,8]{1,0:T(4,128)S(1)} %copy-done.3), channel_id=1, source_target_pairs={{0,4},{4,0},{8,12},{12,8},{16,20},{20,16},{24,28},{28,24},{1,5},{5... | collective-permute-start | bytes 296 | tf_op jit(solution)/shard_map/ppermute | solution.py:304
  75.8 2.1 %collective-permute-done.other_pattern = s32[3,8]{1,0:T(4,128)S(1)} collective-permute-done((s32[3,8]{1,0:T(4,128)S(1)}, s32[3,8]{1,0:T(4,128)S(1)}, u32[]{:S(2)}, u32[]{:S(2)}) %collective-permute-start) | collective-permute-done | bytes 128 | tf_op jit(solution)/shard_map/ppermute | solution.py:304
  78.6 1.6 %collective-permute-start.23 = (f32[192,384]{1,0:T(8,128)S(1)}, f32[192,384]{1,0:T(8,128)S(1)}, u32[]{:S(2)}, u32[]{:S(2)}) collective-permute-start(f32[192,384]{1,0:T(8,128)S(1)} %get-tuple-element.183), channel_id=1, source_target_pairs={{0,4},{4,0},{8,12},{12,8},{16,20},{20,16},{24,28},{28,24},{1,5},{5... | collective-permute-start | bytes 884744 | tf_op jit(solution)/shard_map/ppermute | solution.py:391
  82.6 3.6 %collective-permute-done.20 = f32[1,512]{1,0:T(1,128)S(1)} collective-permute-done((f32[1,512]{1,0:T(1,128)S(1)}, f32[1,512]{1,0:T(1,128)S(1)}, u32[]{:S(2)}, u32[]{:S(2)}) %collective-permute-start.20) | collective-permute-done | bytes 2080 | tf_op jit(solution)/shard_map/ppermute | solution.py:400
  86.2 4.5 %collective-permute-done.21 = f32[1,512]{1,0:T(1,128)S(1)} collective-permute-done((f32[1,512]{1,0:T(1,128)S(1)}, f32[1,512]{1,0:T(1,128)S(1)}, u32[]{:S(2)}, u32[]{:S(2)}) %collective-permute-start.21) | collective-permute-done | bytes 2080 | tf_op jit(solution)/shard_map/ppermute | solution.py:400
  90.7 1.5 %collective-permute-start.22 = (f32[1,512]{1,0:T(1,128)S(1)}, f32[1,512]{1,0:T(1,128)S(1)}, u32[]{:S(2)}, u32[]{:S(2)}) collective-permute-start(f32[1,512]{1,0:T(1,128)S(1)} %add.11.sums), channel_id=1, source_target_pairs={{0,4},{4,0},{8,12},{12,8},{16,20},{20,16},{24,28},{28,24},{1,5},{5... | collective-permute-start | bytes 6152 | tf_op jit(solution)/shard_map/ppermute | solution.py:401
  92.2 2.1 %collective-permute-done.22.other_sums = f32[1,512]{1,0:T(1,128)S(1)} collective-permute-done((f32[1,512]{1,0:T(1,128)S(1)}, f32[1,512]{1,0:T(1,128)S(1)}, u32[]{:S(2)}, u32[]{:S(2)}) %collective-permute-start.22) | collective-permute-done | bytes 2080 | tf_op jit(solution)/shard_map/ppermute | solution.py:401
  (61 shorter events, 23.5 us)
Async XLA Ops:
  0.0 30.6 %collective-permute-start.1 = (f32[192,1,2,768]{3,2,1,0:T(2,128)}, f32[192,1,2,768]{3,2,1,0:T(2,128)S(1)}, u32[]{:S(2)}, u32[]{:S(2)}) collective-permute-start(f32[192,1,2,768]{3,2,1,0:T(2,128)} %refs_0_.1), channel_id=1, source_target_pairs={{0,2},{2,0},{1,3},{3,1},{4,6},{6,4},{5,7},{7,5},{8,10},{10,8},{9,1... | collective-permute-start | bytes 3538952 | tf_op jit(solution)/shard_map/ppermute | solution.py:296
  3.0 16.8 %collective-permute-start.11 = (f32[1,2,96,512]{3,2,1,0:T(8,128)S(1)}, f32[1,2,96,512]{3,2,1,0:T(8,128)}, u32[]{:S(2)}, u32[]{:S(2)}) collective-permute-start(f32[1,2,96,512]{3,2,1,0:T(8,128)S(1)} %constant_dynamic-slice_fusion.1.refs_0_), channel_id=1, source_target_pairs={{0,16},{4,20},{8,0},{12,4},{24,8},{28,12},{16,24},{20,28},{1,17},{... | collective-permute-start | bytes 1179656 | tf_op jit(solution)/shard_map/ppermute | solution.py:291
  5.7 18.4 %collective-permute-start.10 = (f32[1,2,96,512]{3,2,1,0:T(8,128)S(1)}, f32[1,2,96,512]{3,2,1,0:T(8,128)}, u32[]{:S(2)}, u32[]{:S(2)}) collective-permute-start(f32[1,2,96,512]{3,2,1,0:T(8,128)S(1)} %constant_dynamic-slice_fusion.1.refs_0_), channel_id=1, source_target_pairs={{0,8},{4,12},{8,24},{12,28},{24,16},{28,20},{16,0},{20,4},{1,9},{5... | collective-permute-start | bytes 1179656 | tf_op jit(solution)/shard_map/ppermute | solution.py:290
  5.7 3.8 %collective-permute-start.2 = (s32[3,1,2,6]{3,2,1,0:T(2,128)}, s32[3,1,2,6]{3,2,1,0:T(2,128)S(1)}, u32[]{:S(2)}, u32[]{:S(2)}) collective-permute-start(s32[3,1,2,6]{3,2,1,0:T(2,128)} %pattern.17), channel_id=1, source_target_pairs={{0,4},{4,0},{8,12},{12,8},{16,20},{20,16},{24,28},{28,24},{1,5},{5... | collective-permute-start | bytes 440 | tf_op jit(solution)/shard_map/ppermute | solution.py:303
  7.2 12.1 %collective-permute-start.9 = (f32[1,2,96,512]{3,2,1,0:T(8,128)S(1)}, f32[1,2,96,512]{3,2,1,0:T(8,128)S(1)}, u32[]{:S(2)}, u32[]{:S(2)}) collective-permute-start(f32[1,2,96,512]{3,2,1,0:T(8,128)S(1)} %constant_dynamic-slice_fusion), channel_id=1, source_target_pairs={{0,4},{4,0},{8,12},{12,8},{16,20},{20,16},{24,28},{28,24},{1,5},{5... | collective-permute-start | bytes 1179656 | tf_op jit(solution)/shard_map/ppermute | solution.py:288
  9.5 18.2 %collective-permute-start.3 = (f32[64,1,2,768]{3,2,1,0:T(2,128)S(1)}, f32[64,1,2,768]{3,2,1,0:T(2,128)S(1)}, u32[]{:S(2)}, u32[]{:S(2)}) collective-permute-start(f32[64,1,2,768]{3,2,1,0:T(2,128)S(1)} %get-tuple-element.186), channel_id=1, source_target_pairs={{0,4},{4,0},{8,12},{12,8},{16,20},{20,16},{24,28},{28,24},{1,5},{5... | collective-permute-start | bytes 1179656 | tf_op jit(solution)/shard_map/ppermute | solution.py:298
  19.3 16.9 %collective-permute-start.4 = (f32[64,1,2,768]{3,2,1,0:T(2,128)S(1)}, f32[64,1,2,768]{3,2,1,0:T(2,128)S(1)}, u32[]{:S(2)}, u32[]{:S(2)}) collective-permute-start(f32[64,1,2,768]{3,2,1,0:T(2,128)S(1)} %get-tuple-element.187), channel_id=1, source_target_pairs={{0,4},{4,0},{8,12},{12,8},{16,20},{20,16},{24,28},{28,24},{1,5},{5... | collective-permute-start | bytes 1179656 | tf_op jit(solution)/shard_map/ppermute | solution.py:298
  19.8 22.8 %collective-permute-start.5 = (f32[64,1,2,768]{3,2,1,0:T(2,128)S(1)}, f32[64,1,2,768]{3,2,1,0:T(2,128)S(1)}, u32[]{:S(2)}, u32[]{:S(2)}) collective-permute-start(f32[64,1,2,768]{3,2,1,0:T(2,128)S(1)} %get-tuple-element.185), channel_id=1, source_target_pairs={{0,4},{4,0},{8,12},{12,8},{16,20},{20,16},{24,28},{28,24},{1,5},{5... | collective-permute-start | bytes 1179656 | tf_op jit(solution)/shard_map/ppermute | solution.py:298
  24.1 20.4 %collective-permute-start.12 = (f32[1,2,96,512]{3,2,1,0:T(8,128)S(1)}, f32[1,2,96,512]{3,2,1,0:T(8,128)S(1)}, u32[]{:S(2)}, u32[]{:S(2)}) collective-permute-start(f32[1,2,96,512]{3,2,1,0:T(8,128)S(1)} %collective-permute-done.9.refs_1_), channel_id=1, source_target_pairs={{0,8},{4,12},{8,24},{12,28},{24,16},{28,20},{16,0},{20,4},{1,9},{5... | collective-permute-start | bytes 1179656 | tf_op jit(solution)/shard_map/ppermute | solution.py:290
  27.7 25.0 %collective-permute-start.13 = (f32[1,2,96,512]{3,2,1,0:T(8,128)S(1)}, f32[1,2,96,512]{3,2,1,0:T(8,128)S(1)}, u32[]{:S(2)}, u32[]{:S(2)}) collective-permute-start(f32[1,2,96,512]{3,2,1,0:T(8,128)S(1)} %collective-permute-done.9.refs_1_), channel_id=1, source_target_pairs={{0,16},{4,20},{8,0},{12,4},{24,8},{28,12},{16,24},{20,28},{1,17},{... | collective-permute-start | bytes 1179656 | tf_op jit(solution)/shard_map/ppermute | solution.py:291
  30.6 25.2 %collective-permute-start.6 = (f32[64,1,2,768]{3,2,1,0:T(2,128)S(1)}, f32[64,1,2,768]{3,2,1,0:T(2,128)S(1)}, u32[]{:S(2)}, u32[]{:S(2)}) collective-permute-start(f32[64,1,2,768]{3,2,1,0:T(2,128)S(1)} %collective-permute-done.3.refs_0_), channel_id=1, source_target_pairs={{0,2},{2,0},{1,3},{3,1},{4,6},{6,4},{5,7},{7,5},{8,10},{10,8},{9,1... | collective-permute-start | bytes 1179656 | tf_op jit(solution)/shard_map/ppermute | solution.py:301
  36.1 26.2 %collective-permute-start.8 = (f32[64,1,2,768]{3,2,1,0:T(2,128)S(1)}, f32[64,1,2,768]{3,2,1,0:T(2,128)S(1)}, u32[]{:S(2)}, u32[]{:S(2)}) collective-permute-start(f32[64,1,2,768]{3,2,1,0:T(2,128)S(1)} %collective-permute-done.4.refs_0_), channel_id=1, source_target_pairs={{0,2},{2,0},{1,3},{3,1},{4,6},{6,4},{5,7},{7,5},{8,10},{10,8},{9,1... | collective-permute-start | bytes 1179656 | tf_op jit(solution)/shard_map/ppermute | solution.py:302
  42.6 19.8 %collective-permute-start.7 = (f32[64,1,2,768]{3,2,1,0:T(2,128)S(1)}, f32[64,1,2,768]{3,2,1,0:T(2,128)S(1)}, u32[]{:S(2)}, u32[]{:S(2)}) collective-permute-start(f32[64,1,2,768]{3,2,1,0:T(2,128)S(1)} %slice.24), channel_id=1, source_target_pairs={{0,4},{4,0},{8,12},{12,8},{16,20},{20,16},{24,28},{28,24},{1,5},{5... | collective-permute-start | bytes 1179656 | tf_op jit(solution)/shard_map/ppermute | solution.py:300
  44.5 21.2 %collective-permute-start.14 = (f32[1,2,96,512]{3,2,1,0:T(8,128)}, f32[1,2,96,512]{3,2,1,0:T(8,128)S(1)}, u32[]{:S(2)}, u32[]{:S(2)}) collective-permute-start(f32[1,2,96,512]{3,2,1,0:T(8,128)} %collective-permute-done.10.refs_2_), channel_id=1, source_target_pairs={{0,8},{4,12},{8,24},{12,28},{24,16},{28,20},{16,0},{20,4},{1,9},{5... | collective-permute-start | bytes 1179656 | tf_op jit(solution)/shard_map/ppermute | solution.py:292
  52.7 13.8 %collective-permute-start.17 = (f32[1,2,96,384]{3,2,1,0:T(8,128)S(1)}, f32[1,2,96,384]{3,2,1,0:T(8,128)S(1)}, u32[]{:S(2)}, u32[]{:S(2)}) collective-permute-start(f32[1,2,96,384]{3,2,1,0:T(8,128)S(1)} %slice.26), channel_id=1, source_target_pairs={{0,8},{4,12},{8,24},{12,28},{24,16},{28,20},{16,0},{20,4},{1,9},{5... | collective-permute-start | bytes 884744 | tf_op jit(solution)/shard_map/ppermute | solution.py:293
  67.4 10.5 %collective-permute-start.18 = (f32[2,192,384]{2,1,0:T(8,128)S(1)}, f32[2,192,384]{2,1,0:T(8,128)S(1)}, u32[]{:S(2)}, u32[]{:S(2)}) collective-permute-start(f32[2,192,384]{2,1,0:T(8,128)S(1)} %get-tuple-element.178), channel_id=1, source_target_pairs={{0,1},{1,0},{2,3},{3,2},{4,5},{5,4},{6,7},{7,6},{8,9},{9,8},{10,11... | collective-permute-start | bytes 1769480 | tf_op jit(solution)/shard_map/ppermute | solution.py:383
  67.5 6.1 %collective-permute-start.15 = (f32[1,2,96,128]{3,2,1,0:T(8,128)S(1)}, f32[1,2,96,128]{3,2,1,0:T(8,128)S(1)}, u32[]{:S(2)}, u32[]{:S(2)}) collective-permute-start(f32[1,2,96,128]{3,2,1,0:T(8,128)S(1)} %slice.25), channel_id=1, source_target_pairs={{0,8},{4,12},{8,24},{12,28},{24,16},{28,20},{16,0},{20,4},{1,9},{5... | collective-permute-start | bytes 294920 | tf_op jit(solution)/shard_map/ppermute | solution.py:294
  74.1 7.2 %collective-permute-start.16 = (f32[4,192,128]{2,1,0:T(8,128)S(1)}, f32[4,192,128]{2,1,0:T(8,128)S(1)}, u32[]{:S(2)}, u32[]{:S(2)}) collective-permute-start(f32[4,192,128]{2,1,0:T(8,128)S(1)} %shard_map.59.mine), channel_id=1, source_target_pairs={{0,1},{1,0},{2,3},{3,2},{4,5},{5,4},{6,7},{7,6},{8,9},{9,8},{10,11... | collective-permute-start | bytes 1179656 | tf_op jit(solution)/shard_map/ppermute | solution.py:385
  74.2 3.7 %collective-permute-start = (s32[3,8]{1,0:T(4,128)S(1)}, s32[3,8]{1,0:T(4,128)S(1)}, u32[]{:S(2)}, u32[]{:S(2)}) collective-permute-start(s32[3,8]{1,0:T(4,128)S(1)} %copy-done.3), channel_id=1, source_target_pairs={{0,4},{4,0},{8,12},{12,8},{16,20},{20,16},{24,28},{28,24},{1,5},{5... | collective-permute-start | bytes 296 | tf_op jit(solution)/shard_map/ppermute | solution.py:304
  78.6 15.7 %collective-permute-start.23 = (f32[192,384]{1,0:T(8,128)S(1)}, f32[192,384]{1,0:T(8,128)S(1)}, u32[]{:S(2)}, u32[]{:S(2)}) collective-permute-start(f32[192,384]{1,0:T(8,128)S(1)} %get-tuple-element.183), channel_id=1, source_target_pairs={{0,4},{4,0},{8,12},{12,8},{16,20},{20,16},{24,28},{28,24},{1,5},{5... | collective-permute-start | bytes 884744 | tf_op jit(solution)/shard_map/ppermute | solution.py:391
  82.0 12.2 %collective-permute-start.24 = (f32[192,128]{1,0:T(8,128)S(1)}, f32[192,128]{1,0:T(8,128)S(1)}, u32[]{:S(2)}, u32[]{:S(2)}) collective-permute-start(f32[192,128]{1,0:T(8,128)S(1)} %get-tuple-element.184), channel_id=1, source_target_pairs={{0,4},{4,0},{8,12},{12,8},{16,20},{20,16},{24,28},{28,24},{1,5},{5... | collective-permute-start | bytes 294920 | tf_op jit(solution)/shard_map/ppermute | solution.py:398
  82.6 3.6 %collective-permute-start.20 = (f32[1,512]{1,0:T(1,128)S(1)}, f32[1,512]{1,0:T(1,128)S(1)}, u32[]{:S(2)}, u32[]{:S(2)}) collective-permute-start(f32[1,512]{1,0:T(1,128)S(1)} %get-tuple-element.180), channel_id=1, source_target_pairs={{0,8},{4,12},{8,0},{12,4},{16,24},{20,28},{24,16},{28,20},{1,9},{5... | collective-permute-start | bytes 6152 | tf_op jit(solution)/shard_map/ppermute | solution.py:400
  86.2 4.5 %collective-permute-start.21 = (f32[1,512]{1,0:T(1,128)S(1)}, f32[1,512]{1,0:T(1,128)S(1)}, u32[]{:S(2)}, u32[]{:S(2)}) collective-permute-start(f32[1,512]{1,0:T(1,128)S(1)} %add.10), channel_id=1, source_target_pairs={{0,16},{4,20},{8,24},{12,28},{16,0},{20,4},{24,8},{28,12},{1,17},{... | collective-permute-start | bytes 6152 | tf_op jit(solution)/shard_map/ppermute | solution.py:400
  90.7 3.6 %collective-permute-start.22 = (f32[1,512]{1,0:T(1,128)S(1)}, f32[1,512]{1,0:T(1,128)S(1)}, u32[]{:S(2)}, u32[]{:S(2)}) collective-permute-start(f32[1,512]{1,0:T(1,128)S(1)} %add.11.sums), channel_id=1, source_target_pairs={{0,4},{4,0},{8,12},{12,8},{16,20},{20,16},{24,28},{28,24},{1,5},{5... | collective-permute-start | bytes 6152 | tf_op jit(solution)/shard_map/ppermute | solution.py:401
  (5 other events, 56.2 us)

commit v5 on v4

--- a/solution.py
+++ b/solution.py
@@ -348,12 +348,10 @@
         )(*lefts, *rights)
         return total
 
-    early_sets += [left((y2, 1, False, 2 * UNIT)), left((d0, 1, True, 0))]
+    early_sets.append(left((y2, 1, False, 2 * UNIT), (d0, 1, True, 0)))
     near = product(early_sets)
     d2, d1, near = together(d2, d1, near)
-    late_sets = [left((d1, 1, True, UNIT))]
-    d2, late_sets[0] = together(d2, late_sets[0])
-    late_sets.append(left((d2, 1, True, 2 * UNIT)))
+    late_sets = [left((d1, 1, True, UNIT), (d2, 1, True, 2 * UNIT))]
     near_late = product(late_sets)
 
     all_sets = [*early_sets, *late_sets]

time: 95.4 us -> 90.4 us (0.948)
  waiting for transfers between devices: 45.5 us -> 42.6 us
  Pallas kernels: 22.3 us -> 20.9 us
    ppermute x3, waiting for transfers between devices: 12.6 us -> 6.68 us  [local(): lax.ppermute(a_panels[u * UNIT:(u + 1) * UNIT], 'row', swap_y)]
    ppermute x2, waiting for transfers between devices: 4.14 us -> 5.93 us  [local(): shards[-1, turn] = lax.ppermute(shards[0, turn], 'row', line_pairs(1))]
    pallas_call x18 -> x16, Pallas kernels: 22.3 us -> 20.9 us  [run(): pl.pallas_call(kernel, out_shape=out_shapes, in_specs=specs, out_specs=[V...]
    ppermute x3, starting transfers between devices: 3.54 us -> 2.53 us  [local(): lax.ppermute(a_panels[u * UNIT:(u + 1) * UNIT], 'row', swap_y)]
    ppermute x1, waiting for transfers between devices: 0.01 us -> 0.97 us  [local(): from_x = lax.ppermute(a_panels, 'col', swap)]
where the time goes in v5:
time: 90.4 us; the launch traced here: 90.2 us
  waiting for transfers between devices  42.6 us (47%)
  starting transfers between devices  25.9 us (29%)
  Pallas kernels  20.9 us (23%)
    pallas_call x16, Pallas kernels, run(): pl.pallas_call(kernel, out_shape=out_shapes, in_specs=specs, out_specs=[V...  20.9 us
    ppermute x1, waiting for transfers between devices, local(): shards[0, 1] = lax.ppermute(columns_half(1 - my_y), 'row', swap_y)  8.26 us
    ppermute x2, waiting for transfers between devices, local(): lax.ppermute(sums, 'row', [(r, r ^ bit) for r in range(n_row)])  8.06 us
    ppermute x3, waiting for transfers between devices, local(): lax.ppermute(a_panels[u * UNIT:(u + 1) * UNIT], 'row', swap_y)  6.68 us
    ppermute x1, waiting for transfers between devices, local(): far_last = lax.ppermute(shards[-1, 1][..., cut:], 'row', line_pairs(1))  6.07 us
    ppermute x2, waiting for transfers between devices, local(): shards[-1, turn] = lax.ppermute(shards[0, turn], 'row', line_pairs(1))  5.93 us
    ppermute x2, starting transfers between devices, local(): shards[1, turn] = lax.ppermute(shards[0, turn], 'row', line_pairs(-1))  5.56 us
    ppermute x1, starting transfers between devices, local(): from_x = lax.ppermute(a_panels, 'col', swap)  2.97 us
  transfers between devices with their start and end apart: 25, of which 13 were waited for; matrix products, arithmetic and copies ran while one was open for 1% of the time, Pallas kernels for 21%

profile of v5, /device:TPU:0, one launch (start us, length us, event | category | flops | bytes accessed | tf_op | source)
XLA Modules:
  0.0 90.2 jit_solution(16695160197800609833)
XLA Ops:
  0.0 3.0 %collective-permute-start.1 = (f32[192,1,2,768]{3,2,1,0:T(2,128)}, f32[192,1,2,768]{3,2,1,0:T(2,128)S(1)}, u32[]{:S(2)}, u32[]{:S(2)}) collective-permute-start(f32[192,1,2,768]{3,2,1,0:T(2,128)} %refs_0_.1), channel_id=1, source_target_pairs={{0,2},{2,0},{1,3},{3,1},{4,6},{6,4},{5,7},{7,5},{8,10},{10,8},{9,1... | collective-permute-start | bytes 3538952 | tf_op jit(solution)/shard_map/ppermute | solution.py:296
  3.0 2.6 %collective-permute-start.11 = (f32[1,2,96,512]{3,2,1,0:T(8,128)S(1)}, f32[1,2,96,512]{3,2,1,0:T(8,128)}, u32[]{:S(2)}, u32[]{:S(2)}) collective-permute-start(f32[1,2,96,512]{3,2,1,0:T(8,128)S(1)} %constant_dynamic-slice_fusion.1.refs_0_), channel_id=1, source_target_pairs={{0,16},{4,20},{8,0},{12,4},{24,8},{28,12},{16,24},{20,28},{1,17},{... | collective-permute-start | bytes 1179656 | tf_op jit(solution)/shard_map/ppermute | solution.py:291
  5.7 1.5 %collective-permute-start.2 = (s32[3,1,2,6]{3,2,1,0:T(2,128)}, s32[3,1,2,6]{3,2,1,0:T(2,128)S(1)}, u32[]{:S(2)}, u32[]{:S(2)}) collective-permute-start(s32[3,1,2,6]{3,2,1,0:T(2,128)} %pattern.13), channel_id=1, source_target_pairs={{0,4},{4,0},{8,12},{12,8},{16,20},{20,16},{24,28},{28,24},{1,5},{5... | collective-permute-start | bytes 440 | tf_op jit(solution)/shard_map/ppermute | solution.py:303
  9.5 1.5 %collective-permute-start.3 = (f32[64,1,2,768]{3,2,1,0:T(2,128)S(1)}, f32[64,1,2,768]{3,2,1,0:T(2,128)S(1)}, u32[]{:S(2)}, u32[]{:S(2)}) collective-permute-start(f32[64,1,2,768]{3,2,1,0:T(2,128)S(1)} %get-tuple-element.136), channel_id=1, source_target_pairs={{0,4},{4,0},{8,12},{12,8},{16,20},{20,16},{24,28},{28,24},{1,5},{5... | collective-permute-start | bytes 1179656 | tf_op jit(solution)/shard_map/ppermute | solution.py:298
  11.0 8.3 %collective-permute-done.9.refs_1_ = f32[1,2,96,512]{3,2,1,0:T(8,128)S(1)} collective-permute-done((f32[1,2,96,512]{3,2,1,0:T(8,128)S(1)}, f32[1,2,96,512]{3,2,1,0:T(8,128)S(1)}, u32[]{:S(2)}, u32[]{:S(2)}) %collective-permute-start.9) | collective-permute-done | bytes 393248 | tf_op jit(solution)/shard_map/ppermute | solution.py:288
  19.8 2.9 %collective-permute-start.13 = (f32[1,2,96,512]{3,2,1,0:T(8,128)S(1)}, f32[1,2,96,512]{3,2,1,0:T(8,128)S(1)}, u32[]{:S(2)}, u32[]{:S(2)}) collective-permute-start(f32[1,2,96,512]{3,2,1,0:T(8,128)S(1)} %collective-permute-done.9.refs_1_), channel_id=1, source_target_pairs={{0,16},{4,20},{8,0},{12,4},{24,8},{28,12},{16,24},{20,28},{1,17},{... | collective-permute-start | bytes 1179656 | tf_op jit(solution)/shard_map/ppermute | solution.py:291
  22.7 2.8 %collective-permute-done.10.refs_2_ = f32[1,2,96,512]{3,2,1,0:T(8,128)} collective-permute-done((f32[1,2,96,512]{3,2,1,0:T(8,128)S(1)}, f32[1,2,96,512]{3,2,1,0:T(8,128)}, u32[]{:S(2)}, u32[]{:S(2)}) %collective-permute-start.10) | collective-permute-done | bytes 393248 | tf_op jit(solution)/shard_map/ppermute | solution.py:290
  29.2 1.7 %collective-permute-start.6 = (f32[64,1,2,768]{3,2,1,0:T(2,128)S(1)}, f32[64,1,2,768]{3,2,1,0:T(2,128)S(1)}, u32[]{:S(2)}, u32[]{:S(2)}) collective-permute-start(f32[64,1,2,768]{3,2,1,0:T(2,128)S(1)} %collective-permute-done.3.refs_0_), channel_id=1, source_target_pairs={{0,2},{2,0},{1,3},{3,1},{4,6},{6,4},{5,7},{7,5},{8,10},{10,8},{9,1... | collective-permute-start | bytes 1179656 | tf_op jit(solution)/shard_map/ppermute | solution.py:301
  30.9 5.2 %collective-permute-done.4.refs_0_ = f32[64,1,2,768]{3,2,1,0:T(2,128)S(1)} collective-permute-done((f32[64,1,2,768]{3,2,1,0:T(2,128)S(1)}, f32[64,1,2,768]{3,2,1,0:T(2,128)S(1)}, u32[]{:S(2)}, u32[]{:S(2)}) %collective-permute-start.4) | collective-permute-done | bytes 393248 | tf_op jit(solution)/shard_map/ppermute | solution.py:298
  37.8 3.1 %collective-permute-done.12.refs_0_ = f32[1,2,96,512]{3,2,1,0:T(8,128)S(1)} collective-permute-done((f32[1,2,96,512]{3,2,1,0:T(8,128)S(1)}, f32[1,2,96,512]{3,2,1,0:T(8,128)S(1)}, u32[]{:S(2)}, u32[]{:S(2)}) %collective-permute-start.12) | collective-permute-done | bytes 393248 | tf_op jit(solution)/shard_map/ppermute | solution.py:290
  41.6 2.5 %shard_map.46 = (bf16[192,768]{1,0:T(8,128)(2,1)S(1)}, bf16[192,768]{1,0:T(8,128)(2,1)S(1)}, bf16[192,384]{1,0:T(8,128)(2,1)S(1)}, bf16[192,384]{1,0:T(8,128)(2,...) custom-call(s32[3,1,2,6]{3,2,1,0:T(2,128)S(1)} %copy-done.2, ...), custom_call_target="tpu_custom_call" | custom-call | bytes 2359584 | tf_op jit(solution)/shard_map/pallas_call | solution.py:250
  48.3 2.6 %collective-permute-start.17 = (f32[1,2,96,384]{3,2,1,0:T(8,128)S(1)}, f32[1,2,96,384]{3,2,1,0:T(8,128)S(1)}, u32[]{:S(2)}, u32[]{:S(2)}) collective-permute-start(f32[1,2,96,384]{3,2,1,0:T(8,128)S(1)} %slice.26), channel_id=1, source_target_pairs={{0,8},{4,12},{8,24},{12,28},{24,16},{28,20},{16,0},{20,4},{1,9},{5... | collective-permute-start | bytes 884744 | tf_op jit(solution)/shard_map/ppermute | solution.py:293
  50.8 1.9 %shard_map.50 = (bf16[128,768]{1,0:T(8,128)(2,1)S(1)}, bf16[128,768]{1,0:T(8,128)(2,1)S(1)}, bf16[128,384]{1,0:T(8,128)(2,1)S(1)}, bf16[128,384]{1,0:T(8,128)(2,...) custom-call(s32[3,1,2,6]{3,2,1,0:T(2,128)S(1)} %copy-done.2, ...), custom_call_target="tpu_custom_call" | custom-call | bytes 1573152 | tf_op jit(solution)/shard_map/pallas_call | solution.py:250
  52.8 2.5 %shard_map.47 = (bf16[192,768]{1,0:T(8,128)(2,1)S(1)}, bf16[192,768]{1,0:T(8,128)(2,1)S(1)}, bf16[192,384]{1,0:T(8,128)(2,1)S(1)}, bf16[192,384]{1,0:T(8,128)(2,...) custom-call(s32[3,1,2,6]{3,2,1,0:T(2,128)S(1)} %copy-done.2, ...), custom_call_target="tpu_custom_call" | custom-call | bytes 2359584 | tf_op jit(solution)/shard_map/pallas_call | solution.py:250
  55.3 2.7 %shard_map.53.refs_12_ = f32[640,512]{1,0:T(8,128)S(1)} custom-call(bf16[192,768]{1,0:T(8,128)(2,1)S(1)} %get-tuple-element.75.refs_0_, bf16[192,768]{1,0:T(8,128)(2,1)S(1)} %get-tuple-element.76.refs_1_, bf16[64,768]{1,0:T(8,128)(2,1)S(1)} %get-tuple-element.77.refs_2_, bf16[64,768]{1,0:T(8,128)(2,1)S(1)} %get-tuple-element.78.refs_3_, ...), custom_call_target="tpu_custom_call" | custom-call | flops 2264924160 | bytes 6619136 | tf_op jit(solution)/shard_map/pallas_call | solution.py:250
  58.0 1.9 %shard_map.54 = (bf16[128,768]{1,0:T(8,128)(2,1)S(1)}, bf16[128,768]{1,0:T(8,128)(2,1)S(1)}, bf16[128,384]{1,0:T(8,128)(2,1)S(1)}, bf16[128,384]{1,0:T(8,128)(2,...) custom-call(s32[3,1,2,6]{3,2,1,0:T(2,128)S(1)} %copy-done.2, ...), custom_call_target="tpu_custom_call" | custom-call | bytes 1573152 | tf_op jit(solution)/shard_map/pallas_call | solution.py:250
  62.5 6.1 %collective-permute-done.15.refs_13_ = f32[1,2,96,128]{3,2,1,0:T(8,128)S(1)} collective-permute-done((f32[1,2,96,128]{3,2,1,0:T(8,128)S(1)}, f32[1,2,96,128]{3,2,1,0:T(8,128)S(1)}, u32[]{:S(2)}, u32[]{:S(2)}) %collective-permute-start.15) | collective-permute-done | bytes 98336 | tf_op jit(solution)/shard_map/ppermute | solution.py:294
  69.2 1.6 %collective-permute-start = (s32[3,8]{1,0:T(4,128)S(1)}, s32[3,8]{1,0:T(4,128)S(1)}, u32[]{:S(2)}, u32[]{:S(2)}) collective-permute-start(s32[3,8]{1,0:T(4,128)S(1)} %copy-done.3), channel_id=1, source_target_pairs={{0,4},{4,0},{8,12},{12,8},{16,20},{20,16},{24,28},{28,24},{1,5},{5... | collective-permute-start | bytes 296 | tf_op jit(solution)/shard_map/ppermute | solution.py:304
  70.7 2.1 %collective-permute-done.other_pattern = s32[3,8]{1,0:T(4,128)S(1)} collective-permute-done((s32[3,8]{1,0:T(4,128)S(1)}, s32[3,8]{1,0:T(4,128)S(1)}, u32[]{:S(2)}, u32[]{:S(2)}) %collective-permute-start) | collective-permute-done | bytes 128 | tf_op jit(solution)/shard_map/ppermute | solution.py:304
  73.5 1.6 %collective-permute-start.23 = (f32[192,384]{1,0:T(8,128)S(1)}, f32[192,384]{1,0:T(8,128)S(1)}, u32[]{:S(2)}, u32[]{:S(2)}) collective-permute-start(f32[192,384]{1,0:T(8,128)S(1)} %get-tuple-element.133), channel_id=1, source_target_pairs={{0,4},{4,0},{8,12},{12,8},{16,20},{20,16},{24,28},{28,24},{1,5},{5... | collective-permute-start | bytes 884744 | tf_op jit(solution)/shard_map/ppermute | solution.py:389
  77.6 3.6 %collective-permute-done.20 = f32[1,512]{1,0:T(1,128)S(1)} collective-permute-done((f32[1,512]{1,0:T(1,128)S(1)}, f32[1,512]{1,0:T(1,128)S(1)}, u32[]{:S(2)}, u32[]{:S(2)}) %collective-permute-start.20) | collective-permute-done | bytes 2080 | tf_op jit(solution)/shard_map/ppermute | solution.py:398
  81.1 4.5 %collective-permute-done.21 = f32[1,512]{1,0:T(1,128)S(1)} collective-permute-done((f32[1,512]{1,0:T(1,128)S(1)}, f32[1,512]{1,0:T(1,128)S(1)}, u32[]{:S(2)}, u32[]{:S(2)}) %collective-permute-start.21) | collective-permute-done | bytes 2080 | tf_op jit(solution)/shard_map/ppermute | solution.py:398
  85.6 1.5 %collective-permute-start.22 = (f32[1,512]{1,0:T(1,128)S(1)}, f32[1,512]{1,0:T(1,128)S(1)}, u32[]{:S(2)}, u32[]{:S(2)}) collective-permute-start(f32[1,512]{1,0:T(1,128)S(1)} %add.11.sums), channel_id=1, source_target_pairs={{0,4},{4,0},{8,12},{12,8},{16,20},{20,16},{24,28},{28,24},{1,5},{5... | collective-permute-start | bytes 6152 | tf_op jit(solution)/shard_map/ppermute | solution.py:399
  87.1 2.1 %collective-permute-done.22.other_sums = f32[1,512]{1,0:T(1,128)S(1)} collective-permute-done((f32[1,512]{1,0:T(1,128)S(1)}, f32[1,512]{1,0:T(1,128)S(1)}, u32[]{:S(2)}, u32[]{:S(2)}) %collective-permute-start.22) | collective-permute-done | bytes 2080 | tf_op jit(solution)/shard_map/ppermute | solution.py:399
  (59 shorter events, 20.2 us)
Async XLA Ops:
  0.0 29.2 %collective-permute-start.1 = (f32[192,1,2,768]{3,2,1,0:T(2,128)}, f32[192,1,2,768]{3,2,1,0:T(2,128)S(1)}, u32[]{:S(2)}, u32[]{:S(2)}) collective-permute-start(f32[192,1,2,768]{3,2,1,0:T(2,128)} %refs_0_.1), channel_id=1, source_target_pairs={{0,2},{2,0},{1,3},{3,1},{4,6},{6,4},{5,7},{7,5},{8,10},{10,8},{9,1... | collective-permute-start | bytes 3538952 | tf_op jit(solution)/shard_map/ppermute | solution.py:296
  3.0 16.8 %collective-permute-start.11 = (f32[1,2,96,512]{3,2,1,0:T(8,128)S(1)}, f32[1,2,96,512]{3,2,1,0:T(8,128)}, u32[]{:S(2)}, u32[]{:S(2)}) collective-permute-start(f32[1,2,96,512]{3,2,1,0:T(8,128)S(1)} %constant_dynamic-slice_fusion.1.refs_0_), channel_id=1, source_target_pairs={{0,16},{4,20},{8,0},{12,4},{24,8},{28,12},{16,24},{20,28},{1,17},{... | collective-permute-start | bytes 1179656 | tf_op jit(solution)/shard_map/ppermute | solution.py:291
  5.7 19.9 %collective-permute-start.10 = (f32[1,2,96,512]{3,2,1,0:T(8,128)S(1)}, f32[1,2,96,512]{3,2,1,0:T(8,128)}, u32[]{:S(2)}, u32[]{:S(2)}) collective-permute-start(f32[1,2,96,512]{3,2,1,0:T(8,128)S(1)} %constant_dynamic-slice_fusion.1.refs_0_), channel_id=1, source_target_pairs={{0,8},{4,12},{8,24},{12,28},{24,16},{28,20},{16,0},{20,4},{1,9},{5... | collective-permute-start | bytes 1179656 | tf_op jit(solution)/shard_map/ppermute | solution.py:290
  5.7 3.8 %collective-permute-start.2 = (s32[3,1,2,6]{3,2,1,0:T(2,128)}, s32[3,1,2,6]{3,2,1,0:T(2,128)S(1)}, u32[]{:S(2)}, u32[]{:S(2)}) collective-permute-start(s32[3,1,2,6]{3,2,1,0:T(2,128)} %pattern.13), channel_id=1, source_target_pairs={{0,4},{4,0},{8,12},{12,8},{16,20},{20,16},{24,28},{28,24},{1,5},{5... | collective-permute-start | bytes 440 | tf_op jit(solution)/shard_map/ppermute | solution.py:303
  7.2 12.1 %collective-permute-start.9 = (f32[1,2,96,512]{3,2,1,0:T(8,128)S(1)}, f32[1,2,96,512]{3,2,1,0:T(8,128)S(1)}, u32[]{:S(2)}, u32[]{:S(2)}) collective-permute-start(f32[1,2,96,512]{3,2,1,0:T(8,128)S(1)} %constant_dynamic-slice_fusion), channel_id=1, source_target_pairs={{0,4},{4,0},{8,12},{12,8},{16,20},{20,16},{24,28},{28,24},{1,5},{5... | collective-permute-start | bytes 1179656 | tf_op jit(solution)/shard_map/ppermute | solution.py:288
  9.5 18.2 %collective-permute-start.3 = (f32[64,1,2,768]{3,2,1,0:T(2,128)S(1)}, f32[64,1,2,768]{3,2,1,0:T(2,128)S(1)}, u32[]{:S(2)}, u32[]{:S(2)}) collective-permute-start(f32[64,1,2,768]{3,2,1,0:T(2,128)S(1)} %get-tuple-element.136), channel_id=1, source_target_pairs={{0,4},{4,0},{8,12},{12,8},{16,20},{20,16},{24,28},{28,24},{1,5},{5... | collective-permute-start | bytes 1179656 | tf_op jit(solution)/shard_map/ppermute | solution.py:298
  19.3 16.9 %collective-permute-start.4 = (f32[64,1,2,768]{3,2,1,0:T(2,128)S(1)}, f32[64,1,2,768]{3,2,1,0:T(2,128)S(1)}, u32[]{:S(2)}, u32[]{:S(2)}) collective-permute-start(f32[64,1,2,768]{3,2,1,0:T(2,128)S(1)} %get-tuple-element.137), channel_id=1, source_target_pairs={{0,4},{4,0},{8,12},{12,8},{16,20},{20,16},{24,28},{28,24},{1,5},{5... | collective-permute-start | bytes 1179656 | tf_op jit(solution)/shard_map/ppermute | solution.py:298
  19.8 17.5 %collective-permute-start.13 = (f32[1,2,96,512]{3,2,1,0:T(8,128)S(1)}, f32[1,2,96,512]{3,2,1,0:T(8,128)S(1)}, u32[]{:S(2)}, u32[]{:S(2)}) collective-permute-start(f32[1,2,96,512]{3,2,1,0:T(8,128)S(1)} %collective-permute-done.9.refs_1_), channel_id=1, source_target_pairs={{0,16},{4,20},{8,0},{12,4},{24,8},{28,12},{16,24},{20,28},{1,17},{... | collective-permute-start | bytes 1179656 | tf_op jit(solution)/shard_map/ppermute | solution.py:291
  25.5 15.3 %collective-permute-start.12 = (f32[1,2,96,512]{3,2,1,0:T(8,128)S(1)}, f32[1,2,96,512]{3,2,1,0:T(8,128)S(1)}, u32[]{:S(2)}, u32[]{:S(2)}) collective-permute-start(f32[1,2,96,512]{3,2,1,0:T(8,128)S(1)} %collective-permute-done.9.refs_1_), channel_id=1, source_target_pairs={{0,8},{4,12},{8,24},{12,28},{24,16},{28,20},{16,0},{20,4},{1,9},{5... | collective-permute-start | bytes 1179656 | tf_op jit(solution)/shard_map/ppermute | solution.py:290
  27.7 20.6 %collective-permute-start.5 = (f32[64,1,2,768]{3,2,1,0:T(2,128)S(1)}, f32[64,1,2,768]{3,2,1,0:T(2,128)S(1)}, u32[]{:S(2)}, u32[]{:S(2)}) collective-permute-start(f32[64,1,2,768]{3,2,1,0:T(2,128)S(1)} %get-tuple-element.135), channel_id=1, source_target_pairs={{0,4},{4,0},{8,12},{12,8},{16,20},{20,16},{24,28},{28,24},{1,5},{5... | collective-permute-start | bytes 1179656 | tf_op jit(solution)/shard_map/ppermute | solution.py:298
  29.2 21.7 %collective-permute-start.6 = (f32[64,1,2,768]{3,2,1,0:T(2,128)S(1)}, f32[64,1,2,768]{3,2,1,0:T(2,128)S(1)}, u32[]{:S(2)}, u32[]{:S(2)}) collective-permute-start(f32[64,1,2,768]{3,2,1,0:T(2,128)S(1)} %collective-permute-done.3.refs_0_), channel_id=1, source_target_pairs={{0,2},{2,0},{1,3},{3,1},{4,6},{6,4},{5,7},{7,5},{8,10},{10,8},{9,1... | collective-permute-start | bytes 1179656 | tf_op jit(solution)/shard_map/ppermute | solution.py:301
  36.1 21.9 %collective-permute-start.8 = (f32[64,1,2,768]{3,2,1,0:T(2,128)S(1)}, f32[64,1,2,768]{3,2,1,0:T(2,128)S(1)}, u32[]{:S(2)}, u32[]{:S(2)}) collective-permute-start(f32[64,1,2,768]{3,2,1,0:T(2,128)S(1)} %collective-permute-done.4.refs_0_), channel_id=1, source_target_pairs={{0,2},{2,0},{1,3},{3,1},{4,6},{6,4},{5,7},{7,5},{8,10},{10,8},{9,1... | collective-permute-start | bytes 1179656 | tf_op jit(solution)/shard_map/ppermute | solution.py:302
  37.3 20.8 %collective-permute-start.7 = (f32[64,1,2,768]{3,2,1,0:T(2,128)S(1)}, f32[64,1,2,768]{3,2,1,0:T(2,128)S(1)}, u32[]{:S(2)}, u32[]{:S(2)}) collective-permute-start(f32[64,1,2,768]{3,2,1,0:T(2,128)S(1)} %slice.24), channel_id=1, source_target_pairs={{0,4},{4,0},{8,12},{12,8},{16,20},{20,16},{24,28},{28,24},{1,5},{5... | collective-permute-start | bytes 1179656 | tf_op jit(solution)/shard_map/ppermute | solution.py:300
  40.9 19.8 %collective-permute-start.14 = (f32[1,2,96,512]{3,2,1,0:T(8,128)}, f32[1,2,96,512]{3,2,1,0:T(8,128)S(1)}, u32[]{:S(2)}, u32[]{:S(2)}) collective-permute-start(f32[1,2,96,512]{3,2,1,0:T(8,128)} %collective-permute-done.10.refs_2_), channel_id=1, source_target_pairs={{0,8},{4,12},{8,24},{12,28},{24,16},{28,20},{16,0},{20,4},{1,9},{5... | collective-permute-start | bytes 1179656 | tf_op jit(solution)/shard_map/ppermute | solution.py:292
  48.3 13.2 %collective-permute-start.17 = (f32[1,2,96,384]{3,2,1,0:T(8,128)S(1)}, f32[1,2,96,384]{3,2,1,0:T(8,128)S(1)}, u32[]{:S(2)}, u32[]{:S(2)}) collective-permute-start(f32[1,2,96,384]{3,2,1,0:T(8,128)S(1)} %slice.26), channel_id=1, source_target_pairs={{0,8},{4,12},{8,24},{12,28},{24,16},{28,20},{16,0},{20,4},{1,9},{5... | collective-permute-start | bytes 884744 | tf_op jit(solution)/shard_map/ppermute | solution.py:293
  62.3 10.5 %collective-permute-start.18 = (f32[2,192,384]{2,1,0:T(8,128)S(1)}, f32[2,192,384]{2,1,0:T(8,128)S(1)}, u32[]{:S(2)}, u32[]{:S(2)}) collective-permute-start(f32[2,192,384]{2,1,0:T(8,128)S(1)} %get-tuple-element.128), channel_id=1, source_target_pairs={{0,1},{1,0},{2,3},{3,2},{4,5},{5,4},{6,7},{7,6},{8,9},{9,8},{10,11... | collective-permute-start | bytes 1769480 | tf_op jit(solution)/shard_map/ppermute | solution.py:381
  62.4 6.1 %collective-permute-start.15 = (f32[1,2,96,128]{3,2,1,0:T(8,128)S(1)}, f32[1,2,96,128]{3,2,1,0:T(8,128)S(1)}, u32[]{:S(2)}, u32[]{:S(2)}) collective-permute-start(f32[1,2,96,128]{3,2,1,0:T(8,128)S(1)} %slice.25), channel_id=1, source_target_pairs={{0,8},{4,12},{8,24},{12,28},{24,16},{28,20},{16,0},{20,4},{1,9},{5... | collective-permute-start | bytes 294920 | tf_op jit(solution)/shard_map/ppermute | solution.py:294
  69.1 7.2 %collective-permute-start.16 = (f32[4,192,128]{2,1,0:T(8,128)S(1)}, f32[4,192,128]{2,1,0:T(8,128)S(1)}, u32[]{:S(2)}, u32[]{:S(2)}) collective-permute-start(f32[4,192,128]{2,1,0:T(8,128)S(1)} %shard_map.57.mine), channel_id=1, source_target_pairs={{0,1},{1,0},{2,3},{3,2},{4,5},{5,4},{6,7},{7,6},{8,9},{9,8},{10,11... | collective-permute-start | bytes 1179656 | tf_op jit(solution)/shard_map/ppermute | solution.py:383
  69.2 3.7 %collective-permute-start = (s32[3,8]{1,0:T(4,128)S(1)}, s32[3,8]{1,0:T(4,128)S(1)}, u32[]{:S(2)}, u32[]{:S(2)}) collective-permute-start(s32[3,8]{1,0:T(4,128)S(1)} %copy-done.3), channel_id=1, source_target_pairs={{0,4},{4,0},{8,12},{12,8},{16,20},{20,16},{24,28},{28,24},{1,5},{5... | collective-permute-start | bytes 296 | tf_op jit(solution)/shard_map/ppermute | solution.py:304
  73.5 15.7 %collective-permute-start.23 = (f32[192,384]{1,0:T(8,128)S(1)}, f32[192,384]{1,0:T(8,128)S(1)}, u32[]{:S(2)}, u32[]{:S(2)}) collective-permute-start(f32[192,384]{1,0:T(8,128)S(1)} %get-tuple-element.133), channel_id=1, source_target_pairs={{0,4},{4,0},{8,12},{12,8},{16,20},{20,16},{24,28},{28,24},{1,5},{5... | collective-permute-start | bytes 884744 | tf_op jit(solution)/shard_map/ppermute | solution.py:389
  77.0 12.3 %collective-permute-start.24 = (f32[192,128]{1,0:T(8,128)S(1)}, f32[192,128]{1,0:T(8,128)S(1)}, u32[]{:S(2)}, u32[]{:S(2)}) collective-permute-start(f32[192,128]{1,0:T(8,128)S(1)} %get-tuple-element.134), channel_id=1, source_target_pairs={{0,4},{4,0},{8,12},{12,8},{16,20},{20,16},{24,28},{28,24},{1,5},{5... | collective-permute-start | bytes 294920 | tf_op jit(solution)/shard_map/ppermute | solution.py:396
  77.6 3.6 %collective-permute-start.20 = (f32[1,512]{1,0:T(1,128)S(1)}, f32[1,512]{1,0:T(1,128)S(1)}, u32[]{:S(2)}, u32[]{:S(2)}) collective-permute-start(f32[1,512]{1,0:T(1,128)S(1)} %get-tuple-element.130), channel_id=1, source_target_pairs={{0,8},{4,12},{8,0},{12,4},{16,24},{20,28},{24,16},{28,20},{1,9},{5... | collective-permute-start | bytes 6152 | tf_op jit(solution)/shard_map/ppermute | solution.py:398
  81.1 4.5 %collective-permute-start.21 = (f32[1,512]{1,0:T(1,128)S(1)}, f32[1,512]{1,0:T(1,128)S(1)}, u32[]{:S(2)}, u32[]{:S(2)}) collective-permute-start(f32[1,512]{1,0:T(1,128)S(1)} %add.10), channel_id=1, source_target_pairs={{0,16},{4,20},{8,24},{12,28},{16,0},{20,4},{24,8},{28,12},{1,17},{... | collective-permute-start | bytes 6152 | tf_op jit(solution)/shard_map/ppermute | solution.py:398
  85.6 3.6 %collective-permute-start.22 = (f32[1,512]{1,0:T(1,128)S(1)}, f32[1,512]{1,0:T(1,128)S(1)}, u32[]{:S(2)}, u32[]{:S(2)}) collective-permute-start(f32[1,512]{1,0:T(1,128)S(1)} %add.11.sums), channel_id=1, source_target_pairs={{0,4},{4,0},{8,12},{12,8},{16,20},{20,16},{24,28},{28,24},{1,5},{5... | collective-permute-start | bytes 6152 | tf_op jit(solution)/shard_map/ppermute | solution.py:399
  (5 other events, 53.0 us)

commit v6 on v5

--- a/solution.py
+++ b/solution.py
@@ -16,20 +16,8 @@
 UNIT = 64
 
 
-LINE = (0, 1, 3, 2)
-
-
-def line_pairs(shift):
-    size = len(LINE)
-    return [
-        (LINE[i] * 2 + y, LINE[(i + shift) % size] * 2 + y) for i in range(size) for y in range(2)
-    ]
-
-
-def line_at(z, step):
-    place = jnp.where(z < 2, z, 5 - z)
-    place = (place + step + len(LINE)) % len(LINE)
-    return jnp.where(place < 2, place, 5 - place)
+def z_pairs(bits):
+    return [(row, row ^ (2 * bits)) for row in range(8)]
 
 
 def all_sum(value, axis_name):
@@ -114,7 +102,7 @@
                     turned[r, s] = value[:, r * depth : (r + 1) * depth]
             place = pl.ds(done, UNIT)
             for i, members in enumerate(groups):
-                owners = [line_at(row // 2, step) * 2 + (row + turn) % 2 for step, turn in members]
+                owners = [row ^ (2 * bits + turn) for bits, turn in members]
                 pieces = [turned[r, s] for r in owners for s in range(sections)]
                 high, low = split(jnp.concatenate(pieces, axis=1))
                 outs[2 * i][place, :] = high
@@ -287,11 +275,11 @@
     shards = {(0, 0): own}
     shards[0, 1] = lax.ppermute(columns_half(1 - my_y), "row", swap_y)
     for turn in range(2):
-        shards[-1, turn] = lax.ppermute(shards[0, turn], "row", line_pairs(1))
-        shards[1, turn] = lax.ppermute(shards[0, turn], "row", line_pairs(-1))
-    shards[2, 0] = lax.ppermute(shards[-1, 0], "row", line_pairs(1))
-    far_early = lax.ppermute(shards[-1, 1][..., :cut], "row", line_pairs(1))
-    far_last = lax.ppermute(shards[-1, 1][..., cut:], "row", line_pairs(1))
+        shards[1, turn] = lax.ppermute(shards[0, turn], "row", z_pairs(1))
+        shards[2, turn] = lax.ppermute(shards[0, turn], "row", z_pairs(2))
+    shards[3, 0] = lax.ppermute(shards[2, 0], "row", z_pairs(1))
+    far_early = lax.ppermute(shards[2, 1][..., :cut], "row", z_pairs(1))
+    far_last = lax.ppermute(shards[2, 1][..., cut:], "row", z_pairs(1))
 
     from_x = lax.ppermute(a_panels, "col", swap)
     y0, y1, y2 = (
@@ -303,7 +291,7 @@
     a_tables = [a_pattern, lax.ppermute(a_pattern, "row", swap_y)]
     c_tables = [c_pattern, lax.ppermute(c_pattern, "row", swap_y)]
 
-    groups = [[(0, 0), (0, 1), (-1, 0), (1, 0)], [(-1, 1), (1, 1)], [(2, 0)], [(2, 1)]]
+    groups = [[(0, 0), (0, 1), (1, 0), (2, 0)], [(1, 1), (2, 1)], [(3, 0)], [(3, 1)]]
     shard_depth = sections * depth
 
     def left(*sources):
@@ -363,7 +351,7 @@
         [VMEM] * (len(hop_lefts) + 3),
         [factor, factor],
         6 * 4 * rows * half * shard_depth,
-    )(*hop_lefts, near, near_late, shards[2, 0])
+    )(*hop_lefts, near, near_late, shards[3, 0])
 
     far_lefts = picked(all_sets, 3)
 

time: 90.4 us -> 91.5 us (1.012)
  waiting for transfers between devices: 42.6 us -> 43.7 us
    ppermute x3, waiting for transfers between devices: 6.68 us -> 8.9 us  [local(): lax.ppermute(a_panels[u * UNIT:(u + 1) * UNIT], 'row', swap_y)]
    ppermute x7, waiting for transfers between devices: 12 us -> 10.9 us  [the longest x2 5.55 us: local(): shards[2, turn] = lax.ppermute(shards[0, turn], 'row', z_pairs(2))]
    ppermute x2, starting transfers between devices: 0.01 us -> 1.08 us  [local(): lax.ppermute(sums, 'row', [(r, r ^ bit) for r in range(n_row)])]
    ppermute x2, waiting for transfers between devices: 8.06 us -> 6.99 us  [local(): lax.ppermute(sums, 'row', [(r, r ^ bit) for r in range(n_row)])]
    ppermute x1, starting transfers between devices: 0.51 us -> 1.52 us  [local(): d2 = lax.ppermute(from_x[2 * UNIT:], 'row', swap_y)]
    ppermute x1, starting transfers between devices: 0.58 us -> 1.59 us  [local(): last_comes = lax.ppermute(last_goes, 'row', swap_y)]
    ppermute x1, starting transfers between devices: 1.57 us -> 0.56 us  [local(): c_tables = [c_pattern, lax.ppermute(c_pattern, 'row', swap_y)]]
    ppermute x1, starting transfers between devices: 1.57 us -> 0.56 us  [local(): comes = lax.ppermute(goes, 'row', swap_y)]
where the time goes in v6:
time: 91.5 us; the launch traced here: 91.4 us
  waiting for transfers between devices  43.7 us (48%)
  starting transfers between devices  26 us (28%)
  Pallas kernels  20.9 us (23%)
    pallas_call x16, Pallas kernels, run(): pl.pallas_call(kernel, out_shape=out_shapes, in_specs=specs, out_specs=[V...  20.9 us
    ppermute x3, waiting for transfers between devices, local(): lax.ppermute(a_panels[u * UNIT:(u + 1) * UNIT], 'row', swap_y)  8.9 us
    ppermute x1, waiting for transfers between devices, local(): shards[0, 1] = lax.ppermute(columns_half(1 - my_y), 'row', swap_y)  8.26 us
    ppermute x2, waiting for transfers between devices, local(): lax.ppermute(sums, 'row', [(r, r ^ bit) for r in range(n_row)])  6.99 us
    ppermute x2, waiting for transfers between devices, local(): shards[2, turn] = lax.ppermute(shards[0, turn], 'row', z_pairs(2))  5.55 us
    ppermute x2, starting transfers between devices, local(): shards[1, turn] = lax.ppermute(shards[0, turn], 'row', z_pairs(1))  5.34 us
    ppermute x1, waiting for transfers between devices, local(): far_last = lax.ppermute(shards[2, 1][..., cut:], 'row', z_pairs(1))  5.18 us
    ppermute x1, waiting for transfers between devices, local(): c_tables = [c_pattern, lax.ppermute(c_pattern, 'row', swap_y)]  3.09 us
  transfers between devices with their start and end apart: 25, of which 13 were waited for; matrix products, arithmetic and copies ran while one was open for 1% of the time, Pallas kernels for 21%

profile of v6, /device:TPU:0, one launch (start us, length us, event | category | flops | bytes accessed | tf_op | source)
XLA Modules:
  0.0 91.4 jit_solution(3033272275597630263)
XLA Ops:
  0.0 3.0 %collective-permute-start.1 = (f32[192,1,2,768]{3,2,1,0:T(2,128)}, f32[192,1,2,768]{3,2,1,0:T(2,128)S(1)}, u32[]{:S(2)}, u32[]{:S(2)}) collective-permute-start(f32[192,1,2,768]{3,2,1,0:T(2,128)} %refs_0_.1), channel_id=1, source_target_pairs={{0,2},{2,0},{1,3},{3,1},{4,6},{6,4},{5,7},{7,5},{8,10},{10,8},{9,1... | collective-permute-start | bytes 3538952 | tf_op jit(solution)/shard_map/ppermute | solution.py:284
  3.0 2.7 %collective-permute-start.11 = (f32[1,2,96,512]{3,2,1,0:T(8,128)S(1)}, f32[1,2,96,512]{3,2,1,0:T(8,128)}, u32[]{:S(2)}, u32[]{:S(2)}) collective-permute-start(f32[1,2,96,512]{3,2,1,0:T(8,128)S(1)} %constant_dynamic-slice_fusion.1.refs_0_), channel_id=1, source_target_pairs={{0,16},{4,20},{8,24},{12,28},{16,0},{20,4},{24,8},{28,12},{1,17},{... | collective-permute-start | bytes 1179656 | tf_op jit(solution)/shard_map/ppermute | solution.py:279
  5.7 1.6 %collective-permute-start.10 = (f32[1,2,96,512]{3,2,1,0:T(8,128)S(1)}, f32[1,2,96,512]{3,2,1,0:T(8,128)}, u32[]{:S(2)}, u32[]{:S(2)}) collective-permute-start(f32[1,2,96,512]{3,2,1,0:T(8,128)S(1)} %constant_dynamic-slice_fusion.1.refs_0_), channel_id=1, source_target_pairs={{0,8},{4,12},{8,0},{12,4},{16,24},{20,28},{24,16},{28,20},{1,9},{5... | collective-permute-start | bytes 1179656 | tf_op jit(solution)/shard_map/ppermute | solution.py:278
  7.2 1.5 %collective-permute-start.2 = (s32[3,1,2,6]{3,2,1,0:T(2,128)}, s32[3,1,2,6]{3,2,1,0:T(2,128)S(1)}, u32[]{:S(2)}, u32[]{:S(2)}) collective-permute-start(s32[3,1,2,6]{3,2,1,0:T(2,128)} %pattern.13), channel_id=1, source_target_pairs={{0,4},{4,0},{8,12},{12,8},{16,20},{20,16},{24,28},{28,24},{1,5},{5... | collective-permute-start | bytes 440 | tf_op jit(solution)/shard_map/ppermute | solution.py:291
  11.1 1.5 %collective-permute-start.3 = (f32[64,1,2,768]{3,2,1,0:T(2,128)S(1)}, f32[64,1,2,768]{3,2,1,0:T(2,128)S(1)}, u32[]{:S(2)}, u32[]{:S(2)}) collective-permute-start(f32[64,1,2,768]{3,2,1,0:T(2,128)S(1)} %get-tuple-element.136), channel_id=1, source_target_pairs={{0,4},{4,0},{8,12},{12,8},{16,20},{20,16},{24,28},{28,24},{1,5},{5... | collective-permute-start | bytes 1179656 | tf_op jit(solution)/shard_map/ppermute | solution.py:286
  12.6 8.3 %collective-permute-done.9.refs_1_ = f32[1,2,96,512]{3,2,1,0:T(8,128)S(1)} collective-permute-done((f32[1,2,96,512]{3,2,1,0:T(8,128)S(1)}, f32[1,2,96,512]{3,2,1,0:T(8,128)S(1)}, u32[]{:S(2)}, u32[]{:S(2)}) %collective-permute-start.9) | collective-permute-done | bytes 393248 | tf_op jit(solution)/shard_map/ppermute | solution.py:276
  21.4 1.8 %collective-permute-done.11.refs_3_ = f32[1,2,96,512]{3,2,1,0:T(8,128)} collective-permute-done((f32[1,2,96,512]{3,2,1,0:T(8,128)S(1)}, f32[1,2,96,512]{3,2,1,0:T(8,128)}, u32[]{:S(2)}, u32[]{:S(2)}) %collective-permute-start.11) | collective-permute-done | bytes 393248 | tf_op jit(solution)/shard_map/ppermute | solution.py:279
  23.4 3.8 %collective-permute-start.12 = (f32[1,2,96,512]{3,2,1,0:T(8,128)S(1)}, f32[1,2,96,512]{3,2,1,0:T(8,128)S(1)}, u32[]{:S(2)}, u32[]{:S(2)}) collective-permute-start(f32[1,2,96,512]{3,2,1,0:T(8,128)S(1)} %collective-permute-done.9.refs_1_), channel_id=1, source_target_pairs={{0,8},{4,12},{8,0},{12,4},{16,24},{20,28},{24,16},{28,20},{1,9},{5... | collective-permute-start | bytes 1179656 | tf_op jit(solution)/shard_map/ppermute | solution.py:278
  27.1 2.1 %collective-permute-done.3.refs_0_ = f32[64,1,2,768]{3,2,1,0:T(2,128)S(1)} collective-permute-done((f32[64,1,2,768]{3,2,1,0:T(2,128)S(1)}, f32[64,1,2,768]{3,2,1,0:T(2,128)S(1)}, u32[]{:S(2)}, u32[]{:S(2)}) %collective-permute-start.3) | collective-permute-done | bytes 393248 | tf_op jit(solution)/shard_map/ppermute | solution.py:286
  31.0 6.7 %collective-permute-done.4.refs_0_ = f32[64,1,2,768]{3,2,1,0:T(2,128)S(1)} collective-permute-done((f32[64,1,2,768]{3,2,1,0:T(2,128)S(1)}, f32[64,1,2,768]{3,2,1,0:T(2,128)S(1)}, u32[]{:S(2)}, u32[]{:S(2)}) %collective-permute-start.4) | collective-permute-done | bytes 393248 | tf_op jit(solution)/shard_map/ppermute | solution.py:286
  38.8 3.7 %collective-permute-done.13.refs_1_ = f32[1,2,96,512]{3,2,1,0:T(8,128)S(1)} collective-permute-done((f32[1,2,96,512]{3,2,1,0:T(8,128)S(1)}, f32[1,2,96,512]{3,2,1,0:T(8,128)S(1)}, u32[]{:S(2)}, u32[]{:S(2)}) %collective-permute-start.13) | collective-permute-done | bytes 393248 | tf_op jit(solution)/shard_map/ppermute | solution.py:279
  42.6 1.5 %collective-permute-start.7 = (f32[64,1,2,768]{3,2,1,0:T(2,128)S(1)}, f32[64,1,2,768]{3,2,1,0:T(2,128)S(1)}, u32[]{:S(2)}, u32[]{:S(2)}) collective-permute-start(f32[64,1,2,768]{3,2,1,0:T(2,128)S(1)} %slice.24), channel_id=1, source_target_pairs={{0,4},{4,0},{8,12},{12,8},{16,20},{20,16},{24,28},{28,24},{1,5},{5... | collective-permute-start | bytes 1179656 | tf_op jit(solution)/shard_map/ppermute | solution.py:288
  44.1 2.5 %shard_map.46 = (bf16[192,768]{1,0:T(8,128)(2,1)S(1)}, bf16[192,768]{1,0:T(8,128)(2,1)S(1)}, bf16[192,384]{1,0:T(8,128)(2,1)S(1)}, bf16[192,384]{1,0:T(8,128)(2,...) custom-call(s32[3,1,2,6]{3,2,1,0:T(2,128)S(1)} %copy-done.2, ...), custom_call_target="tpu_custom_call" | custom-call | bytes 2359584 | tf_op jit(solution)/shard_map/pallas_call | solution.py:238
  50.8 2.1 %collective-permute-start.17 = (f32[1,2,96,384]{3,2,1,0:T(8,128)S(1)}, f32[1,2,96,384]{3,2,1,0:T(8,128)S(1)}, u32[]{:S(2)}, u32[]{:S(2)}) collective-permute-start(f32[1,2,96,384]{3,2,1,0:T(8,128)S(1)} %slice.26), channel_id=1, source_target_pairs={{0,8},{4,12},{8,0},{12,4},{16,24},{20,28},{24,16},{28,20},{1,9},{5... | collective-permute-start | bytes 884744 | tf_op jit(solution)/shard_map/ppermute | solution.py:281
  52.9 1.9 %shard_map.50 = (bf16[128,768]{1,0:T(8,128)(2,1)S(1)}, bf16[128,768]{1,0:T(8,128)(2,1)S(1)}, bf16[128,384]{1,0:T(8,128)(2,1)S(1)}, bf16[128,384]{1,0:T(8,128)(2,...) custom-call(s32[3,1,2,6]{3,2,1,0:T(2,128)S(1)} %copy-done.2, ...), custom_call_target="tpu_custom_call" | custom-call | bytes 1573152 | tf_op jit(solution)/shard_map/pallas_call | solution.py:238
  54.8 2.5 %shard_map.47 = (bf16[192,768]{1,0:T(8,128)(2,1)S(1)}, bf16[192,768]{1,0:T(8,128)(2,1)S(1)}, bf16[192,384]{1,0:T(8,128)(2,1)S(1)}, bf16[192,384]{1,0:T(8,128)(2,...) custom-call(s32[3,1,2,6]{3,2,1,0:T(2,128)S(1)} %copy-done.2, ...), custom_call_target="tpu_custom_call" | custom-call | bytes 2359584 | tf_op jit(solution)/shard_map/pallas_call | solution.py:238
  57.4 2.7 %shard_map.53.refs_12_ = f32[640,512]{1,0:T(8,128)S(1)} custom-call(bf16[192,768]{1,0:T(8,128)(2,1)S(1)} %get-tuple-element.75.refs_0_, bf16[192,768]{1,0:T(8,128)(2,1)S(1)} %get-tuple-element.76.refs_1_, bf16[64,768]{1,0:T(8,128)(2,1)S(1)} %get-tuple-element.77.refs_2_, bf16[64,768]{1,0:T(8,128)(2,1)S(1)} %get-tuple-element.78.refs_3_, ...), custom_call_target="tpu_custom_call" | custom-call | flops 2264924160 | bytes 6619136 | tf_op jit(solution)/shard_map/pallas_call | solution.py:238
  60.1 1.9 %shard_map.54 = (bf16[128,768]{1,0:T(8,128)(2,1)S(1)}, bf16[128,768]{1,0:T(8,128)(2,1)S(1)}, bf16[128,384]{1,0:T(8,128)(2,1)S(1)}, bf16[128,384]{1,0:T(8,128)(2,...) custom-call(s32[3,1,2,6]{3,2,1,0:T(2,128)S(1)} %copy-done.2, ...), custom_call_target="tpu_custom_call" | custom-call | bytes 1573152 | tf_op jit(solution)/shard_map/pallas_call | solution.py:238
  64.6 5.2 %collective-permute-done.15.refs_13_ = f32[1,2,96,128]{3,2,1,0:T(8,128)S(1)} collective-permute-done((f32[1,2,96,128]{3,2,1,0:T(8,128)S(1)}, f32[1,2,96,128]{3,2,1,0:T(8,128)S(1)}, u32[]{:S(2)}, u32[]{:S(2)}) %collective-permute-start.15) | collective-permute-done | bytes 98336 | tf_op jit(solution)/shard_map/ppermute | solution.py:282
  70.9 3.1 %collective-permute-done.other_pattern = s32[3,8]{1,0:T(4,128)S(1)} collective-permute-done((s32[3,8]{1,0:T(4,128)S(1)}, s32[3,8]{1,0:T(4,128)S(1)}, u32[]{:S(2)}, u32[]{:S(2)}) %collective-permute-start) | collective-permute-done | bytes 128 | tf_op jit(solution)/shard_map/ppermute | solution.py:292
  77.1 1.6 %collective-permute-start.24 = (f32[192,128]{1,0:T(8,128)S(1)}, f32[192,128]{1,0:T(8,128)S(1)}, u32[]{:S(2)}, u32[]{:S(2)}) collective-permute-start(f32[192,128]{1,0:T(8,128)S(1)} %get-tuple-element.134), channel_id=1, source_target_pairs={{0,4},{4,0},{8,12},{12,8},{16,20},{20,16},{24,28},{28,24},{1,5},{5... | collective-permute-start | bytes 294920 | tf_op jit(solution)/shard_map/ppermute | solution.py:384
  79.0 3.3 %collective-permute-done.20 = f32[1,512]{1,0:T(1,128)S(1)} collective-permute-done((f32[1,512]{1,0:T(1,128)S(1)}, f32[1,512]{1,0:T(1,128)S(1)}, u32[]{:S(2)}, u32[]{:S(2)}) %collective-permute-start.20) | collective-permute-done | bytes 2080 | tf_op jit(solution)/shard_map/ppermute | solution.py:386
  83.1 3.7 %collective-permute-done.21 = f32[1,512]{1,0:T(1,128)S(1)} collective-permute-done((f32[1,512]{1,0:T(1,128)S(1)}, f32[1,512]{1,0:T(1,128)S(1)}, u32[]{:S(2)}, u32[]{:S(2)}) %collective-permute-start.21) | collective-permute-done | bytes 2080 | tf_op jit(solution)/shard_map/ppermute | solution.py:386
  87.3 3.1 %collective-permute-done.22.other_sums = f32[1,512]{1,0:T(1,128)S(1)} collective-permute-done((f32[1,512]{1,0:T(1,128)S(1)}, f32[1,512]{1,0:T(1,128)S(1)}, u32[]{:S(2)}, u32[]{:S(2)}) %collective-permute-start.22) | collective-permute-done | bytes 2080 | tf_op jit(solution)/shard_map/ppermute | solution.py:387
  (59 shorter events, 19.3 us)
Async XLA Ops:
  0.0 29.8 %collective-permute-start.1 = (f32[192,1,2,768]{3,2,1,0:T(2,128)}, f32[192,1,2,768]{3,2,1,0:T(2,128)S(1)}, u32[]{:S(2)}, u32[]{:S(2)}) collective-permute-start(f32[192,1,2,768]{3,2,1,0:T(2,128)} %refs_0_.1), channel_id=1, source_target_pairs={{0,2},{2,0},{1,3},{3,1},{4,6},{6,4},{5,7},{7,5},{8,10},{10,8},{9,1... | collective-permute-start | bytes 3538952 | tf_op jit(solution)/shard_map/ppermute | solution.py:284
  3.0 20.2 %collective-permute-start.11 = (f32[1,2,96,512]{3,2,1,0:T(8,128)S(1)}, f32[1,2,96,512]{3,2,1,0:T(8,128)}, u32[]{:S(2)}, u32[]{:S(2)}) collective-permute-start(f32[1,2,96,512]{3,2,1,0:T(8,128)S(1)} %constant_dynamic-slice_fusion.1.refs_0_), channel_id=1, source_target_pairs={{0,16},{4,20},{8,24},{12,28},{16,0},{20,4},{24,8},{28,12},{1,17},{... | collective-permute-start | bytes 1179656 | tf_op jit(solution)/shard_map/ppermute | solution.py:279
  5.7 17.7 %collective-permute-start.10 = (f32[1,2,96,512]{3,2,1,0:T(8,128)S(1)}, f32[1,2,96,512]{3,2,1,0:T(8,128)}, u32[]{:S(2)}, u32[]{:S(2)}) collective-permute-start(f32[1,2,96,512]{3,2,1,0:T(8,128)S(1)} %constant_dynamic-slice_fusion.1.refs_0_), channel_id=1, source_target_pairs={{0,8},{4,12},{8,0},{12,4},{16,24},{20,28},{24,16},{28,20},{1,9},{5... | collective-permute-start | bytes 1179656 | tf_op jit(solution)/shard_map/ppermute | solution.py:278
  7.2 3.8 %collective-permute-start.2 = (s32[3,1,2,6]{3,2,1,0:T(2,128)}, s32[3,1,2,6]{3,2,1,0:T(2,128)S(1)}, u32[]{:S(2)}, u32[]{:S(2)}) collective-permute-start(s32[3,1,2,6]{3,2,1,0:T(2,128)} %pattern.13), channel_id=1, source_target_pairs={{0,4},{4,0},{8,12},{12,8},{16,20},{20,16},{24,28},{28,24},{1,5},{5... | collective-permute-start | bytes 440 | tf_op jit(solution)/shard_map/ppermute | solution.py:291
  8.8 12.1 %collective-permute-start.9 = (f32[1,2,96,512]{3,2,1,0:T(8,128)S(1)}, f32[1,2,96,512]{3,2,1,0:T(8,128)S(1)}, u32[]{:S(2)}, u32[]{:S(2)}) collective-permute-start(f32[1,2,96,512]{3,2,1,0:T(8,128)S(1)} %constant_dynamic-slice_fusion), channel_id=1, source_target_pairs={{0,4},{4,0},{8,12},{12,8},{16,20},{20,16},{24,28},{28,24},{1,5},{5... | collective-permute-start | bytes 1179656 | tf_op jit(solution)/shard_map/ppermute | solution.py:276
  11.1 18.2 %collective-permute-start.3 = (f32[64,1,2,768]{3,2,1,0:T(2,128)S(1)}, f32[64,1,2,768]{3,2,1,0:T(2,128)S(1)}, u32[]{:S(2)}, u32[]{:S(2)}) collective-permute-start(f32[64,1,2,768]{3,2,1,0:T(2,128)S(1)} %get-tuple-element.136), channel_id=1, source_target_pairs={{0,4},{4,0},{8,12},{12,8},{16,20},{20,16},{24,28},{28,24},{1,5},{5... | collective-permute-start | bytes 1179656 | tf_op jit(solution)/shard_map/ppermute | solution.py:286
  20.9 16.9 %collective-permute-start.4 = (f32[64,1,2,768]{3,2,1,0:T(2,128)S(1)}, f32[64,1,2,768]{3,2,1,0:T(2,128)S(1)}, u32[]{:S(2)}, u32[]{:S(2)}) collective-permute-start(f32[64,1,2,768]{3,2,1,0:T(2,128)S(1)} %get-tuple-element.137), channel_id=1, source_target_pairs={{0,4},{4,0},{8,12},{12,8},{16,20},{20,16},{24,28},{28,24},{1,5},{5... | collective-permute-start | bytes 1179656 | tf_op jit(solution)/shard_map/ppermute | solution.py:286
  23.2 19.4 %collective-permute-start.13 = (f32[1,2,96,512]{3,2,1,0:T(8,128)S(1)}, f32[1,2,96,512]{3,2,1,0:T(8,128)S(1)}, u32[]{:S(2)}, u32[]{:S(2)}) collective-permute-start(f32[1,2,96,512]{3,2,1,0:T(8,128)S(1)} %collective-permute-done.9.refs_1_), channel_id=1, source_target_pairs={{0,16},{4,20},{8,24},{12,28},{16,0},{20,4},{24,8},{28,12},{1,17},{... | collective-permute-start | bytes 1179656 | tf_op jit(solution)/shard_map/ppermute | solution.py:279
  23.4 20.7 %collective-permute-start.12 = (f32[1,2,96,512]{3,2,1,0:T(8,128)S(1)}, f32[1,2,96,512]{3,2,1,0:T(8,128)S(1)}, u32[]{:S(2)}, u32[]{:S(2)}) collective-permute-start(f32[1,2,96,512]{3,2,1,0:T(8,128)S(1)} %collective-permute-done.9.refs_1_), channel_id=1, source_target_pairs={{0,8},{4,12},{8,0},{12,4},{16,24},{20,28},{24,16},{28,20},{1,9},{5... | collective-permute-start | bytes 1179656 | tf_op jit(solution)/shard_map/ppermute | solution.py:278
  29.3 21.5 %collective-permute-start.5 = (f32[64,1,2,768]{3,2,1,0:T(2,128)S(1)}, f32[64,1,2,768]{3,2,1,0:T(2,128)S(1)}, u32[]{:S(2)}, u32[]{:S(2)}) collective-permute-start(f32[64,1,2,768]{3,2,1,0:T(2,128)S(1)} %get-tuple-element.135), channel_id=1, source_target_pairs={{0,4},{4,0},{8,12},{12,8},{16,20},{20,16},{24,28},{28,24},{1,5},{5... | collective-permute-start | bytes 1179656 | tf_op jit(solution)/shard_map/ppermute | solution.py:286
  29.8 23.1 %collective-permute-start.6 = (f32[64,1,2,768]{3,2,1,0:T(2,128)S(1)}, f32[64,1,2,768]{3,2,1,0:T(2,128)S(1)}, u32[]{:S(2)}, u32[]{:S(2)}) collective-permute-start(f32[64,1,2,768]{3,2,1,0:T(2,128)S(1)} %collective-permute-done.3.refs_0_), channel_id=1, source_target_pairs={{0,2},{2,0},{1,3},{3,1},{4,6},{6,4},{5,7},{7,5},{8,10},{10,8},{9,1... | collective-permute-start | bytes 1179656 | tf_op jit(solution)/shard_map/ppermute | solution.py:289
  37.7 22.3 %collective-permute-start.8 = (f32[64,1,2,768]{3,2,1,0:T(2,128)S(1)}, f32[64,1,2,768]{3,2,1,0:T(2,128)S(1)}, u32[]{:S(2)}, u32[]{:S(2)}) collective-permute-start(f32[64,1,2,768]{3,2,1,0:T(2,128)S(1)} %collective-permute-done.4.refs_0_), channel_id=1, source_target_pairs={{0,2},{2,0},{1,3},{3,1},{4,6},{6,4},{5,7},{7,5},{8,10},{10,8},{9,1... | collective-permute-start | bytes 1179656 | tf_op jit(solution)/shard_map/ppermute | solution.py:290
  42.6 17.5 %collective-permute-start.7 = (f32[64,1,2,768]{3,2,1,0:T(2,128)S(1)}, f32[64,1,2,768]{3,2,1,0:T(2,128)S(1)}, u32[]{:S(2)}, u32[]{:S(2)}) collective-permute-start(f32[64,1,2,768]{3,2,1,0:T(2,128)S(1)} %slice.24), channel_id=1, source_target_pairs={{0,4},{4,0},{8,12},{12,8},{16,20},{20,16},{24,28},{28,24},{1,5},{5... | collective-permute-start | bytes 1179656 | tf_op jit(solution)/shard_map/ppermute | solution.py:288
  44.1 18.6 %collective-permute-start.14 = (f32[1,2,96,512]{3,2,1,0:T(8,128)}, f32[1,2,96,512]{3,2,1,0:T(8,128)S(1)}, u32[]{:S(2)}, u32[]{:S(2)}) collective-permute-start(f32[1,2,96,512]{3,2,1,0:T(8,128)} %collective-permute-done.11.refs_3_), channel_id=1, source_target_pairs={{0,8},{4,12},{8,0},{12,4},{16,24},{20,28},{24,16},{28,20},{1,9},{5... | collective-permute-start | bytes 1179656 | tf_op jit(solution)/shard_map/ppermute | solution.py:280
  50.8 12.7 %collective-permute-start.17 = (f32[1,2,96,384]{3,2,1,0:T(8,128)S(1)}, f32[1,2,96,384]{3,2,1,0:T(8,128)S(1)}, u32[]{:S(2)}, u32[]{:S(2)}) collective-permute-start(f32[1,2,96,384]{3,2,1,0:T(8,128)S(1)} %slice.26), channel_id=1, source_target_pairs={{0,8},{4,12},{8,0},{12,4},{16,24},{20,28},{24,16},{28,20},{1,9},{5... | collective-permute-start | bytes 884744 | tf_op jit(solution)/shard_map/ppermute | solution.py:281
  64.4 9.6 %collective-permute-start.18 = (f32[2,192,384]{2,1,0:T(8,128)S(1)}, f32[2,192,384]{2,1,0:T(8,128)S(1)}, u32[]{:S(2)}, u32[]{:S(2)}) collective-permute-start(f32[2,192,384]{2,1,0:T(8,128)S(1)} %get-tuple-element.128), channel_id=1, source_target_pairs={{0,1},{1,0},{2,3},{3,2},{4,5},{5,4},{6,7},{7,6},{8,9},{9,8},{10,11... | collective-permute-start | bytes 1769480 | tf_op jit(solution)/shard_map/ppermute | solution.py:369
  64.5 5.3 %collective-permute-start.15 = (f32[1,2,96,128]{3,2,1,0:T(8,128)S(1)}, f32[1,2,96,128]{3,2,1,0:T(8,128)S(1)}, u32[]{:S(2)}, u32[]{:S(2)}) collective-permute-start(f32[1,2,96,128]{3,2,1,0:T(8,128)S(1)} %slice.25), channel_id=1, source_target_pairs={{0,8},{4,12},{8,0},{12,4},{16,24},{20,28},{24,16},{28,20},{1,9},{5... | collective-permute-start | bytes 294920 | tf_op jit(solution)/shard_map/ppermute | solution.py:282
  70.2 6.2 %collective-permute-start.16 = (f32[4,192,128]{2,1,0:T(8,128)S(1)}, f32[4,192,128]{2,1,0:T(8,128)S(1)}, u32[]{:S(2)}, u32[]{:S(2)}) collective-permute-start(f32[4,192,128]{2,1,0:T(8,128)S(1)} %shard_map.57.mine), channel_id=1, source_target_pairs={{0,1},{1,0},{2,3},{3,2},{4,5},{5,4},{6,7},{7,6},{8,9},{9,8},{10,11... | collective-permute-start | bytes 1179656 | tf_op jit(solution)/shard_map/ppermute | solution.py:371
  70.3 3.7 %collective-permute-start = (s32[3,8]{1,0:T(4,128)S(1)}, s32[3,8]{1,0:T(4,128)S(1)}, u32[]{:S(2)}, u32[]{:S(2)}) collective-permute-start(s32[3,8]{1,0:T(4,128)S(1)} %copy-done.3), channel_id=1, source_target_pairs={{0,4},{4,0},{8,12},{12,8},{16,20},{20,16},{24,28},{28,24},{1,5},{5... | collective-permute-start | bytes 296 | tf_op jit(solution)/shard_map/ppermute | solution.py:292
  74.7 15.7 %collective-permute-start.23 = (f32[192,384]{1,0:T(8,128)S(1)}, f32[192,384]{1,0:T(8,128)S(1)}, u32[]{:S(2)}, u32[]{:S(2)}) collective-permute-start(f32[192,384]{1,0:T(8,128)S(1)} %get-tuple-element.133), channel_id=1, source_target_pairs={{0,4},{4,0},{8,12},{12,8},{16,20},{20,16},{24,28},{28,24},{1,5},{5... | collective-permute-start | bytes 884744 | tf_op jit(solution)/shard_map/ppermute | solution.py:377
  77.1 13.3 %collective-permute-start.24 = (f32[192,128]{1,0:T(8,128)S(1)}, f32[192,128]{1,0:T(8,128)S(1)}, u32[]{:S(2)}, u32[]{:S(2)}) collective-permute-start(f32[192,128]{1,0:T(8,128)S(1)} %get-tuple-element.134), channel_id=1, source_target_pairs={{0,4},{4,0},{8,12},{12,8},{16,20},{20,16},{24,28},{28,24},{1,5},{5... | collective-permute-start | bytes 294920 | tf_op jit(solution)/shard_map/ppermute | solution.py:384
  78.7 3.6 %collective-permute-start.20 = (f32[1,512]{1,0:T(1,128)S(1)}, f32[1,512]{1,0:T(1,128)S(1)}, u32[]{:S(2)}, u32[]{:S(2)}) collective-permute-start(f32[1,512]{1,0:T(1,128)S(1)} %get-tuple-element.130), channel_id=1, source_target_pairs={{0,8},{4,12},{8,0},{12,4},{16,24},{20,28},{24,16},{28,20},{1,9},{5... | collective-permute-start | bytes 6152 | tf_op jit(solution)/shard_map/ppermute | solution.py:386
  82.3 4.5 %collective-permute-start.21 = (f32[1,512]{1,0:T(1,128)S(1)}, f32[1,512]{1,0:T(1,128)S(1)}, u32[]{:S(2)}, u32[]{:S(2)}) collective-permute-start(f32[1,512]{1,0:T(1,128)S(1)} %add.10), channel_id=1, source_target_pairs={{0,16},{4,20},{8,24},{12,28},{16,0},{20,4},{24,8},{28,12},{1,17},{... | collective-permute-start | bytes 6152 | tf_op jit(solution)/shard_map/ppermute | solution.py:386
  86.8 3.6 %collective-permute-start.22 = (f32[1,512]{1,0:T(1,128)S(1)}, f32[1,512]{1,0:T(1,128)S(1)}, u32[]{:S(2)}, u32[]{:S(2)}) collective-permute-start(f32[1,512]{1,0:T(1,128)S(1)} %add.11.sums), channel_id=1, source_target_pairs={{0,4},{4,0},{8,12},{12,8},{16,20},{20,16},{24,28},{28,24},{1,5},{5... | collective-permute-start | bytes 6152 | tf_op jit(solution)/shard_map/ppermute | solution.py:387
  (5 other events, 54.7 us)

commit v7 on v6

--- a/solution.py
+++ b/solution.py
@@ -213,15 +213,25 @@
     sums[:, first:] = total
 
 
-def scale_kernel(row_total, sums, other_sums, *refs):
-    *parts, out = refs
-    half = sums.shape[1]
+def scaled(row_total, sums, early, last):
+    factor = 1.0 / (sums[...] / row_total + EPS)
+    cut = early.shape[1]
+    return early[...] * factor[:, :cut], last[...] * factor[:, cut:]
+
+
+def scale_own_kernel(row_total, sums, early, last, out):
+    cut = early.shape[1]
+    out[:, :cut], out[:, cut:] = scaled(row_total, sums, early, last)
+
+
+def scale_kernel(row_total, sums, early, last, own, out):
+    half, cut = own.shape[1], early.shape[1]
     y = lax.axis_index("row") % 2
-    for side, total, (early, last) in ((y, sums, parts[:2]), (1 - y, other_sums, parts[2:])):
-        scale = total[...] / row_total + EPS
-        cut = early.shape[1]
-        out[:, pl.ds(pl.multiple_of(side * half, BLK), cut)] = early[...] / scale[:, :cut]
-        out[:, pl.ds(pl.multiple_of(side * half + cut, BLK), half - cut)] = last[...] / scale[:, cut:]
+    first = (1 - y) * half
+    out[:, pl.ds(pl.multiple_of(y * half, BLK), half)] = own[...]
+    left, right = scaled(row_total, sums, early, last)
+    out[:, pl.ds(pl.multiple_of(first, BLK), cut)] = left
+    out[:, pl.ds(pl.multiple_of(first + cut, BLK), half - cut)] = right
 
 
 def together(*values):
@@ -385,11 +395,13 @@
     for bit in (2, 4):
         sums = sums + lax.ppermute(sums, "row", [(r, r ^ bit) for r in range(n_row)])
     other_sums = lax.ppermute(sums, "row", swap_y)
+    row_total = share * fibers * n_row
+    (own_scaled,) = call(
+        functools.partial(scale_own_kernel, row_total), [shape((share, half), f32)], [VMEM] * 3
+    )(sums, stays, last_stays)
     (out,) = call(
-        functools.partial(scale_kernel, share * fibers * n_row),
-        [shape((share, columns), f32)],
-        [VMEM] * 6,
-    )(sums, other_sums, stays, last_stays, comes, last_comes)
+        functools.partial(scale_kernel, row_total), [shape((share, columns), f32)], [VMEM] * 4
+    )(other_sums, comes, last_comes, own_scaled)
     return out
 
 

time: 91.5 us -> 91.5 us (level)
    pallas_call x16 -> x17, Pallas kernels: 20.9 us -> 20.9 us  [run(): pl.pallas_call(kernel, out_shape=out_shapes, in_specs=specs, out_specs=[V...]
where the time goes in v7:
time: 91.5 us; the launch traced here: 91.3 us
  waiting for transfers between devices  43.7 us (48%)
  starting transfers between devices  26 us (28%)
  Pallas kernels  20.9 us (23%)
    pallas_call x17, Pallas kernels, run(): pl.pallas_call(kernel, out_shape=out_shapes, in_specs=specs, out_specs=[V...  20.9 us
    ppermute x3, waiting for transfers between devices, local(): lax.ppermute(a_panels[u * UNIT:(u + 1) * UNIT], 'row', swap_y)  8.9 us
    ppermute x1, waiting for transfers between devices, local(): shards[0, 1] = lax.ppermute(columns_half(1 - my_y), 'row', swap_y)  8.26 us
    ppermute x2, waiting for transfers between devices, local(): lax.ppermute(sums, 'row', [(r, r ^ bit) for r in range(n_row)])  6.99 us
    ppermute x2, waiting for transfers between devices, local(): shards[2, turn] = lax.ppermute(shards[0, turn], 'row', z_pairs(2))  5.55 us
    ppermute x2, starting transfers between devices, local(): shards[1, turn] = lax.ppermute(shards[0, turn], 'row', z_pairs(1))  5.34 us
    ppermute x1, waiting for transfers between devices, local(): far_last = lax.ppermute(shards[2, 1][..., cut:], 'row', z_pairs(1))  5.18 us
    ppermute x1, waiting for transfers between devices, local(): c_tables = [c_pattern, lax.ppermute(c_pattern, 'row', swap_y)]  3.09 us
  transfers between devices with their start and end apart: 25, of which 13 were waited for; matrix products, arithmetic and copies ran while one was open for 1% of the time, Pallas kernels for 21%

profile of v7, /device:TPU:0, one launch (start us, length us, event | category | flops | bytes accessed | tf_op | source)
XLA Modules:
  0.0 91.3 jit_solution(15822644589395057883)
XLA Ops:
  0.0 3.0 %collective-permute-start.1 = (f32[192,1,2,768]{3,2,1,0:T(2,128)}, f32[192,1,2,768]{3,2,1,0:T(2,128)S(1)}, u32[]{:S(2)}, u32[]{:S(2)}) collective-permute-start(f32[192,1,2,768]{3,2,1,0:T(2,128)} %refs_0_.1), channel_id=1, source_target_pairs={{0,2},{2,0},{1,3},{3,1},{4,6},{6,4},{5,7},{7,5},{8,10},{10,8},{9,1... | collective-permute-start | bytes 3538952 | tf_op jit(solution)/shard_map/ppermute | solution.py:294
  3.0 2.7 %collective-permute-start.11 = (f32[1,2,96,512]{3,2,1,0:T(8,128)S(1)}, f32[1,2,96,512]{3,2,1,0:T(8,128)}, u32[]{:S(2)}, u32[]{:S(2)}) collective-permute-start(f32[1,2,96,512]{3,2,1,0:T(8,128)S(1)} %constant_dynamic-slice_fusion.1.refs_0_), channel_id=1, source_target_pairs={{0,16},{4,20},{8,24},{12,28},{16,0},{20,4},{24,8},{28,12},{1,17},{... | collective-permute-start | bytes 1179656 | tf_op jit(solution)/shard_map/ppermute | solution.py:289
  5.7 1.6 %collective-permute-start.10 = (f32[1,2,96,512]{3,2,1,0:T(8,128)S(1)}, f32[1,2,96,512]{3,2,1,0:T(8,128)}, u32[]{:S(2)}, u32[]{:S(2)}) collective-permute-start(f32[1,2,96,512]{3,2,1,0:T(8,128)S(1)} %constant_dynamic-slice_fusion.1.refs_0_), channel_id=1, source_target_pairs={{0,8},{4,12},{8,0},{12,4},{16,24},{20,28},{24,16},{28,20},{1,9},{5... | collective-permute-start | bytes 1179656 | tf_op jit(solution)/shard_map/ppermute | solution.py:288
  7.2 1.5 %collective-permute-start.2 = (s32[3,1,2,6]{3,2,1,0:T(2,128)}, s32[3,1,2,6]{3,2,1,0:T(2,128)S(1)}, u32[]{:S(2)}, u32[]{:S(2)}) collective-permute-start(s32[3,1,2,6]{3,2,1,0:T(2,128)} %pattern.13), channel_id=1, source_target_pairs={{0,4},{4,0},{8,12},{12,8},{16,20},{20,16},{24,28},{28,24},{1,5},{5... | collective-permute-start | bytes 440 | tf_op jit(solution)/shard_map/ppermute | solution.py:301
  11.1 1.5 %collective-permute-start.3 = (f32[64,1,2,768]{3,2,1,0:T(2,128)S(1)}, f32[64,1,2,768]{3,2,1,0:T(2,128)S(1)}, u32[]{:S(2)}, u32[]{:S(2)}) collective-permute-start(f32[64,1,2,768]{3,2,1,0:T(2,128)S(1)} %get-tuple-element.136), channel_id=1, source_target_pairs={{0,4},{4,0},{8,12},{12,8},{16,20},{20,16},{24,28},{28,24},{1,5},{5... | collective-permute-start | bytes 1179656 | tf_op jit(solution)/shard_map/ppermute | solution.py:296
  12.6 8.3 %collective-permute-done.9.refs_1_ = f32[1,2,96,512]{3,2,1,0:T(8,128)S(1)} collective-permute-done((f32[1,2,96,512]{3,2,1,0:T(8,128)S(1)}, f32[1,2,96,512]{3,2,1,0:T(8,128)S(1)}, u32[]{:S(2)}, u32[]{:S(2)}) %collective-permute-start.9) | collective-permute-done | bytes 393248 | tf_op jit(solution)/shard_map/ppermute | solution.py:286
  21.4 1.8 %collective-permute-done.11.refs_3_ = f32[1,2,96,512]{3,2,1,0:T(8,128)} collective-permute-done((f32[1,2,96,512]{3,2,1,0:T(8,128)S(1)}, f32[1,2,96,512]{3,2,1,0:T(8,128)}, u32[]{:S(2)}, u32[]{:S(2)}) %collective-permute-start.11) | collective-permute-done | bytes 393248 | tf_op jit(solution)/shard_map/ppermute | solution.py:289
  23.4 3.8 %collective-permute-start.12 = (f32[1,2,96,512]{3,2,1,0:T(8,128)S(1)}, f32[1,2,96,512]{3,2,1,0:T(8,128)S(1)}, u32[]{:S(2)}, u32[]{:S(2)}) collective-permute-start(f32[1,2,96,512]{3,2,1,0:T(8,128)S(1)} %collective-permute-done.9.refs_1_), channel_id=1, source_target_pairs={{0,8},{4,12},{8,0},{12,4},{16,24},{20,28},{24,16},{28,20},{1,9},{5... | collective-permute-start | bytes 1179656 | tf_op jit(solution)/shard_map/ppermute | solution.py:288
  27.1 2.1 %collective-permute-done.3.refs_0_ = f32[64,1,2,768]{3,2,1,0:T(2,128)S(1)} collective-permute-done((f32[64,1,2,768]{3,2,1,0:T(2,128)S(1)}, f32[64,1,2,768]{3,2,1,0:T(2,128)S(1)}, u32[]{:S(2)}, u32[]{:S(2)}) %collective-permute-start.3) | collective-permute-done | bytes 393248 | tf_op jit(solution)/shard_map/ppermute | solution.py:296
  31.0 6.7 %collective-permute-done.4.refs_0_ = f32[64,1,2,768]{3,2,1,0:T(2,128)S(1)} collective-permute-done((f32[64,1,2,768]{3,2,1,0:T(2,128)S(1)}, f32[64,1,2,768]{3,2,1,0:T(2,128)S(1)}, u32[]{:S(2)}, u32[]{:S(2)}) %collective-permute-start.4) | collective-permute-done | bytes 393248 | tf_op jit(solution)/shard_map/ppermute | solution.py:296
  38.8 3.7 %collective-permute-done.13.refs_1_ = f32[1,2,96,512]{3,2,1,0:T(8,128)S(1)} collective-permute-done((f32[1,2,96,512]{3,2,1,0:T(8,128)S(1)}, f32[1,2,96,512]{3,2,1,0:T(8,128)S(1)}, u32[]{:S(2)}, u32[]{:S(2)}) %collective-permute-start.13) | collective-permute-done | bytes 393248 | tf_op jit(solution)/shard_map/ppermute | solution.py:289
  42.6 1.5 %collective-permute-start.7 = (f32[64,1,2,768]{3,2,1,0:T(2,128)S(1)}, f32[64,1,2,768]{3,2,1,0:T(2,128)S(1)}, u32[]{:S(2)}, u32[]{:S(2)}) collective-permute-start(f32[64,1,2,768]{3,2,1,0:T(2,128)S(1)} %slice.24), channel_id=1, source_target_pairs={{0,4},{4,0},{8,12},{12,8},{16,20},{20,16},{24,28},{28,24},{1,5},{5... | collective-permute-start | bytes 1179656 | tf_op jit(solution)/shard_map/ppermute | solution.py:298
  44.1 2.5 %shard_map.46 = (bf16[192,768]{1,0:T(8,128)(2,1)S(1)}, bf16[192,768]{1,0:T(8,128)(2,1)S(1)}, bf16[192,384]{1,0:T(8,128)(2,1)S(1)}, bf16[192,384]{1,0:T(8,128)(2,...) custom-call(s32[3,1,2,6]{3,2,1,0:T(2,128)S(1)} %copy-done.2, ...), custom_call_target="tpu_custom_call" | custom-call | bytes 2359584 | tf_op jit(solution)/shard_map/pallas_call | solution.py:248
  50.8 2.1 %collective-permute-start.17 = (f32[1,2,96,384]{3,2,1,0:T(8,128)S(1)}, f32[1,2,96,384]{3,2,1,0:T(8,128)S(1)}, u32[]{:S(2)}, u32[]{:S(2)}) collective-permute-start(f32[1,2,96,384]{3,2,1,0:T(8,128)S(1)} %slice.26), channel_id=1, source_target_pairs={{0,8},{4,12},{8,0},{12,4},{16,24},{20,28},{24,16},{28,20},{1,9},{5... | collective-permute-start | bytes 884744 | tf_op jit(solution)/shard_map/ppermute | solution.py:291
  52.9 1.9 %shard_map.50 = (bf16[128,768]{1,0:T(8,128)(2,1)S(1)}, bf16[128,768]{1,0:T(8,128)(2,1)S(1)}, bf16[128,384]{1,0:T(8,128)(2,1)S(1)}, bf16[128,384]{1,0:T(8,128)(2,...) custom-call(s32[3,1,2,6]{3,2,1,0:T(2,128)S(1)} %copy-done.2, ...), custom_call_target="tpu_custom_call" | custom-call | bytes 1573152 | tf_op jit(solution)/shard_map/pallas_call | solution.py:248
  54.8 2.5 %shard_map.47 = (bf16[192,768]{1,0:T(8,128)(2,1)S(1)}, bf16[192,768]{1,0:T(8,128)(2,1)S(1)}, bf16[192,384]{1,0:T(8,128)(2,1)S(1)}, bf16[192,384]{1,0:T(8,128)(2,...) custom-call(s32[3,1,2,6]{3,2,1,0:T(2,128)S(1)} %copy-done.2, ...), custom_call_target="tpu_custom_call" | custom-call | bytes 2359584 | tf_op jit(solution)/shard_map/pallas_call | solution.py:248
  57.4 2.7 %shard_map.53.refs_12_ = f32[640,512]{1,0:T(8,128)S(1)} custom-call(bf16[192,768]{1,0:T(8,128)(2,1)S(1)} %get-tuple-element.75.refs_0_, bf16[192,768]{1,0:T(8,128)(2,1)S(1)} %get-tuple-element.76.refs_1_, bf16[64,768]{1,0:T(8,128)(2,1)S(1)} %get-tuple-element.77.refs_2_, bf16[64,768]{1,0:T(8,128)(2,1)S(1)} %get-tuple-element.78.refs_3_, ...), custom_call_target="tpu_custom_call" | custom-call | flops 2264924160 | bytes 6619136 | tf_op jit(solution)/shard_map/pallas_call | solution.py:248
  60.1 1.9 %shard_map.54 = (bf16[128,768]{1,0:T(8,128)(2,1)S(1)}, bf16[128,768]{1,0:T(8,128)(2,1)S(1)}, bf16[128,384]{1,0:T(8,128)(2,1)S(1)}, bf16[128,384]{1,0:T(8,128)(2,...) custom-call(s32[3,1,2,6]{3,2,1,0:T(2,128)S(1)} %copy-done.2, ...), custom_call_target="tpu_custom_call" | custom-call | bytes 1573152 | tf_op jit(solution)/shard_map/pallas_call | solution.py:248
  64.6 5.2 %collective-permute-done.15.refs_13_ = f32[1,2,96,128]{3,2,1,0:T(8,128)S(1)} collective-permute-done((f32[1,2,96,128]{3,2,1,0:T(8,128)S(1)}, f32[1,2,96,128]{3,2,1,0:T(8,128)S(1)}, u32[]{:S(2)}, u32[]{:S(2)}) %collective-permute-start.15) | collective-permute-done | bytes 98336 | tf_op jit(solution)/shard_map/ppermute | solution.py:292
  70.9 3.1 %collective-permute-done.other_pattern = s32[3,8]{1,0:T(4,128)S(1)} collective-permute-done((s32[3,8]{1,0:T(4,128)S(1)}, s32[3,8]{1,0:T(4,128)S(1)}, u32[]{:S(2)}, u32[]{:S(2)}) %collective-permute-start) | collective-permute-done | bytes 128 | tf_op jit(solution)/shard_map/ppermute | solution.py:302
  77.1 1.6 %collective-permute-start.24 = (f32[192,128]{1,0:T(8,128)S(1)}, f32[192,128]{1,0:T(8,128)S(1)}, u32[]{:S(2)}, u32[]{:S(2)}) collective-permute-start(f32[192,128]{1,0:T(8,128)S(1)} %get-tuple-element.132), channel_id=1, source_target_pairs={{0,4},{4,0},{8,12},{12,8},{16,20},{20,16},{24,28},{28,24},{1,5},{5... | collective-permute-start | bytes 294920 | tf_op jit(solution)/shard_map/ppermute | solution.py:394
  79.0 3.3 %collective-permute-done.20 = f32[1,512]{1,0:T(1,128)S(1)} collective-permute-done((f32[1,512]{1,0:T(1,128)S(1)}, f32[1,512]{1,0:T(1,128)S(1)}, u32[]{:S(2)}, u32[]{:S(2)}) %collective-permute-start.20) | collective-permute-done | bytes 2080 | tf_op jit(solution)/shard_map/ppermute | solution.py:396
  83.1 3.7 %collective-permute-done.21 = f32[1,512]{1,0:T(1,128)S(1)} collective-permute-done((f32[1,512]{1,0:T(1,128)S(1)}, f32[1,512]{1,0:T(1,128)S(1)}, u32[]{:S(2)}, u32[]{:S(2)}) %collective-permute-start.21) | collective-permute-done | bytes 2080 | tf_op jit(solution)/shard_map/ppermute | solution.py:396
  87.3 3.0 %collective-permute-done.22.sums = f32[1,512]{1,0:T(1,128)S(1)} collective-permute-done((f32[1,512]{1,0:T(1,128)S(1)}, f32[1,512]{1,0:T(1,128)S(1)}, u32[]{:S(2)}, u32[]{:S(2)}) %collective-permute-start.22) | collective-permute-done | bytes 2080 | tf_op jit(solution)/shard_map/ppermute | solution.py:397
  (60 shorter events, 19.3 us)
Async XLA Ops:
  0.0 29.8 %collective-permute-start.1 = (f32[192,1,2,768]{3,2,1,0:T(2,128)}, f32[192,1,2,768]{3,2,1,0:T(2,128)S(1)}, u32[]{:S(2)}, u32[]{:S(2)}) collective-permute-start(f32[192,1,2,768]{3,2,1,0:T(2,128)} %refs_0_.1), channel_id=1, source_target_pairs={{0,2},{2,0},{1,3},{3,1},{4,6},{6,4},{5,7},{7,5},{8,10},{10,8},{9,1... | collective-permute-start | bytes 3538952 | tf_op jit(solution)/shard_map/ppermute | solution.py:294
  3.0 20.2 %collective-permute-start.11 = (f32[1,2,96,512]{3,2,1,0:T(8,128)S(1)}, f32[1,2,96,512]{3,2,1,0:T(8,128)}, u32[]{:S(2)}, u32[]{:S(2)}) collective-permute-start(f32[1,2,96,512]{3,2,1,0:T(8,128)S(1)} %constant_dynamic-slice_fusion.1.refs_0_), channel_id=1, source_target_pairs={{0,16},{4,20},{8,24},{12,28},{16,0},{20,4},{24,8},{28,12},{1,17},{... | collective-permute-start | bytes 1179656 | tf_op jit(solution)/shard_map/ppermute | solution.py:289
  5.7 17.7 %collective-permute-start.10 = (f32[1,2,96,512]{3,2,1,0:T(8,128)S(1)}, f32[1,2,96,512]{3,2,1,0:T(8,128)}, u32[]{:S(2)}, u32[]{:S(2)}) collective-permute-start(f32[1,2,96,512]{3,2,1,0:T(8,128)S(1)} %constant_dynamic-slice_fusion.1.refs_0_), channel_id=1, source_target_pairs={{0,8},{4,12},{8,0},{12,4},{16,24},{20,28},{24,16},{28,20},{1,9},{5... | collective-permute-start | bytes 1179656 | tf_op jit(solution)/shard_map/ppermute | solution.py:288
  7.2 3.8 %collective-permute-start.2 = (s32[3,1,2,6]{3,2,1,0:T(2,128)}, s32[3,1,2,6]{3,2,1,0:T(2,128)S(1)}, u32[]{:S(2)}, u32[]{:S(2)}) collective-permute-start(s32[3,1,2,6]{3,2,1,0:T(2,128)} %pattern.13), channel_id=1, source_target_pairs={{0,4},{4,0},{8,12},{12,8},{16,20},{20,16},{24,28},{28,24},{1,5},{5... | collective-permute-start | bytes 440 | tf_op jit(solution)/shard_map/ppermute | solution.py:301
  8.8 12.1 %collective-permute-start.9 = (f32[1,2,96,512]{3,2,1,0:T(8,128)S(1)}, f32[1,2,96,512]{3,2,1,0:T(8,128)S(1)}, u32[]{:S(2)}, u32[]{:S(2)}) collective-permute-start(f32[1,2,96,512]{3,2,1,0:T(8,128)S(1)} %constant_dynamic-slice_fusion), channel_id=1, source_target_pairs={{0,4},{4,0},{8,12},{12,8},{16,20},{20,16},{24,28},{28,24},{1,5},{5... | collective-permute-start | bytes 1179656 | tf_op jit(solution)/shard_map/ppermute | solution.py:286
  11.1 18.2 %collective-permute-start.3 = (f32[64,1,2,768]{3,2,1,0:T(2,128)S(1)}, f32[64,1,2,768]{3,2,1,0:T(2,128)S(1)}, u32[]{:S(2)}, u32[]{:S(2)}) collective-permute-start(f32[64,1,2,768]{3,2,1,0:T(2,128)S(1)} %get-tuple-element.136), channel_id=1, source_target_pairs={{0,4},{4,0},{8,12},{12,8},{16,20},{20,16},{24,28},{28,24},{1,5},{5... | collective-permute-start | bytes 1179656 | tf_op jit(solution)/shard_map/ppermute | solution.py:296
  20.9 16.9 %collective-permute-start.4 = (f32[64,1,2,768]{3,2,1,0:T(2,128)S(1)}, f32[64,1,2,768]{3,2,1,0:T(2,128)S(1)}, u32[]{:S(2)}, u32[]{:S(2)}) collective-permute-start(f32[64,1,2,768]{3,2,1,0:T(2,128)S(1)} %get-tuple-element.137), channel_id=1, source_target_pairs={{0,4},{4,0},{8,12},{12,8},{16,20},{20,16},{24,28},{28,24},{1,5},{5... | collective-permute-start | bytes 1179656 | tf_op jit(solution)/shard_map/ppermute | solution.py:296
  23.2 19.4 %collective-permute-start.13 = (f32[1,2,96,512]{3,2,1,0:T(8,128)S(1)}, f32[1,2,96,512]{3,2,1,0:T(8,128)S(1)}, u32[]{:S(2)}, u32[]{:S(2)}) collective-permute-start(f32[1,2,96,512]{3,2,1,0:T(8,128)S(1)} %collective-permute-done.9.refs_1_), channel_id=1, source_target_pairs={{0,16},{4,20},{8,24},{12,28},{16,0},{20,4},{24,8},{28,12},{1,17},{... | collective-permute-start | bytes 1179656 | tf_op jit(solution)/shard_map/ppermute | solution.py:289
  23.4 20.7 %collective-permute-start.12 = (f32[1,2,96,512]{3,2,1,0:T(8,128)S(1)}, f32[1,2,96,512]{3,2,1,0:T(8,128)S(1)}, u32[]{:S(2)}, u32[]{:S(2)}) collective-permute-start(f32[1,2,96,512]{3,2,1,0:T(8,128)S(1)} %collective-permute-done.9.refs_1_), channel_id=1, source_target_pairs={{0,8},{4,12},{8,0},{12,4},{16,24},{20,28},{24,16},{28,20},{1,9},{5... | collective-permute-start | bytes 1179656 | tf_op jit(solution)/shard_map/ppermute | solution.py:288
  29.3 21.5 %collective-permute-start.5 = (f32[64,1,2,768]{3,2,1,0:T(2,128)S(1)}, f32[64,1,2,768]{3,2,1,0:T(2,128)S(1)}, u32[]{:S(2)}, u32[]{:S(2)}) collective-permute-start(f32[64,1,2,768]{3,2,1,0:T(2,128)S(1)} %get-tuple-element.135), channel_id=1, source_target_pairs={{0,4},{4,0},{8,12},{12,8},{16,20},{20,16},{24,28},{28,24},{1,5},{5... | collective-permute-start | bytes 1179656 | tf_op jit(solution)/shard_map/ppermute | solution.py:296
  29.8 23.1 %collective-permute-start.6 = (f32[64,1,2,768]{3,2,1,0:T(2,128)S(1)}, f32[64,1,2,768]{3,2,1,0:T(2,128)S(1)}, u32[]{:S(2)}, u32[]{:S(2)}) collective-permute-start(f32[64,1,2,768]{3,2,1,0:T(2,128)S(1)} %collective-permute-done.3.refs_0_), channel_id=1, source_target_pairs={{0,2},{2,0},{1,3},{3,1},{4,6},{6,4},{5,7},{7,5},{8,10},{10,8},{9,1... | collective-permute-start | bytes 1179656 | tf_op jit(solution)/shard_map/ppermute | solution.py:299
  37.7 22.3 %collective-permute-start.8 = (f32[64,1,2,768]{3,2,1,0:T(2,128)S(1)}, f32[64,1,2,768]{3,2,1,0:T(2,128)S(1)}, u32[]{:S(2)}, u32[]{:S(2)}) collective-permute-start(f32[64,1,2,768]{3,2,1,0:T(2,128)S(1)} %collective-permute-done.4.refs_0_), channel_id=1, source_target_pairs={{0,2},{2,0},{1,3},{3,1},{4,6},{6,4},{5,7},{7,5},{8,10},{10,8},{9,1... | collective-permute-start | bytes 1179656 | tf_op jit(solution)/shard_map/ppermute | solution.py:300
  42.6 17.5 %collective-permute-start.7 = (f32[64,1,2,768]{3,2,1,0:T(2,128)S(1)}, f32[64,1,2,768]{3,2,1,0:T(2,128)S(1)}, u32[]{:S(2)}, u32[]{:S(2)}) collective-permute-start(f32[64,1,2,768]{3,2,1,0:T(2,128)S(1)} %slice.24), channel_id=1, source_target_pairs={{0,4},{4,0},{8,12},{12,8},{16,20},{20,16},{24,28},{28,24},{1,5},{5... | collective-permute-start | bytes 1179656 | tf_op jit(solution)/shard_map/ppermute | solution.py:298
  44.1 18.6 %collective-permute-start.14 = (f32[1,2,96,512]{3,2,1,0:T(8,128)}, f32[1,2,96,512]{3,2,1,0:T(8,128)S(1)}, u32[]{:S(2)}, u32[]{:S(2)}) collective-permute-start(f32[1,2,96,512]{3,2,1,0:T(8,128)} %collective-permute-done.11.refs_3_), channel_id=1, source_target_pairs={{0,8},{4,12},{8,0},{12,4},{16,24},{20,28},{24,16},{28,20},{1,9},{5... | collective-permute-start | bytes 1179656 | tf_op jit(solution)/shard_map/ppermute | solution.py:290
  50.8 12.7 %collective-permute-start.17 = (f32[1,2,96,384]{3,2,1,0:T(8,128)S(1)}, f32[1,2,96,384]{3,2,1,0:T(8,128)S(1)}, u32[]{:S(2)}, u32[]{:S(2)}) collective-permute-start(f32[1,2,96,384]{3,2,1,0:T(8,128)S(1)} %slice.26), channel_id=1, source_target_pairs={{0,8},{4,12},{8,0},{12,4},{16,24},{20,28},{24,16},{28,20},{1,9},{5... | collective-permute-start | bytes 884744 | tf_op jit(solution)/shard_map/ppermute | solution.py:291
  64.4 9.6 %collective-permute-start.18 = (f32[2,192,384]{2,1,0:T(8,128)S(1)}, f32[2,192,384]{2,1,0:T(8,128)S(1)}, u32[]{:S(2)}, u32[]{:S(2)}) collective-permute-start(f32[2,192,384]{2,1,0:T(8,128)S(1)} %get-tuple-element.128), channel_id=1, source_target_pairs={{0,1},{1,0},{2,3},{3,2},{4,5},{5,4},{6,7},{7,6},{8,9},{9,8},{10,11... | collective-permute-start | bytes 1769480 | tf_op jit(solution)/shard_map/ppermute | solution.py:379
  64.5 5.3 %collective-permute-start.15 = (f32[1,2,96,128]{3,2,1,0:T(8,128)S(1)}, f32[1,2,96,128]{3,2,1,0:T(8,128)S(1)}, u32[]{:S(2)}, u32[]{:S(2)}) collective-permute-start(f32[1,2,96,128]{3,2,1,0:T(8,128)S(1)} %slice.25), channel_id=1, source_target_pairs={{0,8},{4,12},{8,0},{12,4},{16,24},{20,28},{24,16},{28,20},{1,9},{5... | collective-permute-start | bytes 294920 | tf_op jit(solution)/shard_map/ppermute | solution.py:292
  70.2 6.2 %collective-permute-start.16 = (f32[4,192,128]{2,1,0:T(8,128)S(1)}, f32[4,192,128]{2,1,0:T(8,128)S(1)}, u32[]{:S(2)}, u32[]{:S(2)}) collective-permute-start(f32[4,192,128]{2,1,0:T(8,128)S(1)} %shard_map.57.mine), channel_id=1, source_target_pairs={{0,1},{1,0},{2,3},{3,2},{4,5},{5,4},{6,7},{7,6},{8,9},{9,8},{10,11... | collective-permute-start | bytes 1179656 | tf_op jit(solution)/shard_map/ppermute | solution.py:381
  70.3 3.7 %collective-permute-start = (s32[3,8]{1,0:T(4,128)S(1)}, s32[3,8]{1,0:T(4,128)S(1)}, u32[]{:S(2)}, u32[]{:S(2)}) collective-permute-start(s32[3,8]{1,0:T(4,128)S(1)} %copy-done.3), channel_id=1, source_target_pairs={{0,4},{4,0},{8,12},{12,8},{16,20},{20,16},{24,28},{28,24},{1,5},{5... | collective-permute-start | bytes 296 | tf_op jit(solution)/shard_map/ppermute | solution.py:302
  74.7 15.7 %collective-permute-start.23 = (f32[192,384]{1,0:T(8,128)S(1)}, f32[192,384]{1,0:T(8,128)S(1)}, u32[]{:S(2)}, u32[]{:S(2)}) collective-permute-start(f32[192,384]{1,0:T(8,128)S(1)} %get-tuple-element.131), channel_id=1, source_target_pairs={{0,4},{4,0},{8,12},{12,8},{16,20},{20,16},{24,28},{28,24},{1,5},{5... | collective-permute-start | bytes 884744 | tf_op jit(solution)/shard_map/ppermute | solution.py:387
  77.1 13.3 %collective-permute-start.24 = (f32[192,128]{1,0:T(8,128)S(1)}, f32[192,128]{1,0:T(8,128)S(1)}, u32[]{:S(2)}, u32[]{:S(2)}) collective-permute-start(f32[192,128]{1,0:T(8,128)S(1)} %get-tuple-element.132), channel_id=1, source_target_pairs={{0,4},{4,0},{8,12},{12,8},{16,20},{20,16},{24,28},{28,24},{1,5},{5... | collective-permute-start | bytes 294920 | tf_op jit(solution)/shard_map/ppermute | solution.py:394
  78.7 3.6 %collective-permute-start.20 = (f32[1,512]{1,0:T(1,128)S(1)}, f32[1,512]{1,0:T(1,128)S(1)}, u32[]{:S(2)}, u32[]{:S(2)}) collective-permute-start(f32[1,512]{1,0:T(1,128)S(1)} %get-tuple-element.130), channel_id=1, source_target_pairs={{0,8},{4,12},{8,0},{12,4},{16,24},{20,28},{24,16},{28,20},{1,9},{5... | collective-permute-start | bytes 6152 | tf_op jit(solution)/shard_map/ppermute | solution.py:396
  82.3 4.5 %collective-permute-start.21 = (f32[1,512]{1,0:T(1,128)S(1)}, f32[1,512]{1,0:T(1,128)S(1)}, u32[]{:S(2)}, u32[]{:S(2)}) collective-permute-start(f32[1,512]{1,0:T(1,128)S(1)} %add.10), channel_id=1, source_target_pairs={{0,16},{4,20},{8,24},{12,28},{16,0},{20,4},{24,8},{28,12},{1,17},{... | collective-permute-start | bytes 6152 | tf_op jit(solution)/shard_map/ppermute | solution.py:396
  86.8 3.6 %collective-permute-start.22 = (f32[1,512]{1,0:T(1,128)S(1)}, f32[1,512]{1,0:T(1,128)S(1)}, u32[]{:S(2)}, u32[]{:S(2)}) collective-permute-start(f32[1,512]{1,0:T(1,128)S(1)} %add.11.sums), channel_id=1, source_target_pairs={{0,4},{4,0},{8,12},{12,8},{16,20},{20,16},{24,28},{28,24},{1,5},{5... | collective-permute-start | bytes 6152 | tf_op jit(solution)/shard_map/ppermute | solution.py:397
  (5 other events, 54.7 us)
